TPU v7x, 32 devices: a whole 2x2x4 slice. The times are simulated.
32 devices in a mesh: dp: 2 (over y), seq: 8 (over z, x), tensor: 2 (over core).
Axes of the slice: x: 2, y: 2, z: 4, core: 2. Of those that a mesh axis runs over, the one named last changes fastest.
Arguments:
- tokens: bfloat16 [4, 8192, 512], P('dp', 'seq'), may hold values from -6 to 6
- segments: int32 [4, 8192], P('dp', 'seq'), may hold values from 0 to 15, never falling along the last dimension, each value on 1 to 5120 neighbouring positions
- keep_mask: int32 [4, 8192], P('dp', 'seq'), may hold values 0 or 1
- cotangent: bfloat16 [4, 8192, 512], P('dp', 'seq'), may hold values from -6 to 6
- ln1_gain: float32 [512], replicated, may hold values from 0.25 to 1.75
- ln1_bias: float32 [512], replicated, may hold values from -1.5 to 1.5
- w_qkv: bfloat16 [3, 512, 512], P(None, None, 'tensor'), may hold values from -0.25 to 0.25
- qv_bias: float32 [2, 512], P(None, 'tensor'), may hold values from -1.5 to 1.5
- w_out: bfloat16 [512, 512], P('tensor'), may hold values from -1.5 to 1.5
- b_out: float32 [512], replicated, may hold values from -1.5 to 1.5
- ln2_gain: float32 [512], replicated, may hold values from 0.25 to 1.75
- ln2_bias: float32 [512], replicated, may hold values from -1.5 to 1.5
- w_fc: bfloat16 [512, 2048], P(None, 'tensor'), may hold values from -0.25 to 0.25
- b_fc: float32 [2048], P('tensor'), may hold values from -1.5 to 1.5
- w_proj: bfloat16 [2048, 512], P('tensor'), may hold values from -0.125 to 0.125
- b_proj: float32 [512], replicated, may hold values from -1.5 to 1.5
Outputs:
- layer_out: bfloat16 [4, 8192, 512], P('dp', 'seq')
- grad_tokens: bfloat16 [4, 8192, 512], P('dp', 'seq')
- grad_ln1_gain: float32 [512], replicated
- grad_ln1_bias: float32 [512], replicated
- grad_w_qkv: float32 [3, 512, 512], P(None, None, 'tensor')
- grad_qv_bias: float32 [2, 512], P(None, 'tensor')
- grad_w_out: float32 [512, 512], P('tensor')
- grad_b_out: float32 [512], replicated
- grad_ln2_gain: float32 [512], replicated
- grad_ln2_bias: float32 [512], replicated
- grad_w_fc: float32 [512, 2048], P(None, 'tensor')
- grad_b_fc: float32 [2048], P('tensor')
- grad_w_proj: float32 [2048, 512], P('tensor')
- grad_b_proj: float32 [512], replicated
Inputs may be any that keep to these rules, and one draw needn't show every extreme that they name: `segments`: in each sequence the document numbers never fall; each document holds 1 to 5120 tokens, and one holds exactly 5120.
All inputs are finite; a program needn't handle non-finite values. No bound on the sum of `keep_mask` on one device may be relied on, other than what follows from the above.
Results may differ from a plain program's by a relative error of at most 0.024.
Values may be sent and summed in bfloat16 or wider, within the bound.
No kernel may reach another device: no remote copies, remote signals or barrier semaphores. Data moves between devices by JAX's collectives and lax.ppermute only.
A program may use at most 512 MiB of HBM per device.

v0:
```python
import jax
import jax.numpy as jnp
from jax import lax
from jax.sharding import PartitionSpec as P

HEAD_DIM = 64


EPSILON = 1e-05
MASKED = -1e30


def layer_norm(rows, gain, offset):
    centred = rows - jnp.mean(rows, -1, keepdims=True)
    rstd = lax.rsqrt(jnp.mean(centred * centred, -1, keepdims=True) + EPSILON)
    normed = centred * rstd
    return (normed * gain + offset, normed, rstd)


def norm_back(grad_norm, normed, rstd, gain):
    scaled = grad_norm * gain
    return rstd * (
        scaled
        - jnp.mean(scaled, -1, keepdims=True)
        - normed * jnp.mean(scaled * normed, -1, keepdims=True)
    )


def gelu_parts(pre_act):
    sigma = jax.nn.sigmoid(1.702 * pre_act)
    return (pre_act * sigma, sigma + 1.702 * pre_act * sigma * (1.0 - sigma))


def visible(query_pos, query_seg, key_pos, key_seg, key_keep):
    allowed = (query_seg[:, None] == key_seg[None, :]) & (key_pos[None, :] <= query_pos[:, None])
    return allowed & ((key_keep[None, :] == 1) | (key_pos[None, :] == query_pos[:, None]))


def on_device(
    tokens,
    segments,
    keep_mask,
    cotangent,
    ln1_gain,
    ln1_bias,
    w_qkv,
    qv_bias,
    w_out,
    b_out,
    ln2_gain,
    ln2_bias,
    w_fc,
    b_fc,
    w_proj,
    b_proj,
):
    sequences, group_rows, width = tokens.shape
    local_width = w_qkv.shape[2]
    heads_here = local_width // HEAD_DIM
    score_scale = HEAD_DIM ** (-0.5)
    seg_all, keep_all = (
        lax.all_gather(segments, "seq", axis=1, tiled=True),
        lax.all_gather(keep_mask, "seq", axis=1, tiled=True),
    )
    full_length = seg_all.shape[1]
    key_block = min(512, full_length)
    block_count = full_length // key_block
    piece_index = lax.axis_index("seq")
    query_pos = piece_index * group_rows + jnp.arange(group_rows, dtype=jnp.int32)
    params = (
        ln1_gain,
        ln1_bias,
        w_qkv,
        qv_bias,
        w_out,
        b_out,
        ln2_gain,
        ln2_bias,
        w_fc,
        b_fc,
        w_proj,
        b_proj,
    )
    sums = [jnp.zeros(p.shape, jnp.float32) for p in params]
    outputs = []
    input_grads = []
    for sequence_index in range(sequences):
        rows = tokens[sequence_index].astype(jnp.float32)
        seg_row = seg_all[sequence_index]
        keep_row = keep_all[sequence_index]
        query_seg = segments[sequence_index]
        normed_one_out, normed_one, rstd_one = layer_norm(rows, ln1_gain, ln1_bias)
        hidden_one = normed_one_out.astype(jnp.bfloat16)
        projected = jnp.einsum("te,ced->ctd", hidden_one, w_qkv, preferred_element_type=jnp.float32)
        queries = (projected[0] + qv_bias[0]).astype(jnp.bfloat16)
        keys = projected[1].astype(jnp.bfloat16)
        values = (projected[2] + qv_bias[1]).astype(jnp.bfloat16)
        query_heads = queries.reshape(group_rows, heads_here, HEAD_DIM)
        best = jnp.full((heads_here, group_rows), MASKED, jnp.float32)
        key_part = lax.all_gather(keys, "seq", axis=0, tiled=True)
        value_part = lax.all_gather(values, "seq", axis=0, tiled=True)
        row_count = key_part.shape[0]
        key_pos = jnp.arange(row_count, dtype=jnp.int32)
        key_seg = seg_row
        key_keep = keep_row
        allowed = visible(query_pos, query_seg, key_pos, key_seg, key_keep)[None]
        scores = (
            jnp.einsum(
                "qhd,khd->hqk",
                query_heads,
                key_part.reshape(row_count, heads_here, HEAD_DIM),
                preferred_element_type=jnp.float32,
            )
            * score_scale
        )
        scores = jnp.where(allowed, scores, MASKED)
        new_best = jnp.maximum(best, jnp.max(scores, -1))
        weights = jnp.where(allowed, jnp.exp(scores - new_best[..., None]), 0.0)
        weight_sum = jnp.sum(weights, -1)
        accum = jnp.einsum(
            "hqk,khd->hqd",
            weights.astype(jnp.bfloat16),
            value_part.reshape(row_count, heads_here, HEAD_DIM),
            preferred_element_type=jnp.float32,
        )
        best, weight_sum, accum = (new_best, weight_sum, accum)
        log_sum = best + jnp.log(weight_sum)
        attn_out = (
            (accum / weight_sum[..., None])
            .transpose(1, 0, 2)
            .reshape(group_rows, local_width)
            .astype(jnp.bfloat16)
        )
        attn_term = jnp.dot(attn_out, w_out, preferred_element_type=jnp.float32)
        middle = (
            rows + lax.psum(attn_term.astype(jnp.bfloat16), "tensor").astype(jnp.float32) + b_out
        )
        normed_two_out, normed_two, rstd_two = layer_norm(middle, ln2_gain, ln2_bias)
        hidden_two = normed_two_out.astype(jnp.bfloat16)
        pre_act = jnp.dot(hidden_two, w_fc, preferred_element_type=jnp.float32) + b_fc
        activated, slope = gelu_parts(pre_act)
        act_low = activated.astype(jnp.bfloat16)
        feed_term = jnp.dot(act_low, w_proj, preferred_element_type=jnp.float32)
        feed = lax.psum(feed_term.astype(jnp.bfloat16), "tensor").astype(jnp.float32) + b_proj
        outputs.append((middle + feed).astype(jnp.bfloat16))
        grad_out = cotangent[sequence_index]
        grad_out_wide = grad_out.astype(jnp.float32)
        sums[11] = sums[11] + jnp.sum(grad_out_wide, 0)
        sums[10] = sums[10] + jnp.einsum(
            "tf,td->fd", act_low, grad_out, preferred_element_type=jnp.float32
        )
        grad_act = jnp.einsum("td,fd->tf", grad_out, w_proj, preferred_element_type=jnp.float32)
        grad_pre = (grad_act * slope).astype(jnp.bfloat16)
        sums[9] = sums[9] + jnp.sum(grad_pre.astype(jnp.float32), 0)
        sums[8] = sums[8] + jnp.einsum(
            "te,tf->ef", hidden_two, grad_pre, preferred_element_type=jnp.float32
        )
        grad_hidden_two = lax.psum(
            jnp.einsum("tf,ef->te", grad_pre, w_fc, preferred_element_type=jnp.float32).astype(
                jnp.bfloat16
            ),
            "tensor",
        ).astype(jnp.float32)
        sums[6] = sums[6] + jnp.sum(grad_hidden_two * normed_two, 0)
        sums[7] = sums[7] + jnp.sum(grad_hidden_two, 0)
        grad_middle = grad_out_wide + norm_back(grad_hidden_two, normed_two, rstd_two, ln2_gain)
        grad_branch = grad_middle.astype(jnp.bfloat16)
        sums[5] = sums[5] + jnp.sum(grad_branch.astype(jnp.float32), 0)
        sums[4] = sums[4] + jnp.einsum(
            "tc,td->cd", attn_out, grad_branch, preferred_element_type=jnp.float32
        )
        grad_mixed = jnp.einsum(
            "td,cd->tc", grad_branch, w_out, preferred_element_type=jnp.float32
        ).astype(jnp.bfloat16)
        grad_heads = grad_mixed.reshape(group_rows, heads_here, HEAD_DIM)
        row_dot = jnp.sum(
            (grad_mixed.astype(jnp.float32) * attn_out.astype(jnp.float32)).reshape(
                group_rows, heads_here, HEAD_DIM
            ),
            -1,
        ).T
        key_use, value_use = (
            lax.all_gather(keys, "seq", axis=0, tiled=True),
            lax.all_gather(values, "seq", axis=0, tiled=True),
        )

        def make_step(key_src, value_src, seg_src, keep_src, pos_base, block_rows):

            def key_step(grad_query_sum, block_index):
                first_row = block_index * block_rows
                key_part = lax.dynamic_slice_in_dim(key_src, first_row, block_rows).reshape(
                    block_rows, heads_here, HEAD_DIM
                )
                value_part = lax.dynamic_slice_in_dim(value_src, first_row, block_rows).reshape(
                    block_rows, heads_here, HEAD_DIM
                )
                key_pos = pos_base + first_row + jnp.arange(block_rows, dtype=jnp.int32)
                key_seg = lax.dynamic_slice_in_dim(seg_src, first_row, block_rows)
                key_keep = lax.dynamic_slice_in_dim(keep_src, first_row, block_rows)
                allowed = visible(query_pos, query_seg, key_pos, key_seg, key_keep)[None]
                scores = (
                    jnp.einsum(
                        "qhd,khd->hqk", query_heads, key_part, preferred_element_type=jnp.float32
                    )
                    * score_scale
                )
                probs = jnp.where(allowed, jnp.exp(scores - log_sum[..., None]), 0.0)
                grad_probs = jnp.einsum(
                    "qhd,khd->hqk", grad_heads, value_part, preferred_element_type=jnp.float32
                )
                grad_scores = (probs * (grad_probs - row_dot[..., None])).astype(jnp.bfloat16)
                grad_query_sum = grad_query_sum + jnp.einsum(
                    "hqk,khd->qhd", grad_scores, key_part, preferred_element_type=jnp.float32
                )
                key_term = jnp.einsum(
                    "hqk,qhd->khd", grad_scores, query_heads, preferred_element_type=jnp.float32
                )
                value_term = jnp.einsum(
                    "hqk,qhd->khd",
                    probs.astype(jnp.bfloat16),
                    grad_heads,
                    preferred_element_type=jnp.float32,
                )
                return (
                    grad_query_sum,
                    (
                        key_term.reshape(block_rows, local_width),
                        value_term.reshape(block_rows, local_width),
                    ),
                )

            return key_step

        query_start = jnp.zeros((group_rows, heads_here, HEAD_DIM), jnp.float32)
        step_fn = make_step(key_use, value_use, seg_row, keep_row, 0, key_block)
        grad_query_sum, (key_terms, value_terms) = lax.scan(
            step_fn, query_start, jnp.arange(block_count, dtype=jnp.int32)
        )
        key_terms = key_terms.reshape(full_length, local_width) * score_scale
        value_terms = value_terms.reshape(full_length, local_width)
        key_grads, value_grads = (
            lax.psum_scatter(
                key_terms.astype(jnp.bfloat16), "seq", scatter_dimension=0, tiled=True
            ).astype(jnp.float32),
            lax.psum_scatter(
                value_terms.astype(jnp.bfloat16), "seq", scatter_dimension=0, tiled=True
            ).astype(jnp.float32),
        )
        grad_queries = (
            (grad_query_sum * score_scale).reshape(group_rows, local_width).astype(jnp.bfloat16)
        )
        value_low = value_grads.astype(jnp.bfloat16)
        stacked = jnp.stack([grad_queries, key_grads.astype(jnp.bfloat16), value_low])
        sums[2] = sums[2] + jnp.einsum(
            "te,ctd->ced", hidden_one, stacked, preferred_element_type=jnp.float32
        )
        sums[3] = sums[3] + jnp.stack(
            [
                jnp.sum(grad_queries.astype(jnp.float32), 0),
                jnp.sum(value_low.astype(jnp.float32), 0),
            ]
        )
        grad_hidden_one = lax.psum(
            jnp.einsum("ctd,ced->te", stacked, w_qkv, preferred_element_type=jnp.float32).astype(
                jnp.bfloat16
            ),
            "tensor",
        ).astype(jnp.float32)
        sums[0] = sums[0] + jnp.sum(grad_hidden_one * normed_one, 0)
        sums[1] = sums[1] + jnp.sum(grad_hidden_one, 0)
        grad_rows = grad_middle + norm_back(grad_hidden_one, normed_one, rstd_one, ln1_gain)
        input_grads.append(grad_rows.astype(jnp.bfloat16))
    totals = (
        lax.psum(sums[0].astype(jnp.bfloat16), ("dp", "seq")).astype(jnp.float32),
        lax.psum(sums[1].astype(jnp.bfloat16), ("dp", "seq")).astype(jnp.float32),
        lax.psum(sums[2].astype(jnp.bfloat16), ("dp", "seq")).astype(jnp.float32),
        lax.psum(sums[3].astype(jnp.bfloat16), ("dp", "seq")).astype(jnp.float32),
        lax.psum(sums[4].astype(jnp.bfloat16), ("dp", "seq")).astype(jnp.float32),
        lax.psum(sums[5].astype(jnp.bfloat16), ("dp", "seq")).astype(jnp.float32),
        lax.psum(sums[6].astype(jnp.bfloat16), ("dp", "seq")).astype(jnp.float32),
        lax.psum(sums[7].astype(jnp.bfloat16), ("dp", "seq")).astype(jnp.float32),
        lax.psum(sums[8].astype(jnp.bfloat16), ("dp", "seq")).astype(jnp.float32),
        lax.psum(sums[9].astype(jnp.bfloat16), ("dp", "seq")).astype(jnp.float32),
        lax.psum(sums[10].astype(jnp.bfloat16), ("dp", "seq")).astype(jnp.float32),
        lax.psum(sums[11].astype(jnp.bfloat16), ("dp", "seq")).astype(jnp.float32),
    )
    return (
        jnp.stack(outputs),
        jnp.stack(input_grads),
        totals[0],
        totals[1],
        totals[2],
        totals[3],
        totals[4],
        totals[5],
        totals[6],
        totals[7],
        totals[8],
        totals[9],
        totals[10],
        totals[11],
    )


def solution(mesh):
    return jax.shard_map(
        on_device,
        mesh=mesh,
        in_specs=(
            P("dp", "seq", None),
            P("dp", "seq"),
            P("dp", "seq"),
            P("dp", "seq", None),
            P(),
            P(),
            P(None, None, "tensor"),
            P(None, "tensor"),
            P("tensor", None),
            P(),
            P(),
            P(),
            P(None, "tensor"),
            P("tensor"),
            P("tensor", None),
            P(),
        ),
        out_specs=(
            P("dp", "seq", None),
            P("dp", "seq", None),
            P(),
            P(),
            P(None, None, "tensor"),
            P(None, "tensor"),
            P("tensor", None),
            P(),
            P(),
            P(),
            P(None, "tensor"),
            P("tensor"),
            P("tensor", None),
            P(),
        ),
        check_vma=False,
    )
```

profile of v0, /device:TPU:0, one launch (start us, length us, event | category | flops | bytes accessed | tf_op | source)
XLA Modules:
  0.0 1567.0 jit_solution(10269686080167025364)
XLA Ops:
  23.1 32.7 %all_gather.22 = s32[2,8192]{1,0:T(2,128)S(1)} all-gather(s32[2,1024]{1,0:T(2,128)S(1)} %copy-done.84), channel_id=1, replica_groups=mesh['dp'=2,'seq'=8,'tensor'=2] {'seq'}, dimensions={1}, use_global_device_ids=true | all-gather | bytes 73728 | tf_op jit(solution)/shard_map/all_gather | solution.py:62
  58.3 31.3 %all_gather.23 = s32[2,8192]{1,0:T(2,128)S(1)} all-gather(s32[2,1024]{1,0:T(2,128)S(1)} %copy-done.89), channel_id=1, replica_groups=mesh['dp'=2,'seq'=8,'tensor'=2] {'seq'}, dimensions={1}, use_global_device_ids=true | all-gather | bytes 73728 | tf_op jit(solution)/shard_map/all_gather | solution.py:63
  91.9 24.5 %fusion.37 = (pred[1024,8192]{1,0:T(8,128)(4,1)}, pred[1024,8192]{1,0:T(8,128)(4,1)}) fusion(s32[8192]{0:T(1024)S(1)} %bitcast.455, s32[1024]{0:T(1024)S(1)} %iota_add_fusion.4, s32[1024]{0:T(1024)S(1)} %bitcast.451, pred[8192]{0:T(1024)(128)(4,1)S(1)} %get-tuple-element.339, pred[8192]{0:T(1024)(128)(4,1)S(1)} %get-tuple-element.338, ...), kind=kLoop, calls=%fused_computation.59 | loop fusion | flops 83886080 | bytes 16871424 | tf_op jit(solution)/shard_map/and | solution.py:36
  116.5 50.0 %fusion.20 = (f32[4,1024]{1,0:T(4,128)S(1)}, f32[4,1024,8192]{2,1,0:T(8,128)}) fusion(pred[1024,8192]{1,0:T(8,128)(4,1)} %get-tuple-element.451, bf16[1024,4,64]{0,2,1:T(8,128)(2,1)S(1)} %get-tuple-element.729, bf16[8192,4,64]{0,2,1:T(8,128)(2,1)} %bitcast.448), kind=kOutput, calls=%fused_computation.42 | convolution fusion | flops 4395626496 | bytes 147341312 | tf_op jit(solution)/shard_map/qhd,khd->hqk/dot_general | solution.py:108
  166.8 50.2 %fusion.21 = (f32[4,1024]{1,0:T(4,128)S(1)}, f32[4,1024,8192]{2,1,0:T(8,128)}) fusion(pred[1024,8192]{1,0:T(8,128)(4,1)} %get-tuple-element.450, bf16[1024,4,64]{0,2,1:T(8,128)(2,1)S(1)} %get-tuple-element.672, bf16[8192,4,64]{0,2,1:T(8,128)(2,1)} %bitcast.445), kind=kOutput, calls=%fused_computation.43 | convolution fusion | flops 4395626496 | bytes 147341312 | tf_op jit(solution)/shard_map/qhd,khd->hqk/dot_general | solution.py:108
  217.6 44.0 %fusion.22 = f32[4,1024]{1,0:T(4,128)S(1)} fusion(f32[4,1024,8192]{2,1,0:T(8,128)} %get-tuple-element.459, f32[4,1024]{1,0:T(4,128)S(1)} %broadcast_maximum_fusion.1, pred[1024,8192]{1,0:T(8,128)(4,1)} %get-tuple-element.451), kind=kLoop, calls=%fused_computation.44 | loop fusion | flops 167768064 | bytes 142639104 | tf_op jit(solution)/shard_map/reduce_sum | solution.py:119
  261.6 51.2 %divide_convert_fusion.1 = bf16[1024,4,64]{0,2,1:T(8,128)(2,1)S(1)} fusion(bf16[8192,4,64]{0,2,1:T(8,128)(2,1)} %bitcast.450, f32[4,1024,8192]{2,1,0:T(8,128)} %get-tuple-element.459, f32[4,1024]{1,0:T(4,128)S(1)} %broadcast_maximum_fusion.1, pred[1024,8192]{1,0:T(8,128)(4,1)} %get-tuple-element.451, f32[1024,4]{0,1:T(4,128)S(1)} %bitcast.460), kind=kOutput, calls=%fused_computation.207 | convolution fusion | flops 4463263744 | bytes 147357696 | tf_op jit(solution)/shard_map/hqk,khd->hqd/dot_general | solution.py:120
  314.3 43.9 %fusion.24 = f32[4,1024]{1,0:T(4,128)S(1)} fusion(f32[4,1024,8192]{2,1,0:T(8,128)} %get-tuple-element.461, f32[4,1024]{1,0:T(4,128)S(1)} %broadcast_maximum_fusion, pred[1024,8192]{1,0:T(8,128)(4,1)} %get-tuple-element.450), kind=kLoop, calls=%fused_computation.46 | loop fusion | flops 167768064 | bytes 142639104 | tf_op jit(solution)/shard_map/reduce_sum | solution.py:119
  358.3 51.0 %divide_convert_fusion = bf16[1024,4,64]{0,2,1:T(8,128)(2,1)} fusion(bf16[8192,4,64]{0,2,1:T(8,128)(2,1)} %bitcast.447, f32[4,1024,8192]{2,1,0:T(8,128)} %get-tuple-element.461, f32[4,1024]{1,0:T(4,128)S(1)} %broadcast_maximum_fusion, pred[1024,8192]{1,0:T(8,128)(4,1)} %get-tuple-element.450, f32[1024,4]{0,1:T(4,128)S(1)} %bitcast.459), kind=kOutput, calls=%fused_computation.205 | convolution fusion | flops 4463263744 | bytes 147357696 | tf_op jit(solution)/shard_map/hqk,khd->hqd/dot_general | solution.py:120
  412.4 21.8 %all-reduce.16.cloned.1.call-done = (bf16[1024,512]{1,0:T(8,128)(2,1)}, bf16[1024,512]{1,0:T(8,128)(2,1)}) async-done(((bf16[1024,512]{1,0:T(8,128)(2,1)}, bf16[1024,512]{1,0:T(8,128)(2,1)}), (bf16[1024,512]{1,0:T(8,128)(2,1)}, bf16[1024,512]{1,0:T(8,128)(2,1)})) %all-reduce.16.cloned.1.call-update) | async-done | bytes 2097168 | tf_op jit(solution)/shard_map/psum | solution.py:136
  462.8 15.3 all-reduce.14.cloned.1.call-done
  493.3 300.7 %while.30 = (s32[]{:T(128)}, f32[1024,4,64]{0,2,1:T(8,128)S(1)}, f32[16,512,256]{1,2,0:T(8,128)}, bf16[16,512,256]{1,2,0:T(8,128)(2,1)}, s32[16]{0:T(128)S(1)}, ...) while((s32[]{:T(128)}, f32[1024,4,64]{0,2,1:T(8,128)S(1)}, ...), condition=%wide.region_21.22_spmd.clone, body=%wide.region_20.21_spmd.clone.sunk | while | flops 1366820864 | bytes 135865776 | solution.py:236
  794.1 6.9 copy.56
  801.7 6.6 multiply_convert_fusion.1
  808.3 6.3 copy.55
  822.0 302.6 %while.31 = (s32[]{:T(128)}, f32[1024,4,64]{0,2,1:T(8,128)S(1)}, f32[16,512,256]{1,2,0:T(8,128)}, bf16[16,512,256]{1,2,0:T(8,128)(2,1)}, s32[16]{0:T(128)S(1)}, ...) while((s32[]{:T(128)}, f32[1024,4,64]{0,2,1:T(8,128)S(1)}, ...), condition=%wide.region_32.33_spmd.clone, body=%wide.region_31.32_spmd.clone.sunk | while | flops 1366820864 | bytes 135865776 | solution.py:236
  1124.6 6.8 copy.59
  1131.4 6.6 multiply_convert_fusion
  1138.0 6.4 copy.58
  1171.1 49.7 %reduce-scatter.11.cloned.1.call-done = bf16[1024,256]{1,0:T(8,128)(2,1)} async-done(((bf16[8192,256]{1,0:T(8,128)(2,1)}), bf16[1024,256]{1,0:T(8,128)(2,1)}) %reduce-scatter.11.cloned.1.call-update) | async-done | bytes 524304 | tf_op jit(solution)/shard_map/reduce_scatter | solution.py:245
  1220.8 91.7 %reduce-scatter.9.cloned.1.call-done = bf16[1024,256]{1,0:T(8,128)(2,1)} async-done(((bf16[8192,256]{1,0:T(8,128)(2,1)}), bf16[1024,256]{1,0:T(8,128)(2,1)}) %reduce-scatter.9.cloned.1.call-update) | async-done | bytes 524304 | tf_op jit(solution)/shard_map/reduce_scatter | solution.py:242
  1332.1 134.8 %all-reduce.10.cloned.1.call-done = (bf16[3,512,256]{1,2,0:T(8,128)(2,1)}, bf16[256,512]{1,0:T(8,128)(2,1)}, bf16[512,1024]{1,0:T(8,128)(2,1)}, bf16[1024,512]{1,0:T(8,128)(2,1)}) async-done(((bf16[3,512,256]{1,2,0:T(8,128)(2,1)}, bf16[256,512]{1,0:T(8,128)(2,1)}, bf16[512,1024]{1,0:T(8,128)(2,1)}, bf16[1024,512]{1,0:T(8,128)(2,1)}), (bf16[3,512,256]{1,2,0:T(8,128)(2,1)}, bf16[256,512]{1,0:T(8,128)(2,1)}, ...) | async-done | bytes 3145744 | tf_op jit(solution)/shard_map/psum | solution.py:276
  1474.8 23.3 %all-reduce.12.cloned.1.call-done = (bf16[1024,512]{1,0:T(8,128)(2,1)}, bf16[1024,512]{1,0:T(8,128)(2,1)}, bf16[1024,512]{1,0:T(8,128)(2,1)}, bf16[1024,512]{1,0:T(8,128)(2,1)}) async-done(((bf16[1024,512]{1,0:T(8,128)(2,1)}, bf16[1024,512]{1,0:T(8,128)(2,1)}, bf16[1024,512]{1,0:T(8,128)(2,1)}, bf16[1024,512]{1,0:T(8,128)(2,1)}), (bf16[1024,512]{1,0:T(8,128)(2,1)}, bf16[1024,512]{1,0:T(8,128)(2,1)}, ...) | async-done | bytes 4194320 | tf_op jit(solution)/shard_map/psum | solution.py:144
  1504.1 42.9 %all-reduce = (bf16[512]{0:T(512)(128)(2,1)S(1)}, bf16[512]{0:T(512)(128)(2,1)S(1)}, bf16[2,256]{1,0:T(2,128)(2,1)S(1)}, bf16[512]{0:T(512)(128)(2,1)S(1)}, bf16...) all-reduce(bf16[512]{0:T(512)(128)(2,1)S(1)} %add_convert_fusion.15, ...), channel_id=1, replica_groups=mesh['dp'=2,'seq'=8,'tensor'=2] {'dp','seq'}, use_global_device_ids=true, to_apply=%region_40.41 | all-reduce | flops 4608 | bytes 18432 | tf_op jit(solution)/shard_map/psum | solution.py:274
  (1116 shorter events, 730.4 us)
Async XLA Ops:
  7.2 431.0 %copy-start = (bf16[512,1024]{1,0:T(8,128)(2,1)S(1)}, bf16[512,1024]{1,0:T(8,128)(2,1)}, u32[]{:S(2)}) copy-start(bf16[512,1024]{1,0:T(8,128)(2,1)} %param.32) | copy-start | bytes 3145732
  7.2 109.2 %all-gather.11.cloned.1.call-start = ((), (), s32[]{:S(2)}) async-start(), calls=%async_computation.10 | async-start | bytes 4718592 | tf_op jit(solution)/shard_map/all_gather | solution.py:100
  14.5 152.3 %all-gather.13.cloned.1.call-start = ((), (), s32[]{:S(2)}) async-start(), calls=%async_computation.11 | async-start | bytes 4718592 | tf_op jit(solution)/shard_map/all_gather | solution.py:100
  19.6 242.0 %all-gather.7.cloned.1.call-start = ((), (), s32[]{:S(2)}) async-start(), calls=%async_computation.4 | async-start | bytes 4718592 | tf_op jit(solution)/shard_map/all_gather | solution.py:101
  22.4 335.8 %all-gather.9.cloned.1.call-start = ((), (), s32[]{:S(2)}) async-start(), calls=%async_computation.5 | async-start | bytes 4718592 | tf_op jit(solution)/shard_map/all_gather | solution.py:101
  23.0 411.1 %all-reduce.16.cloned.1.call-start = ((), (), s32[]{:S(2)}) async-start(), calls=%async_computation.15 | async-start | bytes 4194304 | tf_op jit(solution)/shard_map/psum | solution.py:136
  58.3 58.2 %copy-start.58 = (s32[1,8192]{1,0:T(1,128)}, s32[1,8192]{1,0:T(1,128)S(1)}, u32[]{:S(2)}) copy-start(s32[1,8192]{1,0:T(1,128)S(1)} %get-tuple-element.444) | copy-start | bytes 98308
  58.3 58.2 %copy-start.59 = (s32[1,8192]{1,0:T(1,128)}, s32[1,8192]{1,0:T(1,128)S(1)}, u32[]{:S(2)}) copy-start(s32[1,8192]{1,0:T(1,128)S(1)} %get-tuple-element.445) | copy-start | bytes 98308
  91.9 74.9 %copy-start.14 = (bf16[1024,4,64]{0,2,1:T(8,128)(2,1)}, bf16[1024,4,64]{0,2,1:T(8,128)(2,1)S(1)}, u32[]{:S(2)}) copy-start(bf16[1024,4,64]{0,2,1:T(8,128)(2,1)S(1)} %get-tuple-element.672) | copy-start | bytes 1572868
  166.5 50.5 %copy-start.68 = (f32[4,1024]{1,0:T(4,128)}, f32[4,1024]{1,0:T(4,128)S(1)}, u32[]{:S(2)}) copy-start(f32[4,1024]{1,0:T(4,128)S(1)} %get-tuple-element.458) | copy-start | bytes 49156
  261.6 51.3 %copy-start.64 = (f32[4,1024]{1,0:T(4,128)}, f32[4,1024]{1,0:T(4,128)S(1)}, u32[]{:S(2)}) copy-start(f32[4,1024]{1,0:T(4,128)S(1)} %fusion.22) | copy-start | bytes 49156
  261.6 51.2 %copy-start.37 = (bf16[256,512]{1,0:T(8,128)(2,1)S(1)}, bf16[256,512]{1,0:T(8,128)(2,1)}, u32[]{:S(2)}) copy-start(bf16[256,512]{1,0:T(8,128)(2,1)} %param.28) | copy-start | bytes 786436
  312.9 45.4 %copy-start.32 = (bf16[1024,4,64]{0,2,1:T(8,128)(2,1)}, bf16[1024,4,64]{0,2,1:T(8,128)(2,1)S(1)}, u32[]{:S(2)}) copy-start(bf16[1024,4,64]{0,2,1:T(8,128)(2,1)S(1)} %divide_convert_fusion.1) | copy-start | bytes 1572868
  411.9 66.2 %all-reduce.14.cloned.1.call-start = ((), (), s32[]{:S(2)}) async-start(), calls=%async_computation.14 | async-start | bytes 4194304 | tf_op jit(solution)/shard_map/psum | solution.py:158
  436.6 46.7 %copy-start.72 = (f32[1024]{0:T(1024)}, f32[1024]{0:T(1024)S(1)}, u32[]{:S(2)}) copy-start(f32[1024]{0:T(1024)S(1)} %broadcast_multiply_fusion.10) | copy-start | bytes 12292
  436.7 46.6 %copy-start.70 = (f32[1024]{0:T(1024)}, f32[1024]{0:T(1024)S(1)}, u32[]{:S(2)}) copy-start(f32[1024]{0:T(1024)S(1)} %broadcast_multiply_fusion.8) | copy-start | bytes 12292
  455.5 711.9 %reduce-scatter.7.cloned.1.call-start = ((), (), s32[]{:S(2)}) async-start(), calls=%async_computation.7 | async-start | bytes 4718592 | tf_op jit(solution)/shard_map/reduce_scatter | solution.py:245
  801.0 366.4 %reduce-scatter.5.cloned.1.call-start = ((), (), s32[]{:S(2)}) async-start(), calls=%async_computation.6 | async-start | bytes 4718592 | tf_op jit(solution)/shard_map/reduce_scatter | solution.py:242
  817.5 403.2 %reduce-scatter.11.cloned.1.call-start = ((), (), s32[]{:S(2)}) async-start(), calls=%async_computation.9 | async-start | bytes 4718592 | tf_op jit(solution)/shard_map/reduce_scatter | solution.py:245
  1131.4 181.1 %reduce-scatter.9.cloned.1.call-start = ((), (), s32[]{:S(2)}) async-start(), calls=%async_computation.8 | async-start | bytes 4718592 | tf_op jit(solution)/shard_map/reduce_scatter | solution.py:242
  1144.4 322.5 %all-reduce.10.cloned.1.call-start = ((), (), s32[]{:S(2)}) async-start(), calls=%async_computation.12 | async-start | bytes 6291456 | tf_op jit(solution)/shard_map/psum | solution.py:276
  1167.4 145.2 %copy-start.61 = (f32[1024]{0:T(1024)S(1)}, f32[1024]{0:T(1024)}, u32[]{:S(2)}) copy-start(f32[1024]{0:T(1024)} %copy-done.60) | copy-start | bytes 12292
  1167.4 145.1 %copy-start.79 = (f32[1024]{0:T(1024)S(1)}, f32[1024]{0:T(1024)}, u32[]{:S(2)}) copy-start(f32[1024]{0:T(1024)} %copy-done.78) | copy-start | bytes 12292
  1316.5 181.5 %all-reduce.12.cloned.1.call-start = ((), (), s32[]{:S(2)}) async-start(), calls=%async_computation.13 | async-start | bytes 8388608 | tf_op jit(solution)/shard_map/psum | solution.py:144
  (256 other events, 1247.9 us)
Sparse Core Ops, SparseCore 0:
  14.6 77.5 all-gather.10
  95.0 71.6 all-gather.12
  169.5 71.6 all-gather.6
  243.8 71.6 all-gather.8
  412.0 22.0 all-reduce.15
  455.6 22.4 all-reduce.13
  801.1 89.2 reduce-scatter.6
  894.4 87.8 reduce-scatter.4
  1131.5 89.2 reduce-scatter.10
  1224.7 87.7 reduce-scatter.8
  1319.1 147.7 all-reduce.9
  1470.3 27.6 all-reduce.11
where the time goes:
time: 1570 us
  matrix products  660 us (42%)
  waiting for transfers between devices  338 us (22%)
  local copies, waits for them, and re-layouts  215 us (14%)
  other arithmetic  207 us (13%)
  blocking collectives  107 us (7%)
  loops' own time  23.1 us (1%)
    dot_general x32, matrix products, key_step(): jnp.einsum('qhd,khd->hqk', grad_heads, value_part, preferred_element_type...  148 us
    psum x1, waiting for transfers between devices, on_device(): lax.psum(sums[2].astype(jnp.bfloat16), ('dp', 'seq')).astype(jnp.float32)  135 us
    dot_general x32, matrix products, key_step(): jnp.einsum('hqk,khd->qhd', grad_scores, key_part, preferred_element_type=...  105 us
    dot_general x2, matrix products, on_device(): jnp.einsum('hqk,khd->hqd', weights.astype(jnp.bfloat16), value_part.resha...  102 us
    dot_general x2, matrix products, on_device(): jnp.einsum('qhd,khd->hqk', query_heads, key_part.reshape(row_count, heads...  100 us
    reduce_scatter x2, waiting for transfers between devices, on_device(): lax.psum_scatter(key_terms.astype(jnp.bfloat16), 'seq', scatter_dimension...  91.7 us
    reduce_sum x2, other arithmetic, on_device(): weight_sum = jnp.sum(weights, -1)  87.9 us
    dot_general x32, matrix products, key_step(): jnp.einsum('hqk,qhd->khd', probs.astype(jnp.bfloat16), grad_heads, prefer...  58.4 us
  transfers between devices with their start and end apart: 12, of which 7 were waited for; matrix products, arithmetic and copies ran while one was open for 41% of the time, Pallas kernels for 0%

commit v1 on v0

--- a/solution.py
+++ b/solution.py
@@ -1,13 +1,20 @@
+import functools
+
 import jax
 import jax.numpy as jnp
 from jax import lax
+from jax.experimental import pallas as pl
+from jax.experimental.pallas import tpu as pltpu
 from jax.sharding import PartitionSpec as P
 
 HEAD_DIM = 64
-
-
 EPSILON = 1e-05
 MASKED = -1e30
+DOC_IDS = 16
+TILE = 512
+ALL_AXES = ("dp", "seq", "tensor")
+BF16 = jnp.bfloat16
+F32 = jnp.float32
 
 
 def layer_norm(rows, gain, offset):
@@ -29,6 +36,580 @@
 def gelu_parts(pre_act):
     sigma = jax.nn.sigmoid(1.702 * pre_act)
     return (pre_act * sigma, sigma + 1.702 * pre_act * sigma * (1.0 - sigma))
+
+
+def dot(a, b, ca, cb):
+    return lax.dot_general(a, b, (((ca,), (cb,)), ((), ())), preferred_element_type=F32)
+
+
+def blocks_of(pieces, place_ref, block):
+    per_piece = pieces[0].shape[1] // block
+    for piece_at, piece in enumerate(pieces):
+        for block_at in range(per_piece):
+            start = pl.multiple_of(place_ref[piece_at * per_piece + block_at] * block, block)
+            yield piece, slice(block_at * block, (block_at + 1) * block), pl.ds(start, block)
+
+
+def doc_features(code):
+    ids = lax.broadcasted_iota(jnp.int32, (DOC_IDS, code.shape[1]), 0)
+    same = ids == (code >> 1)
+    as_query = same.astype(F32)
+    as_key = jnp.where(same & ((code & 1) == 1), 0.0, MASKED)
+    return as_query.astype(BF16), as_key.astype(BF16)
+
+
+def mask_diagonal(score_ref, own_score):
+    step = 128
+    row = lax.broadcasted_iota(jnp.int32, (step, step), 0)
+    col = lax.broadcasted_iota(jnp.int32, (step, step), 1)
+    for k in range(TILE // step):
+        for q in range(TILE // step):
+            part = (slice(k * step, (k + 1) * step), slice(q * step, (q + 1) * step))
+            if k > q:
+                score_ref[part] = jnp.full((step, step), MASKED, F32)
+            elif k == q:
+                own = own_score[:, q * step : (q + 1) * step]
+                score_ref[part] = jnp.where(
+                    row < col, score_ref[part], jnp.where(row == col, own, MASKED)
+                )
+
+
+def at(index):
+    return pl.ds(pl.multiple_of(index * TILE, TILE), TILE)
+
+
+def forward_kernel(block, table_ref, place_ref, code_ref, *refs):
+    pieces, outs, lse_ref = refs[:8], refs[8:16], refs[16]
+    query_t, key_t, value_t, key_row, out_t, score_a, score_b, accum, peak = refs[17:]
+    feats = HEAD_DIM
+    ones = jnp.ones((16, block), BF16)
+    for piece, cols, span in blocks_of(pieces, place_ref, block):
+        as_query, as_key = doc_features(code_ref[:, span])
+        part = piece[feats : 2 * feats, cols]
+        query_t[0:feats, span] = piece[0:feats, cols]
+        query_t[feats:, span] = as_query
+        key_t[:, span] = part
+        key_row[span, :] = jnp.concatenate([part, as_key], axis=0).T
+        value_t[0:feats, span] = piece[2 * feats : 3 * feats, cols]
+        value_t[feats:, span] = ones
+    accum[...] = jnp.zeros_like(accum)
+    peak[...] = jnp.full_like(peak, MASKED)
+
+    def score(step, out_ref):
+        out_ref[...] = dot(key_row[at(table_ref[1, step]), :], query_t[:, at(table_ref[0, step])], 1, 0)
+
+    def one(step, now, later):
+        query_at, key_at = table_ref[0, step], table_ref[1, step]
+        first = table_ref[2, step]
+
+        @pl.when(first == 1)
+        def _():
+            own = jnp.sum(
+                query_t[0:feats, at(query_at)].astype(F32) * key_t[:, at(query_at)].astype(F32),
+                axis=0,
+                keepdims=True,
+            )
+            mask_diagonal(now, own)
+
+        score(step + 1, later)
+        scores = now[...]
+        old = jnp.where(first == 1, MASKED, peak[0:1, :])
+        new = jnp.maximum(old, jnp.max(scores, axis=0, keepdims=True))
+        weights = jnp.exp(scores - new).astype(BF16)
+        accum[...] = accum[...] * jnp.exp(old - new) + dot(value_t[:, at(key_at)], weights, 1, 0)
+        peak[0:1, :] = new
+
+        @pl.when(table_ref[3, step] == 1)
+        def _():
+            total = accum[feats : feats + 1, :]
+            out_t[:, at(query_at)] = (accum[0:feats, :] / total).astype(BF16)
+            lse_ref[:, at(query_at)] = peak[0:1, :] + jnp.log(total)
+
+    score(0, score_a)
+
+    def pair(index, carry):
+        one(2 * index, score_a, score_b)
+        one(2 * index + 1, score_b, score_a)
+        return carry
+
+    lax.fori_loop(0, table_ref[4, 0], pair, 0)
+    for piece, cols, span in blocks_of(outs, place_ref, block):
+        piece[:, cols] = out_t[:, span]
+
+
+def backward_kernel(block, table_ref, place_ref, code_ref, lse_ref, *refs):
+    pieces, mixed, grads, outs = refs[:8], refs[8:16], refs[16:24], refs[24:32]
+    (query_t, key_t, grad_t, key_row, value_row, query_row, grad_row, delta,
+     sum_q, sum_k, sum_v, score_a, score_b, dp_a, dp_b) = refs[32:]
+    feats = HEAD_DIM
+    for (piece, cols, span), (grad, _, _), (out, _, _) in zip(
+        blocks_of(pieces, place_ref, block),
+        blocks_of(grads, place_ref, block),
+        blocks_of(mixed, place_ref, block),
+    ):
+        as_query, as_key = doc_features(code_ref[:, span])
+        part_q, part_k = piece[0:feats, cols], piece[feats : 2 * feats, cols]
+        part_g = grad[:, cols]
+        query_t[0:feats, span] = part_q
+        query_t[feats:, span] = as_query
+        key_t[:, span] = part_k
+        grad_t[:, span] = part_g
+        key_row[span, :] = jnp.concatenate([part_k, as_key], axis=0).T
+        value_row[span, :] = piece[2 * feats : 3 * feats, cols].T
+        query_row[span, :] = part_q.T
+        grad_row[span, :] = part_g.T
+        delta[:, span] = jnp.sum(
+            part_g.astype(F32) * out[:, cols].astype(F32), axis=0, keepdims=True
+        )
+    sum_q[...] = jnp.zeros_like(sum_q)
+    sum_k[...] = jnp.zeros_like(sum_k)
+    sum_v[...] = jnp.zeros_like(sum_v)
+
+    def products(step, score_ref, dp_ref):
+        queries, keys = at(table_ref[0, step]), at(table_ref[1, step])
+        score_ref[...] = dot(key_row[keys, :], query_t[:, queries], 1, 0)
+        dp_ref[...] = dot(value_row[keys, :], grad_t[:, queries], 1, 0)
+
+    def one(step, score_now, dp_now, score_later, dp_later):
+        query_at = table_ref[0, step]
+        queries, keys, sink = at(query_at), at(table_ref[1, step]), at(table_ref[5, step])
+
+        @pl.when(table_ref[2, step] == 1)
+        def _():
+            own = jnp.sum(
+                query_t[0:feats, queries].astype(F32) * key_t[:, queries].astype(F32),
+                axis=0,
+                keepdims=True,
+            )
+            mask_diagonal(score_now, own)
+
+        products(step + 1, score_later, dp_later)
+        probs = jnp.exp(score_now[...] - lse_ref[:, queries])
+        grad_scores = (probs * (dp_now[...] - delta[:, queries])).astype(BF16)
+        sum_v[sink, :] += dot(probs.astype(BF16), grad_row[queries, :], 1, 0)
+        sum_k[sink, :] += dot(grad_scores, query_row[queries, :], 1, 0)
+        sum_q[:, at(table_ref[6, step])] += dot(key_t[:, keys], grad_scores, 1, 0)
+
+    products(0, score_a, dp_a)
+
+    def pair(index, carry):
+        one(2 * index, score_a, dp_a, score_b, dp_b)
+        one(2 * index + 1, score_b, dp_b, score_a, dp_a)
+        return carry
+
+    lax.fori_loop(0, table_ref[4, 0], pair, 0)
+    for piece, cols, span in blocks_of(outs, place_ref, block):
+        piece[0:feats, cols] = sum_q[:, span].astype(BF16)
+        piece[feats : 2 * feats, cols] = sum_k[span, :].T.astype(BF16)
+        piece[2 * feats : 3 * feats, cols] = sum_v[span, :].T.astype(BF16)
+
+
+def vmem():
+    return pl.BlockSpec(memory_space=pltpu.VMEM)
+
+
+def smem():
+    return pl.BlockSpec(memory_space=pltpu.SMEM)
+
+
+def attention_forward(table, place, code, pieces, block):
+    length, part = code.shape[1], pieces[0].shape[1]
+    pairs = (length // TILE) * 4
+    wide = HEAD_DIM + DOC_IDS
+    out = pl.pallas_call(
+        functools.partial(forward_kernel, block),
+        out_shape=[jax.ShapeDtypeStruct((HEAD_DIM, part), BF16)] * 8
+        + [jax.ShapeDtypeStruct((1, length), F32)],
+        in_specs=[smem(), smem()] + [vmem()] * 9,
+        out_specs=[vmem()] * 9,
+        scratch_shapes=[
+            pltpu.VMEM((wide, length), BF16),
+            pltpu.VMEM((HEAD_DIM, length), BF16),
+            pltpu.VMEM((HEAD_DIM + 16, length), BF16),
+            pltpu.VMEM((length, wide), BF16),
+            pltpu.VMEM((HEAD_DIM, length), BF16),
+            pltpu.VMEM((TILE, TILE), F32),
+            pltpu.VMEM((TILE, TILE), F32),
+            pltpu.VMEM((HEAD_DIM + 16, TILE), F32),
+            pltpu.VMEM((8, TILE), F32),
+        ],
+        compiler_params=pltpu.CompilerParams(vmem_limit_bytes=40 << 20),
+        cost_estimate=pl.CostEstimate(
+            flops=pairs * 4 * TILE * TILE * HEAD_DIM,
+            bytes_accessed=8 * length * HEAD_DIM,
+            transcendentals=pairs * TILE * TILE,
+        ),
+        name="attention_forward",
+    )(table, place, code, *pieces)
+    return out[:8], out[8]
+
+
+def attention_backward(table, place, code, lse, pieces, mixed, grads, block):
+    length, part = code.shape[1], pieces[0].shape[1]
+    pairs = (length // TILE) * 4
+    wide = HEAD_DIM + DOC_IDS
+    return pl.pallas_call(
+        functools.partial(backward_kernel, block),
+        out_shape=[jax.ShapeDtypeStruct((3 * HEAD_DIM, part), BF16)] * 8,
+        in_specs=[smem(), smem()] + [vmem()] * 26,
+        out_specs=[vmem()] * 8,
+        scratch_shapes=[
+            pltpu.VMEM((wide, length), BF16),
+            pltpu.VMEM((HEAD_DIM, length), BF16),
+            pltpu.VMEM((HEAD_DIM, length), BF16),
+            pltpu.VMEM((length, wide), BF16),
+            pltpu.VMEM((length, HEAD_DIM), BF16),
+            pltpu.VMEM((length, HEAD_DIM), BF16),
+            pltpu.VMEM((length, HEAD_DIM), BF16),
+            pltpu.VMEM((1, length), F32),
+            pltpu.VMEM((HEAD_DIM, length + TILE), F32),
+            pltpu.VMEM((length + TILE, HEAD_DIM), F32),
+            pltpu.VMEM((length + TILE, HEAD_DIM), F32),
+            pltpu.VMEM((TILE, TILE), F32),
+            pltpu.VMEM((TILE, TILE), F32),
+            pltpu.VMEM((TILE, TILE), F32),
+            pltpu.VMEM((TILE, TILE), F32),
+        ],
+        compiler_params=pltpu.CompilerParams(vmem_limit_bytes=56 << 20),
+        cost_estimate=pl.CostEstimate(
+            flops=pairs * 10 * TILE * TILE * HEAD_DIM,
+            bytes_accessed=16 * length * HEAD_DIM,
+            transcendentals=pairs * TILE * TILE,
+        ),
+        name="attention_backward",
+    )(table, place, code, lse, *pieces, *mixed, *grads)
+
+
+def tile_table(segment_row):
+    length = segment_row.shape[0]
+    tiles = length // TILE
+    steps = (tiles * (tiles + 1) // 2 + 2 + 127) // 128 * 128
+    index = jnp.arange(tiles, dtype=jnp.int32)
+    doc_start = jnp.sum(
+        (segment_row[None, :] < segment_row[::TILE][:, None]).astype(jnp.int32), axis=1
+    )
+    low = doc_start // TILE
+    count = index - low + 1
+    ends = jnp.sum(jnp.where(index[None, :] <= index[:, None], count[None, :], 0), axis=1)
+    total = jnp.sum(count)
+    step = jnp.arange(steps, dtype=jnp.int32)
+    live = step < total
+    held = jnp.minimum(step, total - 1)
+    query = jnp.sum((ends[None, :] <= held[:, None]).astype(jnp.int32), axis=1)
+    chosen = query[:, None] == index[None, :]
+    begin = jnp.sum(jnp.where(chosen, (ends - count)[None, :], 0), axis=1)
+    lowest = jnp.sum(jnp.where(chosen, low[None, :], 0), axis=1)
+    rank = held - begin
+    key = jnp.where(rank == 0, query, lowest + rank - 1)
+    first = ((rank == 0) & live).astype(jnp.int32)
+    last = ((rank == query - lowest) & live).astype(jnp.int32)
+    trash = jnp.where(live, key, tiles)
+    trash_query = jnp.where(live, query, tiles)
+    pairs = jnp.broadcast_to((total + 1) // 2, (steps,))
+    return jnp.stack([query, key, first, last, pairs, trash, trash_query, held]).astype(jnp.int32)
+
+
+def project_kernel(gain_ref, offset_ref, weight_ref, bias_ref, *refs):
+    blocks, outs, normed_ref = refs[:2], refs[2:10], refs[10]
+    for block_at, block in enumerate(blocks):
+        size = block.shape[0]
+        span = slice(block_at * size, (block_at + 1) * size)
+        hidden, normed, _ = layer_norm(block[...].astype(F32), gain_ref[...], offset_ref[...])
+        normed_ref[span, :] = normed.astype(BF16)
+        hidden = hidden.astype(BF16)
+        for step, out in enumerate(outs):
+            out[:, span] = (dot(weight_ref[step], hidden, 1, 1) + bias_ref[step]).astype(BF16)
+
+
+def project(gain, offset, weight, bias, blocks):
+    rows, width = 2 * blocks[0].shape[0], blocks[0].shape[1]
+    out = pl.pallas_call(
+        project_kernel,
+        out_shape=[jax.ShapeDtypeStruct((weight.shape[1], rows), BF16)] * 8
+        + [jax.ShapeDtypeStruct((rows, width), BF16)],
+        in_specs=[vmem()] * 6,
+        out_specs=[vmem()] * 9,
+        compiler_params=pltpu.CompilerParams(vmem_limit_bytes=40 << 20),
+        cost_estimate=pl.CostEstimate(
+            flops=2 * rows * weight.size, bytes_accessed=2 * weight.size, transcendentals=0
+        ),
+        name="project",
+    )(gain[None], offset[None], weight, bias[:, :, None], *blocks)
+    return out[:8], out[8]
+
+
+def tail_kernel(gain_ref, weight_ref, middle_ref, *refs):
+    blocks, grads, outs = refs[:2], refs[2:10], refs[10:12]
+    gain = gain_ref[...]
+    for block_at, (block, out) in enumerate(zip(blocks, outs)):
+        size = block.shape[0]
+        span = slice(block_at * size, (block_at + 1) * size)
+        _, normed, rstd = layer_norm(block[...].astype(F32), gain, gain)
+        hidden_grad = sum(dot(grad[:, span], weight_ref[step], 0, 0) for step, grad in enumerate(grads))
+        out[...] = (middle_ref[span, :] + norm_back(hidden_grad, normed, rstd, gain)).astype(BF16)
+
+
+def tail(gain, weight, grad_middle, blocks, grads):
+    return pl.pallas_call(
+        tail_kernel,
+        out_shape=[jax.ShapeDtypeStruct(blocks[0].shape, BF16)] * 2,
+        in_specs=[vmem()] * 13,
+        out_specs=[vmem()] * 2,
+        compiler_params=pltpu.CompilerParams(vmem_limit_bytes=40 << 20),
+        cost_estimate=pl.CostEstimate(
+            flops=2 * grad_middle.shape[0] * weight.size,
+            bytes_accessed=2 * weight.size,
+            transcendentals=0,
+        ),
+        name="tail",
+    )(gain[None], weight, grad_middle, *blocks, *grads)
+
+
+def group_pairs(step):
+    pairs = []
+    for device in range(32):
+        y, z, x, core = device >> 4, (device >> 2) & 3, (device >> 1) & 1, device & 1
+        z, x, core = z ^ (step & 1), x ^ ((step >> 1) & 1), core ^ (step >> 2)
+        pairs.append((device, (y << 4) | (z << 2) | (x << 1) | core))
+    return pairs
+
+
+def across(array):
+    return lax.ppermute(array, "seq", [(i, i ^ 4) for i in range(8)])
+
+
+def exchange(pieces):
+    return [pieces[0]] + [
+        lax.ppermute(pieces[step], ALL_AXES, group_pairs(step)) for step in range(1, 8)
+    ]
+
+
+def swap(array):
+    return lax.ppermute(array, "tensor", [(0, 1), (1, 0)])
+
+
+def pick(array, first, second):
+    array = lax.dynamic_index_in_dim(array, first, 0, keepdims=False)
+    return lax.dynamic_index_in_dim(array, second, 0, keepdims=False)
+
+
+def to_group(array, half, core):
+    parts = array.reshape(2, 2, -1, array.shape[2])
+    return [pick(parts, half, core), across(pick(parts, 1 - half, core))]
+
+
+def tie(*values):
+    return lax.optimization_barrier(values)
+
+
+def scatter_sum(array, part):
+    halves = array.astype(BF16).reshape((2, -1) + array.shape[1:])
+    mine = lax.dynamic_index_in_dim(halves, part, 0, keepdims=False)
+    other = lax.dynamic_index_in_dim(halves, 1 - part, 0, keepdims=False)
+    return mine + lax.ppermute(other, "dp", [(0, 1), (1, 0)])
+
+
+def gather_halves(array, part):
+    other = lax.ppermute(array, "dp", [(0, 1), (1, 0)])
+    low = jnp.where(part == 0, array, other)
+    high = jnp.where(part == 0, other, array)
+    return jnp.concatenate([low, high], axis=0).astype(F32)
+
+
+def from_group(mine, back, half, core):
+    both = jnp.stack([jnp.where(half == 0, mine, back), jnp.where(half == 0, back, mine)])
+    other = swap(both)
+    low = jnp.where(core == 0, both, other)
+    high = jnp.where(core == 0, other, both)
+    return jnp.stack([low, high], axis=1).reshape(2, -1, mine.shape[1])
+
+
+def on_groups(
+    tokens,
+    segments,
+    keep_mask,
+    cotangent,
+    ln1_gain,
+    ln1_bias,
+    w_qkv,
+    qv_bias,
+    w_out,
+    b_out,
+    ln2_gain,
+    ln2_bias,
+    w_fc,
+    b_fc,
+    w_proj,
+    b_proj,
+):
+    width = tokens.shape[2]
+    block = tokens.shape[1] // 2
+    feats = HEAD_DIM
+    piece_at = lax.axis_index("seq")
+    core = lax.axis_index("tensor")
+    z, x = piece_at >> 1, piece_at & 1
+    half = z >> 1
+    chip = 2 * x + (z & 1)
+
+    token_blocks = to_group(tokens, half, core)
+
+    code = (segments * 2 + keep_mask)[None]
+    for bit in (1, 2, 4):
+        code = jnp.concatenate(
+            [code, lax.ppermute(code, "seq", [(i, i ^ bit) for i in range(8)])], axis=0
+        )
+    code = lax.dynamic_index_in_dim(code, half, 1, keepdims=False)
+    code = jnp.take(code, jnp.arange(8) ^ piece_at, axis=0).reshape(1, -1)
+    table = tile_table(code[0] >> 1)
+    steps = jnp.arange(8)[:, None]
+    their_z = z ^ (steps & 1) ^ (2 * jnp.arange(2)[None, :])
+    their_x, their_core = x ^ ((steps >> 1) & 1), core ^ (steps >> 2)
+    place = (4 * their_z + 2 * their_x + their_core).reshape(16).astype(jnp.int32)
+
+    order = jnp.arange(4) ^ chip
+    heads_w = jnp.take(
+        w_qkv.reshape(3, width, 4, feats).transpose(2, 0, 3, 1), order, axis=0
+    )
+    heads_w = heads_w * jnp.array([feats**-0.5, 1.0, 1.0], BF16)[None, :, None, None]
+    heads_w = heads_w.reshape(4, 3 * feats, width)
+    heads_w = jnp.concatenate([heads_w, swap(heads_w)], axis=0)
+    bias = jnp.take(qv_bias.reshape(2, 4, feats).transpose(1, 0, 2), order, axis=0)
+    bias = jnp.stack([bias[:, 0] * feats**-0.5, jnp.zeros_like(bias[:, 0]), bias[:, 1]], axis=1)
+    bias = bias.reshape(4, 3 * feats)
+    bias = jnp.concatenate([bias, swap(bias)], axis=0)
+    heads_out = jnp.take(w_out.reshape(4, feats, width), order, axis=0)
+    heads_out = jnp.concatenate([heads_out, swap(heads_out)], axis=0).reshape(8 * feats, width)
+    fcs = (w_fc, swap(w_fc))
+    projs = (w_proj, swap(w_proj))
+    fc_biases = (b_fc, swap(b_fc))
+
+    pieces, shared = project(ln1_gain, ln1_bias, heads_w, bias, token_blocks)
+    pieces = exchange(pieces)
+    pieces, cotangent, shared = tie(pieces, cotangent, shared)
+    grad_blocks = to_group(cotangent, half, core)
+    shared_x = lax.ppermute(shared, ALL_AXES, group_pairs(2))
+    outs, lse = attention_forward(table, place, code, pieces, block)
+    outs, grad_blocks, shared_x = tie(outs, grad_blocks, shared_x)
+    mixed = exchange(outs)
+    mixed, shared = tie(mixed, shared)
+    shared = [shared, lax.ppermute(shared, ALL_AXES, group_pairs(1)), shared_x,
+              lax.ppermute(shared, ALL_AXES, group_pairs(3))]
+    mixed_t = jnp.concatenate(mixed, axis=0)
+
+    rows = jnp.concatenate(token_blocks, axis=0).astype(F32)
+    middle = rows + jnp.einsum("fr,fd->rd", mixed_t, heads_out, preferred_element_type=F32) + b_out
+    normed_two_out, normed_two, rstd_two = layer_norm(middle, ln2_gain, ln2_bias)
+    hidden_two = normed_two_out.astype(BF16)
+    grad_out = jnp.concatenate(grad_blocks, axis=0)
+    grad_wide = grad_out.astype(F32)
+    feed = b_proj
+    grad_hidden_two = 0.0
+    acts, grad_pres = [], []
+    for fc, fc_bias, proj in zip(fcs, fc_biases, projs):
+        pre_act = jnp.dot(hidden_two, fc, preferred_element_type=F32) + fc_bias
+        activated, slope = gelu_parts(pre_act)
+        acts.append(activated.astype(BF16))
+        feed = feed + jnp.dot(acts[-1], proj, preferred_element_type=F32)
+        grad_act = jnp.einsum("td,fd->tf", grad_out, proj, preferred_element_type=F32)
+        grad_pres.append((grad_act * slope).astype(BF16))
+        grad_hidden_two = grad_hidden_two + jnp.einsum(
+            "tf,ef->te", grad_pres[-1], fc, preferred_element_type=F32
+        )
+    layer_rows = (middle + feed).astype(BF16)
+    grad_middle = grad_wide + norm_back(grad_hidden_two, normed_two, rstd_two, ln2_gain)
+    grad_branch = grad_middle.astype(BF16)
+    grad_mixed_t = jnp.einsum(
+        "fd,rd->fr", heads_out, grad_branch, preferred_element_type=F32
+    ).astype(BF16)
+    grad_pieces = exchange([grad_mixed_t[i * feats : (i + 1) * feats] for i in range(8)])
+
+    def both(mine, other):
+        return mine + swap(other.astype(BF16)).astype(F32)
+
+    proj_sum = both(*[
+        jnp.einsum("tf,td->fd", act, grad_out, preferred_element_type=F32) for act in acts
+    ])
+    fc_sum = both(*[
+        jnp.einsum("te,tf->ef", hidden_two, grad, preferred_element_type=F32) for grad in grad_pres
+    ])
+    out_sum = jnp.einsum("fr,rd->fd", mixed_t, grad_branch, preferred_element_type=F32)
+    out_sum = both(out_sum[: 4 * feats], out_sum[4 * feats :])
+    out_sum = jnp.take(out_sum.reshape(4, feats, width), order, axis=0).reshape(4 * feats, width)
+    fc_bias_sum = both(*[jnp.sum(grad.astype(F32), 0) for grad in grad_pres])
+    vectors = jnp.stack([
+        jnp.sum(grad_wide, 0),
+        jnp.sum(grad_branch.astype(F32), 0),
+        jnp.sum(grad_hidden_two * normed_two, 0),
+        jnp.sum(grad_hidden_two, 0),
+    ])
+    vectors = both(vectors, vectors)
+    early = [fc_sum, proj_sum, jnp.concatenate(
+        [out_sum, vectors, fc_bias_sum.reshape(-1, width), jnp.zeros((10, width), F32)], axis=0
+    )]
+    early = [scatter_sum(part, lax.axis_index("dp")) for part in early]
+    grad_pieces, shared, early, layer_rows = tie(grad_pieces, shared, early, layer_rows)
+    early = lax.psum(early, "seq")
+    layer_back = across(layer_rows[block:])
+    head_grads = attention_backward(table, place, code, lse, pieces, outs, grad_pieces, block)
+    head_grads, layer_back = tie(head_grads, layer_back)
+    grads = exchange(head_grads)
+    layer_out = from_group(layer_rows[:block], layer_back, half, core)
+    grads, early = tie(grads, early)
+    early = [gather_halves(part, lax.axis_index("dp")) for part in early]
+    grad_rows = tail(ln1_gain, heads_w, grad_middle, token_blocks, grads)
+    grad_tokens = from_group(grad_rows[0], across(grad_rows[1]), half, core)
+
+    shared = shared + [swap(part) for part in shared]
+    with_normed = sum(dot(grad, part, 1, 0) for grad, part in zip(head_grads, shared))
+    with_ones = sum(jnp.sum(grad.astype(F32), axis=1) for grad in head_grads)
+    late = jnp.concatenate([
+        with_normed,
+        jnp.pad(with_ones, (0, width - 3 * feats))[None],
+        jnp.zeros((15, width), F32),
+    ], axis=0)
+    late = late + lax.ppermute(late.astype(BF16), "dp", [(0, 1), (1, 0)]).astype(F32)
+    late = late + across(late.astype(BF16)).astype(F32)
+    with_normed, with_ones = late[: 3 * feats], late[3 * feats, : 3 * feats]
+    mine = heads_w[0].astype(F32)
+    late = jnp.concatenate([
+        with_normed * ln1_gain + with_ones[:, None] * ln1_bias,
+        jnp.pad(with_ones, (0, width - 3 * feats))[None],
+        jnp.sum(mine * with_normed, axis=0)[None],
+        jnp.sum(mine * with_ones[:, None], axis=0)[None],
+        jnp.zeros((13, width), F32),
+    ], axis=0).astype(BF16)[None]
+    for bit in (2, 1):
+        late = jnp.concatenate(
+            [late, lax.ppermute(late, "seq", [(i, i ^ bit) for i in range(8)])], axis=0
+        )
+    late = late.astype(F32)
+    ln1_sums = jnp.sum(late[:, 3 * feats + 1 : 3 * feats + 3], axis=0)
+    ln1_sums = ln1_sums + swap(ln1_sums)
+    late = jnp.take(late, order, axis=0)
+    scale = jnp.array([feats**-0.5, 1.0, 1.0], F32)
+    qkv_grad = late[:, : 3 * feats].reshape(4, 3, feats, width) * scale[None, :, None, None]
+    qkv_grad = qkv_grad.transpose(1, 3, 0, 2).reshape(3, width, 4 * feats)
+    bias_grad = late[:, 3 * feats, : 3 * feats].reshape(4, 3, feats)
+    bias_grad = jnp.stack([bias_grad[:, 0] * feats**-0.5, bias_grad[:, 2]]).reshape(2, 4 * feats)
+
+    rest = early[2][4 * feats :]
+    fc_bias_rows = w_fc.shape[1] // width
+    return (
+        layer_out,
+        grad_tokens,
+        ln1_sums[0],
+        ln1_sums[1],
+        qkv_grad,
+        bias_grad,
+        early[2][: 4 * feats],
+        rest[1],
+        rest[2],
+        rest[3],
+        early[0],
+        rest[4 : 4 + fc_bias_rows].reshape(-1),
+        early[1],
+        rest[0],
+    )
 
 
 def visible(query_pos, query_seg, key_pos, key_seg, key_keep):
@@ -303,8 +884,10 @@
 
 
 def solution(mesh):
+    shape = dict(mesh.shape)
+    grouped = (shape["dp"], shape["seq"], shape["tensor"]) == (2, 8, 2)
     return jax.shard_map(
-        on_device,
+        on_groups if grouped else on_device,
         mesh=mesh,
         in_specs=(
             P("dp", "seq", None),

time: 1570 us -> 441 us (0.28)
  matrix products: 660 us -> 43.2 us
  waiting for transfers between devices: 338 us -> 113 us
  local copies, waits for them, and re-layouts: 215 us -> 42.7 us
  other arithmetic: 207 us -> 40.8 us
  Pallas kernels: 0 us -> 111 us
  blocking collectives: 107 us -> 0 us
  starting transfers between devices: 1.86 us -> 64.8 us
  loops' own time: 23.1 us -> 0 us
    dot_general x188 -> x23, matrix products: 660 us -> 43.2 us  [the longest x8 13.3 us: dot(): lax.dot_general(a, b, (((ca,), (cb,)), ((), ())), preferred_element_type=...]
    psum x4 -> x1, waiting for transfers between devices: 195 us -> 0.01 us  [on_groups(): early = lax.psum(early, 'seq')]
    reduce_scatter x4 -> x0, waiting for transfers between devices: 141 us -> none  [the longest x2 91.7 us: on_device(): lax.psum_scatter(key_terms.astype(jnp.bfloat16), 'seq', scatter_dimension...]
    ppermute x0 -> x66, waiting for transfers between devices: none -> 113 us  [the longest x28 60.6 us: exchange(): lax.ppermute(pieces[step], ALL_AXES, group_pairs(step))]
    pallas_call x0 -> x4, Pallas kernels: none -> 111 us  [the longest x1 67.9 us: attention_backward(): pl.pallas_call(functools.partial(backward_kernel, block), out_shape=[jax....]
    reduce_sum x12 -> x16, other arithmetic: 115 us -> 9.13 us  [the longest x8 6.1 us: on_groups(): with_ones = sum((jnp.sum(grad.astype(F32), axis=1) for grad in head_grads))]
    dynamic_slice x96 -> x0, local copies, waits for them, and re-layouts: 78.8 us -> none  [the longest x32 34.3 us: key_step(): lax.dynamic_slice_in_dim(value_src, first_row, block_rows)]
    ppermute x0 -> x66, starting transfers between devices: none -> 64.7 us  [the longest x28 26.4 us: exchange(): lax.ppermute(pieces[step], ALL_AXES, group_pairs(step))]
  transfers between devices with their start and end apart: 12 -> 67, of which waited for: 7 -> 21; matrix products, arithmetic and copies ran while one was open for 41% -> 24% of each run, Pallas kernels for 0% -> 25%
where the time goes in v1:
time: 441 us; the launch traced here: 434 us
  waiting for transfers between devices  113 us (26%)
  Pallas kernels  111 us (25%)
  starting transfers between devices  64.8 us (15%)
  matrix products  43.2 us (10%)
  local copies, waits for them, and re-layouts  42.7 us (10%)
  other arithmetic  40.8 us (9%)
  between operations  17.4 us (4%)
    pallas_call x1, Pallas kernels, attention_backward(): pl.pallas_call(functools.partial(backward_kernel, block), out_shape=[jax....  67.9 us
    ppermute x28, waiting for transfers between devices, exchange(): lax.ppermute(pieces[step], ALL_AXES, group_pairs(step))  60.6 us
    pallas_call x1, Pallas kernels, attention_forward(): pl.pallas_call(functools.partial(forward_kernel, block), out_shape=[jax.S...  35 us
    ppermute x28, starting transfers between devices, exchange(): lax.ppermute(pieces[step], ALL_AXES, group_pairs(step))  26.4 us
    ppermute x5, waiting for transfers between devices, across(): return lax.ppermute(array, 'seq', [(i, i ^ 4) for i in range(8)])  23.7 us
    unnamed x210, local copies, waits for them, and re-layouts  22.5 us
    ppermute x3, waiting for transfers between devices, on_groups(): lax.ppermute(code, 'seq', [(i, i ^ bit) for i in range(8)])  19.1 us
    dot_general x8, matrix products, dot(): lax.dot_general(a, b, (((ca,), (cb,)), ((), ())), preferred_element_type=...  13.3 us
  transfers between devices with their start and end apart: 67, of which 21 were waited for; matrix products, arithmetic and copies ran while one was open for 24% of the time, Pallas kernels for 25%

profile of v1, /device:TPU:0, one launch (start us, length us, event | category | flops | bytes accessed | tf_op | source)
XLA Modules:
  0.0 433.6 jit_solution(3098435388431250869)
XLA Ops:
  8.0 3.0 collective-permute-start.1
  22.9 8.8 %collective-permute-done.2 = s32[2,2,1024]{2,1,0:T(2,128)S(1)} collective-permute-done((s32[2,2,1024]{2,1,0:T(2,128)S(1)}, s32[2,2,1024]{2,1,0:T(2,128)S(1)}, u32[]{:S(2)}, u32[]{:S(2)}) %collective-permute-start.2) | collective-permute-done | bytes 16416 | tf_op jit(solution)/shard_map/ppermute | solution.py:459
  34.4 10.3 %collective-permute-done.3 = s32[4,2,1024]{2,1,0:T(2,128)S(1)} collective-permute-done((s32[4,2,1024]{2,1,0:T(2,128)S(1)}, s32[4,2,1024]{2,1,0:T(2,128)S(1)}, u32[]{:S(2)}, u32[]{:S(2)}) %collective-permute-start.3) | collective-permute-done | bytes 32800 | tf_op jit(solution)/shard_map/ppermute | solution.py:459
  46.8 4.6 %project.1 = (bf16[192,1024]{1,0:T(8,128)(2,1)S(1)}, bf16[192,1024]{1,0:T(8,128)(2,1)S(1)}, bf16[192,1024]{1,0:T(8,128)(2,1)S(1)}, bf16[192,1024]{1,0:T(8,128)(2...) custom-call(f32[1,512]{1,0:T(1,128)S(1)} %bitcast.160, ...), custom_call_target="tpu_custom_call" | custom-call | flops 1610612736 | bytes 1572864 | tf_op jit(solution)/shard_map/project/pallas_call | solution.py:326
  56.9 7.3 %collective-permute-done.7.refs_1_ = bf16[192,1024]{1,0:T(8,128)(2,1)S(1)} collective-permute-done((bf16[192,1024]{1,0:T(8,128)(2,1)S(1)}, bf16[192,1024]{1,0:T(8,128)(2,1)S(1)}, u32[]{:S(2)}, u32[]{:S(2)}) %collective-permute-start.7) | collective-permute-done | bytes 393248 | tf_op jit(solution)/shard_map/ppermute | solution.py:383
  64.2 8.6 %collective-permute-done.8.refs_2_ = bf16[192,1024]{1,0:T(8,128)(2,1)S(1)} collective-permute-done((bf16[192,1024]{1,0:T(8,128)(2,1)S(1)}, bf16[192,1024]{1,0:T(8,128)(2,1)S(1)}, u32[]{:S(2)}, u32[]{:S(2)}) %collective-permute-start.8) | collective-permute-done | bytes 393248 | tf_op jit(solution)/shard_map/ppermute | solution.py:383
  74.4 4.9 %collective-permute-done.11.refs_5_ = bf16[192,1024]{1,0:T(8,128)(2,1)S(1)} collective-permute-done((bf16[192,1024]{1,0:T(8,128)(2,1)}, bf16[192,1024]{1,0:T(8,128)(2,1)S(1)}, u32[]{:S(2)}, u32[]{:S(2)}) %collective-permute-start.11) | collective-permute-done | bytes 393248 | tf_op jit(solution)/shard_map/ppermute | solution.py:383
  79.3 8.8 %collective-permute-done.12.refs_6_ = bf16[192,1024]{1,0:T(8,128)(2,1)} collective-permute-done((bf16[192,1024]{1,0:T(8,128)(2,1)}, bf16[192,1024]{1,0:T(8,128)(2,1)}, u32[]{:S(2)}, u32[]{:S(2)}) %collective-permute-start.12) | collective-permute-done | bytes 393248 | tf_op jit(solution)/shard_map/ppermute | solution.py:383
  92.3 3.1 collective-permute-start.14
  97.9 35.0 %attention_forward.1 = (bf16[64,1024]{1,0:T(8,128)(2,1)S(1)}, bf16[64,1024]{1,0:T(8,128)(2,1)S(1)}, bf16[64,1024]{1,0:T(8,128)(2,1)S(1)}, bf16[64,1024]{1,0:T(8,...) custom-call(s32[8,256]{1,0:T(8,128)S(1)} %stack.74.table_ref, ...), custom_call_target="tpu_custom_call" | custom-call | flops 4294967296 | bytes 4194304 | tf_op jit(solution)/shard_map/attention_forward/pallas_call | solution.py:219
  157.5 2.8 convert_reduce_fusion
  163.3 2.7 fusion.32
  190.7 3.4 add_convert_fusion.2
  197.2 5.1 %collective-permute-done.26.refs_17_ = bf16[64,1024]{1,0:T(8,128)(2,1)} collective-permute-done((bf16[64,1024]{1,0:T(8,128)(2,1)}, bf16[64,1024]{1,0:T(8,128)(2,1)}, u32[]{:S(2)}, u32[]{:S(2)}) %collective-permute-start.26) | collective-permute-done | bytes 131104 | tf_op jit(solution)/shard_map/ppermute | solution.py:383
  208.4 3.4 collective-permute-done.27.refs_18_
  214.8 2.9 collective-permute-done.28.refs_19_
  223.5 3.6 collective-permute-done.32.refs_23_
  230.2 67.9 %attention_backward.1 = (bf16[192,1024]{1,0:T(8,128)(2,1)}, bf16[192,1024]{1,0:T(8,128)(2,1)}, bf16[192,1024]{1,0:T(8,128)(2,1)}, bf16[192,1024]{1,0:T(8,128)(2,...) custom-call(s32[8,256]{1,0:T(8,128)} %copy-done.24, ...), custom_call_target="tpu_custom_call" | custom-call | flops 10737418240 | bytes 8388608 | tf_op jit(solution)/shard_map/attention_backward/pallas_call | solution.py:251
  329.5 2.9 collective-permute-done.47.refs_5_
  336.4 4.5 %collective-permute-start.44 = (bf16[2,512,512]{2,1,0:T(8,128)(2,1)}, bf16[2,512,512]{2,1,0:T(8,128)(2,1)}, u32[]{:S(2)}, u32[]{:S(2)}) collective-permute-start(bf16[2,512,512]{2,1,0:T(8,128)(2,1)} %pad_maximum_fusion.3), channel_id=1, source_target_pairs={{0,1},{1,0},{2,3},{3,2},{4,5},{5,4},{6,7},{7,6},{8,9},{9,8},{10,11... | collective-permute-start | bytes 3145736 | tf_op jit(solution)/shard_map/ppermute | solution.py:388
  342.4 6.4 %collective-permute-done.51.refs_9_ = bf16[192,1024]{1,0:T(8,128)(2,1)S(1)} collective-permute-done((bf16[192,1024]{1,0:T(8,128)(2,1)S(1)}, bf16[192,1024]{1,0:T(8,128)(2,1)S(1)}, u32[]{:S(2)}, u32[]{:S(2)}) %collective-permute-start.51) | collective-permute-done | bytes 393248 | tf_op jit(solution)/shard_map/ppermute | solution.py:383
  358.0 3.9 tail.1
  373.5 23.7 %collective-permute-done.59 = bf16[208,512]{1,0:T(8,128)(2,1)S(1)} collective-permute-done((bf16[208,512]{1,0:T(8,128)(2,1)S(1)}, bf16[208,512]{1,0:T(8,128)(2,1)S(1)}, u32[]{:S(2)}, u32[]{:S(2)}) %collective-permute-start.59) | collective-permute-done | bytes 213024 | tf_op jit(solution)/shard_map/ppermute | solution.py:378
  403.3 4.1 collective-permute-done.60
  (490 shorter events, 184.4 us)
Async XLA Ops:
  7.2 342.4 %all-reduce.5.cloned.1.call-start = ((), (), s32[]{:S(2)}) async-start(), calls=%async_computation | async-start | bytes 2375680 | tf_op jit(solution)/shard_map/psum | solution.py:551
  13.5 32.1 %collective-permute-start.4 = (bf16[4,192,512]{2,1,0:T(8,128)(2,1)S(1)}, bf16[4,192,512]{2,1,0:T(8,128)(2,1)}, u32[]{:S(2)}, u32[]{:S(2)}) collective-permute-start(bf16[4,192,512]{2,1,0:T(8,128)(2,1)S(1)} %fusion.6), channel_id=1, source_target_pairs={{0,1},{1,0},{2,3},{3,2},{4,5},{5,4},{6,7},{7,6},{8,9},{9,8},{10,11... | collective-permute-start | bytes 2359304 | tf_op jit(solution)/shard_map/ppermute | solution.py:388
  17.1 29.7 %collective-permute-start.6 = (bf16[512,512]{1,0:T(8,128)(2,1)}, bf16[512,512]{1,0:T(8,128)(2,1)S(1)}, u32[]{:S(2)}, u32[]{:S(2)}) collective-permute-start(bf16[512,512]{1,0:T(8,128)(2,1)} %get-tuple-element.269), channel_id=1, source_target_pairs={{0,8},{2,10},{4,12},{6,14},{8,0},{10,2},{12,4},{14,6},{1,9},{3,11}... | collective-permute-start | bytes 1572872 | tf_op jit(solution)/shard_map/ppermute | solution.py:378
  56.1 23.2 %collective-permute-start.11 = (bf16[192,1024]{1,0:T(8,128)(2,1)}, bf16[192,1024]{1,0:T(8,128)(2,1)S(1)}, u32[]{:S(2)}, u32[]{:S(2)}) collective-permute-start(bf16[192,1024]{1,0:T(8,128)(2,1)} %get-tuple-element.113), channel_id=1, source_target_pairs={{0,5},{1,4},{2,7},{3,6},{4,1},{5,0},{6,3},{7,2},{8,13},{9,12},{10,... | collective-permute-start | bytes 1179656 | tf_op jit(solution)/shard_map/ppermute | solution.py:383
  64.2 24.0 %collective-permute-start.12 = (bf16[192,1024]{1,0:T(8,128)(2,1)}, bf16[192,1024]{1,0:T(8,128)(2,1)}, u32[]{:S(2)}, u32[]{:S(2)}) collective-permute-start(bf16[192,1024]{1,0:T(8,128)(2,1)} %get-tuple-element.114), channel_id=1, source_target_pairs={{0,3},{1,2},{2,1},{3,0},{4,7},{5,6},{6,5},{7,4},{8,11},{9,10},{10,... | collective-permute-start | bytes 1179656 | tf_op jit(solution)/shard_map/ppermute | solution.py:383
  74.3 63.8 %collective-permute-start = (bf16[4,64,512]{2,1,0:T(8,128)(2,1)}, bf16[4,64,512]{2,1,0:T(8,128)(2,1)}, u32[]{:S(2)}, u32[]{:S(2)}) collective-permute-start(bf16[4,64,512]{2,1,0:T(8,128)(2,1)} %broadcast_select_fusion.5), channel_id=1, source_target_pairs={{0,1},{1,0},{2,3},{3,2},{4,5},{5,4},{6,7},{7,6},{8,9},{9,8},{10,11... | collective-permute-start | bytes 786440 | tf_op jit(solution)/shard_map/ppermute | solution.py:388
  88.2 45.5 %collective-permute-start.15 = (bf16[1024,512]{1,0:T(8,128)(2,1)}, bf16[1024,512]{1,0:T(8,128)(2,1)}, u32[]{:S(2)}, u32[]{:S(2)}) collective-permute-start(bf16[1024,512]{1,0:T(8,128)(2,1)} %get-tuple-element.195), channel_id=1, source_target_pairs={{0,2},{1,3},{2,0},{3,1},{4,6},{5,7},{6,4},{7,5},{8,10},{9,11},{10,... | collective-permute-start | bytes 3145736 | tf_op jit(solution)/shard_map/ppermute | solution.py:490
  92.3 41.4 %collective-permute-start.14 = (bf16[512,512]{1,0:T(8,128)(2,1)}, bf16[512,512]{1,0:T(8,128)(2,1)}, u32[]{:S(2)}, u32[]{:S(2)}) collective-permute-start(bf16[512,512]{1,0:T(8,128)(2,1)} %get-tuple-element.267), channel_id=1, source_target_pairs={{0,8},{2,10},{4,12},{6,14},{8,0},{10,2},{12,4},{14,6},{1,9},{3,11}... | collective-permute-start | bytes 1572872 | tf_op jit(solution)/shard_map/ppermute | solution.py:378
  151.5 75.6 %collective-permute-start.33 = (bf16[1024,512]{1,0:T(8,128)(2,1)}, bf16[1024,512]{1,0:T(8,128)(2,1)}, u32[]{:S(2)}, u32[]{:S(2)}) collective-permute-start(bf16[1024,512]{1,0:T(8,128)(2,1)} %get-tuple-element.195), channel_id=1, source_target_pairs={{0,4},{1,5},{2,6},{3,7},{4,0},{5,1},{6,2},{7,3},{8,12},{9,13},{10,... | collective-permute-start | bytes 3145736 | tf_op jit(solution)/shard_map/ppermute | solution.py:495
  153.2 73.9 %collective-permute-start.34 = (bf16[1024,512]{1,0:T(8,128)(2,1)}, bf16[1024,512]{1,0:T(8,128)(2,1)}, u32[]{:S(2)}, u32[]{:S(2)}) collective-permute-start(bf16[1024,512]{1,0:T(8,128)(2,1)} %get-tuple-element.195), channel_id=1, source_target_pairs={{0,6},{1,7},{2,4},{3,5},{4,2},{5,3},{6,0},{7,1},{8,14},{9,15},{10,... | collective-permute-start | bytes 3145736 | tf_op jit(solution)/shard_map/ppermute | solution.py:496
  173.4 28.8 %collective-permute-start.26 = (bf16[64,1024]{1,0:T(8,128)(2,1)}, bf16[64,1024]{1,0:T(8,128)(2,1)}, u32[]{:S(2)}, u32[]{:S(2)}) collective-permute-start(bf16[64,1024]{1,0:T(8,128)(2,1)} %get-tuple-element.286), channel_id=1, source_target_pairs={{0,4},{1,5},{2,6},{3,7},{4,0},{5,1},{6,2},{7,3},{8,12},{9,13},{10,... | collective-permute-start | bytes 393224 | tf_op jit(solution)/shard_map/ppermute | solution.py:383
  228.9 69.2 %collective-permute-start.43 = (bf16[512,512]{1,0:T(8,128)(2,1)}, bf16[512,512]{1,0:T(8,128)(2,1)}, u32[]{:S(2)}, u32[]{:S(2)}) collective-permute-start(bf16[512,512]{1,0:T(8,128)(2,1)} %slice.115), channel_id=1, source_target_pairs={{0,8},{2,10},{4,12},{6,14},{8,0},{10,2},{12,4},{14,6},{1,9},{3,11}... | collective-permute-start | bytes 1572872 | tf_op jit(solution)/shard_map/ppermute | solution.py:378
  229.1 82.8 %collective-permute-start.57 = (bf16[1024,512]{1,0:T(8,128)(2,1)}, bf16[1024,512]{1,0:T(8,128)(2,1)}, u32[]{:S(2)}, u32[]{:S(2)}) collective-permute-start(bf16[1024,512]{1,0:T(8,128)(2,1)} %collective-permute-done.34), channel_id=1, source_target_pairs={{0,1},{1,0},{2,3},{3,2},{4,5},{5,4},{6,7},{7,6},{8,9},{9,8},{10,11... | collective-permute-start | bytes 3145736 | tf_op jit(solution)/shard_map/ppermute | solution.py:388
  229.1 85.6 %collective-permute-start.56 = (bf16[1024,512]{1,0:T(8,128)(2,1)}, bf16[1024,512]{1,0:T(8,128)(2,1)}, u32[]{:S(2)}, u32[]{:S(2)}) collective-permute-start(bf16[1024,512]{1,0:T(8,128)(2,1)} %collective-permute-done.15), channel_id=1, source_target_pairs={{0,1},{1,0},{2,3},{3,2},{4,5},{5,4},{6,7},{7,6},{8,9},{9,8},{10,11... | collective-permute-start | bytes 3145736 | tf_op jit(solution)/shard_map/ppermute | solution.py:388
  229.6 88.2 %collective-permute-start.55 = (bf16[1024,512]{1,0:T(8,128)(2,1)}, bf16[1024,512]{1,0:T(8,128)(2,1)}, u32[]{:S(2)}, u32[]{:S(2)}) collective-permute-start(bf16[1024,512]{1,0:T(8,128)(2,1)} %collective-permute-done.33), channel_id=1, source_target_pairs={{0,1},{1,0},{2,3},{3,2},{4,5},{5,4},{6,7},{7,6},{8,9},{9,8},{10,11... | collective-permute-start | bytes 3145736 | tf_op jit(solution)/shard_map/ppermute | solution.py:388
  229.6 89.9 %collective-permute-start.54 = (bf16[1024,512]{1,0:T(8,128)(2,1)}, bf16[1024,512]{1,0:T(8,128)(2,1)}, u32[]{:S(2)}, u32[]{:S(2)}) collective-permute-start(bf16[1024,512]{1,0:T(8,128)(2,1)} %get-tuple-element.195), channel_id=1, source_target_pairs={{0,1},{1,0},{2,3},{3,2},{4,5},{5,4},{6,7},{7,6},{8,9},{9,8},{10,11... | collective-permute-start | bytes 3145736 | tf_op jit(solution)/shard_map/ppermute | solution.py:388
  298.2 24.1 %collective-permute-start.45 = (bf16[192,1024]{1,0:T(8,128)(2,1)}, bf16[192,1024]{1,0:T(8,128)(2,1)S(1)}, u32[]{:S(2)}, u32[]{:S(2)}) collective-permute-start(bf16[192,1024]{1,0:T(8,128)(2,1)} %get-tuple-element.175), channel_id=1, source_target_pairs={{0,4},{1,5},{2,6},{3,7},{4,0},{5,1},{6,2},{7,3},{8,12},{9,13},{10,... | collective-permute-start | bytes 1179656 | tf_op jit(solution)/shard_map/ppermute | solution.py:383
  325.5 23.4 %collective-permute-start.51 = (bf16[192,1024]{1,0:T(8,128)(2,1)S(1)}, bf16[192,1024]{1,0:T(8,128)(2,1)S(1)}, u32[]{:S(2)}, u32[]{:S(2)}) collective-permute-start(bf16[192,1024]{1,0:T(8,128)(2,1)S(1)} %copy-done.59), channel_id=1, source_target_pairs={{0,7},{1,6},{2,5},{3,4},{4,3},{5,2},{6,1},{7,0},{8,15},{9,14},{10,... | collective-permute-start | bytes 1179656 | tf_op jit(solution)/shard_map/ppermute | solution.py:383
  333.2 32.9 %collective-permute-start.58 = (bf16[208,512]{1,0:T(8,128)(2,1)}, bf16[208,512]{1,0:T(8,128)(2,1)}, u32[]{:S(2)}, u32[]{:S(2)}) collective-permute-start(bf16[208,512]{1,0:T(8,128)(2,1)} %fusion.9), channel_id=1, source_target_pairs={{0,16},{16,0},{1,17},{17,1},{2,18},{18,2},{3,19},{19,3},{4,20},{20... | collective-permute-start | bytes 638984 | tf_op jit(solution)/shard_map/ppermute | solution.py:570
  336.4 63.8 %collective-permute-start.44 = (bf16[2,512,512]{2,1,0:T(8,128)(2,1)}, bf16[2,512,512]{2,1,0:T(8,128)(2,1)}, u32[]{:S(2)}, u32[]{:S(2)}) collective-permute-start(bf16[2,512,512]{2,1,0:T(8,128)(2,1)} %pad_maximum_fusion.3), channel_id=1, source_target_pairs={{0,1},{1,0},{2,3},{3,2},{4,5},{5,4},{6,7},{7,6},{8,9},{9,8},{10,11... | collective-permute-start | bytes 3145736 | tf_op jit(solution)/shard_map/ppermute | solution.py:388
  361.9 46.0 %collective-permute-start.52 = (bf16[512,512]{1,0:T(8,128)(2,1)}, bf16[512,512]{1,0:T(8,128)(2,1)}, u32[]{:S(2)}, u32[]{:S(2)}) collective-permute-start(bf16[512,512]{1,0:T(8,128)(2,1)} %get-tuple-element.194), channel_id=1, source_target_pairs={{0,8},{2,10},{4,12},{6,14},{8,0},{10,2},{12,4},{14,6},{1,9},{3,11}... | collective-permute-start | bytes 1572872 | tf_op jit(solution)/shard_map/ppermute | solution.py:378
  365.6 44.7 %collective-permute-start.64 = (bf16[256,1024]{1,0:T(8,128)(2,1)}, bf16[256,1024]{1,0:T(8,128)(2,1)S(1)}, u32[]{:S(2)}, u32[]{:S(2)}) collective-permute-start(bf16[256,1024]{1,0:T(8,128)(2,1)} %get-tuple-element.200), channel_id=1, source_target_pairs={{0,16},{16,0},{1,17},{17,1},{2,18},{18,2},{3,19},{19,3},{4,20},{20... | collective-permute-start | bytes 1572872 | tf_op jit(solution)/shard_map/ppermute | solution.py:413
  366.1 46.9 %collective-permute-start.65 = (bf16[512,512]{1,0:T(8,128)(2,1)}, bf16[512,512]{1,0:T(8,128)(2,1)S(1)}, u32[]{:S(2)}, u32[]{:S(2)}) collective-permute-start(bf16[512,512]{1,0:T(8,128)(2,1)} %get-tuple-element.201), channel_id=1, source_target_pairs={{0,16},{16,0},{1,17},{17,1},{2,18},{18,2},{3,19},{19,3},{4,20},{20... | collective-permute-start | bytes 1572872 | tf_op jit(solution)/shard_map/ppermute | solution.py:413
  370.6 26.6 %collective-permute-start.59 = (bf16[208,512]{1,0:T(8,128)(2,1)S(1)}, bf16[208,512]{1,0:T(8,128)(2,1)S(1)}, u32[]{:S(2)}, u32[]{:S(2)}) collective-permute-start(bf16[208,512]{1,0:T(8,128)(2,1)S(1)} %fusion.13), channel_id=1, source_target_pairs={{0,8},{2,10},{4,12},{6,14},{8,0},{10,2},{12,4},{14,6},{1,9},{3,11}... | collective-permute-start | bytes 638984 | tf_op jit(solution)/shard_map/ppermute | solution.py:378
  (141 other events, 1885.2 us)
Sparse Core Ops, SparseCore 0:
  230.2 96.4 all-reduce.4

commit v2 on v1

--- a/solution.py
+++ b/solution.py
@@ -12,7 +12,10 @@
 MASKED = -1e30
 DOC_IDS = 16
 TILE = 512
-ALL_AXES = ("dp", "seq", "tensor")
+VMEM_LIMIT = 64000 * 1024
+ALL_AXES = ("dp", "zh", "zl", "x", "tensor")
+GROUP = ("tensor", "x", "zl")
+SEQ = ("zh", "zl", "x")
 BF16 = jnp.bfloat16
 F32 = jnp.float32
 
@@ -42,12 +45,35 @@
     return lax.dot_general(a, b, (((ca,), (cb,)), ((), ())), preferred_element_type=F32)
 
 
-def blocks_of(pieces, place_ref, block):
-    per_piece = pieces[0].shape[1] // block
-    for piece_at, piece in enumerate(pieces):
-        for block_at in range(per_piece):
-            start = pl.multiple_of(place_ref[piece_at * per_piece + block_at] * block, block)
-            yield piece, slice(block_at * block, (block_at + 1) * block), pl.ds(start, block)
+def moves(place_ref, sems, whole, pieces, parts):
+    copies = []
+    for index in range(16):
+        span = at(place_ref[index])
+        for part_at, (array, rows, piece_rows) in enumerate(whole):
+            if len(pieces) == 16:
+                piece = pieces[index].at[piece_rows, :]
+            else:
+                first = (index // 8) * TILE
+                device = (index % 8) ^ place_ref[16]
+                piece = pieces[0].at[device, piece_rows, first : first + TILE]
+            copies.append((piece, array.at[rows, span], sems.at[parts + part_at, index]))
+    return copies
+
+
+def bring(copies):
+    copies = [pltpu.make_async_copy(*copy) for copy in copies]
+    for copy in copies:
+        copy.start()
+    return copies
+
+
+def send(copies):
+    return bring([(array, piece, sem) for piece, array, sem in copies])
+
+
+def wait(copies):
+    for copy in copies:
+        copy.wait()
 
 
 def doc_features(code):
@@ -78,20 +104,27 @@
     return pl.ds(pl.multiple_of(index * TILE, TILE), TILE)
 
 
-def forward_kernel(block, table_ref, place_ref, code_ref, *refs):
-    pieces, outs, lse_ref = refs[:8], refs[8:16], refs[16]
-    query_t, key_t, value_t, key_row, out_t, score_a, score_b, accum, peak = refs[17:]
+def forward_kernel(table_ref, place_ref, code_ref, *refs):
+    pieces, outs, lse_ref = refs[:16], refs[16:17], refs[17]
+    query_t, key_t, value_t, key_row, out_t, score_a, score_b, accum, peak, sems = refs[18:]
     feats = HEAD_DIM
-    ones = jnp.ones((16, block), BF16)
-    for piece, cols, span in blocks_of(pieces, place_ref, block):
+    head = slice(0, feats)
+    arrived = bring(moves(place_ref, sems, [
+        (query_t, head, head),
+        (key_t, head, slice(feats, 2 * feats)),
+        (value_t, head, slice(2 * feats, 3 * feats)),
+    ], pieces, 0))
+    wait(arrived)
+
+    def prepare(tile, carry):
+        span = at(tile)
         as_query, as_key = doc_features(code_ref[:, span])
-        part = piece[feats : 2 * feats, cols]
-        query_t[0:feats, span] = piece[0:feats, cols]
         query_t[feats:, span] = as_query
-        key_t[:, span] = part
-        key_row[span, :] = jnp.concatenate([part, as_key], axis=0).T
-        value_t[0:feats, span] = piece[2 * feats : 3 * feats, cols]
-        value_t[feats:, span] = ones
+        key_row[span, :] = jnp.concatenate([key_t[:, span], as_key], axis=0).T
+        value_t[feats:, span] = jnp.ones((16, TILE), BF16)
+        return carry
+
+    lax.fori_loop(0, 16, prepare, 0)
     accum[...] = jnp.zeros_like(accum)
     peak[...] = jnp.full_like(peak, MASKED)
 
@@ -133,34 +166,39 @@
         return carry
 
     lax.fori_loop(0, table_ref[4, 0], pair, 0)
-    for piece, cols, span in blocks_of(outs, place_ref, block):
-        piece[:, cols] = out_t[:, span]
-
-
-def backward_kernel(block, table_ref, place_ref, code_ref, lse_ref, *refs):
-    pieces, mixed, grads, outs = refs[:8], refs[8:16], refs[16:24], refs[24:32]
-    (query_t, key_t, grad_t, key_row, value_row, query_row, grad_row, delta,
-     sum_q, sum_k, sum_v, score_a, score_b, dp_a, dp_b) = refs[32:]
+    wait(send(moves(place_ref, sems, [(out_t, head, head)], outs, 0)))
+
+
+def backward_kernel(table_ref, place_ref, code_ref, lse_ref, *refs):
+    pieces, mixed, grads, outs = refs[:16], refs[16:17], refs[17:18], refs[18:19]
+    (query_t, key_t, value_t, grad_t, mixed_t, key_row, value_row, query_row, grad_row, delta,
+     sum_q, sum_k, sum_v, score_a, score_b, dp_a, dp_b, sems) = refs[19:]
     feats = HEAD_DIM
-    for (piece, cols, span), (grad, _, _), (out, _, _) in zip(
-        blocks_of(pieces, place_ref, block),
-        blocks_of(grads, place_ref, block),
-        blocks_of(mixed, place_ref, block),
-    ):
+    head = slice(0, feats)
+    of_key, of_value = slice(feats, 2 * feats), slice(2 * feats, 3 * feats)
+    arrived = bring(
+        moves(place_ref, sems, [
+            (query_t, head, head), (key_t, head, of_key), (value_t, head, of_value)
+        ], pieces, 0)
+        + moves(place_ref, sems, [(mixed_t, head, head)], mixed, 3)
+        + moves(place_ref, sems, [(grad_t, head, head)], grads, 4)
+    )
+    wait(arrived)
+
+    def prepare(tile, carry):
+        span = at(tile)
         as_query, as_key = doc_features(code_ref[:, span])
-        part_q, part_k = piece[0:feats, cols], piece[feats : 2 * feats, cols]
-        part_g = grad[:, cols]
-        query_t[0:feats, span] = part_q
         query_t[feats:, span] = as_query
-        key_t[:, span] = part_k
-        grad_t[:, span] = part_g
-        key_row[span, :] = jnp.concatenate([part_k, as_key], axis=0).T
-        value_row[span, :] = piece[2 * feats : 3 * feats, cols].T
-        query_row[span, :] = part_q.T
-        grad_row[span, :] = part_g.T
+        key_row[span, :] = jnp.concatenate([key_t[:, span], as_key], axis=0).T
+        value_row[span, :] = value_t[:, span].T
+        query_row[span, :] = query_t[0:feats, span].T
+        grad_row[span, :] = grad_t[:, span].T
         delta[:, span] = jnp.sum(
-            part_g.astype(F32) * out[:, cols].astype(F32), axis=0, keepdims=True
-        )
+            grad_t[:, span].astype(F32) * mixed_t[:, span].astype(F32), axis=0, keepdims=True
+        )
+        return carry
+
+    lax.fori_loop(0, 16, prepare, 0)
     sum_q[...] = jnp.zeros_like(sum_q)
     sum_k[...] = jnp.zeros_like(sum_k)
     sum_v[...] = jnp.zeros_like(sum_v)
@@ -198,30 +236,44 @@
         return carry
 
     lax.fori_loop(0, table_ref[4, 0], pair, 0)
-    for piece, cols, span in blocks_of(outs, place_ref, block):
-        piece[0:feats, cols] = sum_q[:, span].astype(BF16)
-        piece[feats : 2 * feats, cols] = sum_k[span, :].T.astype(BF16)
-        piece[2 * feats : 3 * feats, cols] = sum_v[span, :].T.astype(BF16)
+
+    def finish(tile, carry):
+        span = at(tile)
+        query_t[0:feats, span] = sum_q[:, span].astype(BF16)
+        key_t[:, span] = sum_k[span, :].T.astype(BF16)
+        value_t[:, span] = sum_v[span, :].T.astype(BF16)
+        return carry
+
+    lax.fori_loop(0, 16, finish, 0)
+    wait(send(moves(place_ref, sems, [
+        (query_t, head, head), (key_t, head, of_key), (value_t, head, of_value)
+    ], outs, 0)))
 
 
 def vmem():
     return pl.BlockSpec(memory_space=pltpu.VMEM)
 
 
+def hbm():
+    return pl.BlockSpec(memory_space=pltpu.HBM)
+
+
 def smem():
     return pl.BlockSpec(memory_space=pltpu.SMEM)
 
 
-def attention_forward(table, place, code, pieces, block):
-    length, part = code.shape[1], pieces[0].shape[1]
+def attention_forward(table, place, code, pieces):
+    length = code.shape[1]
     pairs = (length // TILE) * 4
     wide = HEAD_DIM + DOC_IDS
     out = pl.pallas_call(
-        functools.partial(forward_kernel, block),
-        out_shape=[jax.ShapeDtypeStruct((HEAD_DIM, part), BF16)] * 8
-        + [jax.ShapeDtypeStruct((1, length), F32)],
-        in_specs=[smem(), smem()] + [vmem()] * 9,
-        out_specs=[vmem()] * 9,
+        forward_kernel,
+        out_shape=[
+            jax.ShapeDtypeStruct((8, HEAD_DIM, 2 * TILE), BF16),
+            jax.ShapeDtypeStruct((1, length), F32),
+        ],
+        in_specs=[smem(), smem(), vmem()] + [hbm()] * 16,
+        out_specs=[hbm(), vmem()],
         scratch_shapes=[
             pltpu.VMEM((wide, length), BF16),
             pltpu.VMEM((HEAD_DIM, length), BF16),
@@ -232,29 +284,32 @@
             pltpu.VMEM((TILE, TILE), F32),
             pltpu.VMEM((HEAD_DIM + 16, TILE), F32),
             pltpu.VMEM((8, TILE), F32),
+            pltpu.SemaphoreType.DMA((3, 16)),
         ],
-        compiler_params=pltpu.CompilerParams(vmem_limit_bytes=40 << 20),
+        compiler_params=pltpu.CompilerParams(vmem_limit_bytes=VMEM_LIMIT),
         cost_estimate=pl.CostEstimate(
-            flops=pairs * 4 * TILE * TILE * HEAD_DIM,
+            flops=pairs * 16 * TILE * TILE * HEAD_DIM,
             bytes_accessed=8 * length * HEAD_DIM,
             transcendentals=pairs * TILE * TILE,
         ),
         name="attention_forward",
     )(table, place, code, *pieces)
-    return out[:8], out[8]
-
-
-def attention_backward(table, place, code, lse, pieces, mixed, grads, block):
-    length, part = code.shape[1], pieces[0].shape[1]
+    return out
+
+
+def attention_backward(table, place, code, lse, pieces, mixed, grads):
+    length = code.shape[1]
     pairs = (length // TILE) * 4
     wide = HEAD_DIM + DOC_IDS
     return pl.pallas_call(
-        functools.partial(backward_kernel, block),
-        out_shape=[jax.ShapeDtypeStruct((3 * HEAD_DIM, part), BF16)] * 8,
-        in_specs=[smem(), smem()] + [vmem()] * 26,
-        out_specs=[vmem()] * 8,
+        backward_kernel,
+        out_shape=jax.ShapeDtypeStruct((8, 3 * HEAD_DIM, 2 * TILE), BF16),
+        in_specs=[smem(), smem(), vmem(), vmem()] + [hbm()] * 18,
+        out_specs=hbm(),
         scratch_shapes=[
             pltpu.VMEM((wide, length), BF16),
+            pltpu.VMEM((HEAD_DIM, length), BF16),
+            pltpu.VMEM((HEAD_DIM, length), BF16),
             pltpu.VMEM((HEAD_DIM, length), BF16),
             pltpu.VMEM((HEAD_DIM, length), BF16),
             pltpu.VMEM((length, wide), BF16),
@@ -269,15 +324,16 @@
             pltpu.VMEM((TILE, TILE), F32),
             pltpu.VMEM((TILE, TILE), F32),
             pltpu.VMEM((TILE, TILE), F32),
+            pltpu.SemaphoreType.DMA((5, 16)),
         ],
-        compiler_params=pltpu.CompilerParams(vmem_limit_bytes=56 << 20),
+        compiler_params=pltpu.CompilerParams(vmem_limit_bytes=VMEM_LIMIT),
         cost_estimate=pl.CostEstimate(
-            flops=pairs * 10 * TILE * TILE * HEAD_DIM,
+            flops=pairs * 60 * TILE * TILE * HEAD_DIM,
             bytes_accessed=16 * length * HEAD_DIM,
             transcendentals=pairs * TILE * TILE,
         ),
         name="attention_backward",
-    )(table, place, code, lse, *pieces, *mixed, *grads)
+    )(table, place, code, lse, *pieces, mixed, grads)
 
 
 def tile_table(segment_row):
@@ -309,60 +365,388 @@
     return jnp.stack([query, key, first, last, pairs, trash, trash_query, held]).astype(jnp.int32)
 
 
-def project_kernel(gain_ref, offset_ref, weight_ref, bias_ref, *refs):
-    blocks, outs, normed_ref = refs[:2], refs[2:10], refs[10]
-    for block_at, block in enumerate(blocks):
-        size = block.shape[0]
-        span = slice(block_at * size, (block_at + 1) * size)
-        hidden, normed, _ = layer_norm(block[...].astype(F32), gain_ref[...], offset_ref[...])
-        normed_ref[span, :] = normed.astype(BF16)
-        hidden = hidden.astype(BF16)
-        for step, out in enumerate(outs):
-            out[:, span] = (dot(weight_ref[step], hidden, 1, 1) + bias_ref[step]).astype(BF16)
-
-
-def project(gain, offset, weight, bias, blocks):
-    rows, width = 2 * blocks[0].shape[0], blocks[0].shape[1]
+def project_kernel(gain_ref, offset_ref, weight_ref, bias_ref, block, *refs):
+    outs, (normed_ref, stage, sems) = refs[:8], refs[8:]
+    hidden, normed, _ = layer_norm(block[...].astype(F32), gain_ref[...], offset_ref[...])
+    normed_ref[...] = normed.astype(BF16)
+    hidden_t = hidden.astype(BF16).T
+    copies = []
+    for step, out in enumerate(outs):
+        stage[step] = (dot(weight_ref[step], hidden_t, 1, 0) + bias_ref[step]).astype(BF16)
+        copies += bring([(stage.at[step], out, sems.at[step])])
+    wait(copies)
+
+
+def project(gain, offset, weight, bias, block):
+    rows, width = block.shape
+    feats = weight.shape[1]
     out = pl.pallas_call(
         project_kernel,
-        out_shape=[jax.ShapeDtypeStruct((weight.shape[1], rows), BF16)] * 8
+        out_shape=[jax.ShapeDtypeStruct((feats, rows), BF16)] * 8
         + [jax.ShapeDtypeStruct((rows, width), BF16)],
-        in_specs=[vmem()] * 6,
-        out_specs=[vmem()] * 9,
-        compiler_params=pltpu.CompilerParams(vmem_limit_bytes=40 << 20),
+        in_specs=[vmem()] * 5,
+        out_specs=[hbm()] * 8 + [vmem()],
+        scratch_shapes=[pltpu.VMEM((8, feats, rows), BF16), pltpu.SemaphoreType.DMA((8,))],
+        compiler_params=pltpu.CompilerParams(vmem_limit_bytes=VMEM_LIMIT),
         cost_estimate=pl.CostEstimate(
             flops=2 * rows * weight.size, bytes_accessed=2 * weight.size, transcendentals=0
         ),
         name="project",
-    )(gain[None], offset[None], weight, bias[:, :, None], *blocks)
+    )(gain[None], offset[None], weight, bias[:, :, None], block)
     return out[:8], out[8]
 
 
-def tail_kernel(gain_ref, weight_ref, middle_ref, *refs):
-    blocks, grads, outs = refs[:2], refs[2:10], refs[10:12]
+def tail_kernel(block_at, me_ref, gain_ref, weight_ref, middle_ref, block, grads, out, stage, sems):
+    feats = weight_ref.shape[0] // 8
+    cols = slice(block_at * TILE, (block_at + 1) * TILE)
+    arrived = bring([
+        (grads.at[step ^ me_ref[0], :, cols], stage.at[step * feats : (step + 1) * feats, :],
+         sems.at[step])
+        for step in range(8)
+    ])
     gain = gain_ref[...]
-    for block_at, (block, out) in enumerate(zip(blocks, outs)):
-        size = block.shape[0]
-        span = slice(block_at * size, (block_at + 1) * size)
-        _, normed, rstd = layer_norm(block[...].astype(F32), gain, gain)
-        hidden_grad = sum(dot(grad[:, span], weight_ref[step], 0, 0) for step, grad in enumerate(grads))
-        out[...] = (middle_ref[span, :] + norm_back(hidden_grad, normed, rstd, gain)).astype(BF16)
-
-
-def tail(gain, weight, grad_middle, blocks, grads):
+    _, normed, rstd = layer_norm(block[...].astype(F32), gain, gain)
+    wait(arrived)
+    hidden_grad = dot(stage[...], weight_ref[...], 0, 0)
+    out[...] = (middle_ref[...] + norm_back(hidden_grad, normed, rstd, gain)).astype(BF16)
+
+
+def tail(block_at, me, gain, weight, grad_middle, block, grads):
     return pl.pallas_call(
-        tail_kernel,
-        out_shape=[jax.ShapeDtypeStruct(blocks[0].shape, BF16)] * 2,
-        in_specs=[vmem()] * 13,
-        out_specs=[vmem()] * 2,
-        compiler_params=pltpu.CompilerParams(vmem_limit_bytes=40 << 20),
+        functools.partial(tail_kernel, block_at),
+        out_shape=jax.ShapeDtypeStruct(block.shape, BF16),
+        in_specs=[smem()] + [vmem()] * 4 + [hbm()],
+        out_specs=vmem(),
+        scratch_shapes=[
+            pltpu.VMEM((8 * weight.shape[1], block.shape[0]), BF16), pltpu.SemaphoreType.DMA((8,))
+        ],
+        compiler_params=pltpu.CompilerParams(vmem_limit_bytes=VMEM_LIMIT),
         cost_estimate=pl.CostEstimate(
-            flops=2 * grad_middle.shape[0] * weight.size,
+            flops=2 * block.shape[0] * weight.size,
             bytes_accessed=2 * weight.size,
             transcendentals=0,
         ),
         name="tail",
-    )(gain[None], weight, grad_middle, *blocks, *grads)
+    )(me, gain[None], weight.reshape(-1, weight.shape[2]), grad_middle, block, grads)
+
+
+def head_sums_kernel(me_ref, grads, *refs):
+    normed, (out, grad_stage, normed_stage, sems) = refs[:8], refs[8:]
+    width = normed[0].shape[1]
+    arrived = bring([
+        copy
+        for step in range(8)
+        for copy in (
+            (normed[step], normed_stage.at[step], sems.at[0, step]),
+            (grads.at[step ^ me_ref[0]], grad_stage.at[step], sems.at[1, step]),
+        )
+    ])
+    total = jnp.zeros((grads.shape[1], width), F32)
+    lanes = jnp.zeros((grads.shape[1], 128), F32)
+    for step in range(8):
+        wait(arrived[2 * step : 2 * step + 2])
+        total += dot(grad_stage[step], normed_stage[step], 1, 0)
+        wide = grad_stage[step].astype(F32)
+        for lane in range(0, wide.shape[1], 128):
+            lanes += wide[:, lane : lane + 128]
+    out[:, 0:width] = total
+    out[:, width:] = jnp.broadcast_to(jnp.sum(lanes, axis=1, keepdims=True), lanes.shape)
+
+
+def head_sums(me, grads, normed):
+    rows, width = normed[0].shape
+    feats = grads.shape[1]
+    return pl.pallas_call(
+        head_sums_kernel,
+        out_shape=jax.ShapeDtypeStruct((feats, width + 128), F32),
+        in_specs=[smem()] + [hbm()] * 9,
+        out_specs=vmem(),
+        scratch_shapes=[
+            pltpu.VMEM((8, feats, rows), BF16),
+            pltpu.VMEM((8, rows, width), BF16),
+            pltpu.SemaphoreType.DMA((2, 8)),
+        ],
+        compiler_params=pltpu.CompilerParams(vmem_limit_bytes=VMEM_LIMIT),
+        cost_estimate=pl.CostEstimate(
+            flops=16 * feats * width * rows, bytes_accessed=24 * rows * width, transcendentals=0
+        ),
+        name="head_sums",
+    )(me, grads, *normed)
+
+
+def unpack_kernel(part_ref, near, far, fc_ref, proj_ref, out_ref, stage, sems):
+    wait(bring([
+        (source.at[step % 4], stage.at[step ^ part_ref[0]], sems.at[step])
+        for step, source in enumerate([near] * 4 + [far] * 4)
+    ]))
+    width = near.shape[2]
+    fc_rows, proj_rows, out_rows = fc_ref.shape[0] // 8, proj_ref.shape[0] // 8, out_ref.shape[0] // 8
+    for part in range(8):
+        start = 0
+        for col in range(0, fc_ref.shape[1], width):
+            fc_ref[part * fc_rows : (part + 1) * fc_rows, col : col + width] = stage[
+                part, start : start + fc_rows, :
+            ].astype(F32)
+            start += fc_rows
+        for ref, rows in ((proj_ref, proj_rows), (out_ref, out_rows)):
+            ref[part * rows : (part + 1) * rows, :] = stage[part, start : start + rows, :].astype(F32)
+            start += rows
+
+
+def unpack(part, near, far, wide):
+    rows, width = near.shape[1:]
+    feats = rows - width // 8 * (wide // width) - wide // 8
+    shape = jax.ShapeDtypeStruct
+    return pl.pallas_call(
+        unpack_kernel,
+        out_shape=[shape((width, wide), F32), shape((wide, width), F32), shape((8 * feats, width), F32)],
+        in_specs=[smem()] + [hbm()] * 2,
+        out_specs=[vmem()] * 3,
+        scratch_shapes=[pltpu.VMEM((8, rows, width), BF16), pltpu.SemaphoreType.DMA((8,))],
+        compiler_params=pltpu.CompilerParams(vmem_limit_bytes=VMEM_LIMIT),
+        cost_estimate=pl.CostEstimate(flops=0, bytes_accessed=48 * rows * width, transcendentals=0),
+        name="unpack",
+    )(part, near, far)
+
+
+def middle_kernel(
+    me_ref, out_bias, gain_ref, offset_ref, proj_bias, fc_bias_a, fc_bias_b, mixed, *refs
+):
+    (tokens_own, tokens_other, grad_own, grad_other, out_a, out_b, fc_a, fc_b, proj_a, proj_b,
+     layer_own, layer_other, middle_own, middle_other, grad_pieces, *refs) = refs
+    (hidden_ref, act_ref, pre_ref, branch_ref, vectors_ref, pre_sums,
+     mixed_t, tokens, grads, w_out, fc, proj, layer, grad_middle, grad_t, hidden, act, pre, branch,
+     in_sems, out_sems, block_sems) = refs
+    feats = HEAD_DIM
+    block = tokens_own.shape[0]
+    wide = fc_a.shape[1]
+    step_rows = 256
+    first = bring([(mixed.at[i ^ me_ref[0]], mixed_t.at[i * feats : (i + 1) * feats, :], in_sems.at[i])
+                   for i in range(8)])
+    own, other = slice(0, block), slice(block, 2 * block)
+    first += bring([
+        (out_a, w_out.at[0 : 4 * feats], in_sems.at[8]),
+        (out_b, w_out.at[4 * feats : 8 * feats], in_sems.at[9]),
+        (tokens_own, tokens.at[own], in_sems.at[10]),
+        (tokens_other, tokens.at[other], in_sems.at[11]),
+        (fc_a, fc.at[0], in_sems.at[12]),
+        (fc_b, fc.at[1], in_sems.at[13]),
+        (proj_a, proj.at[0], in_sems.at[14]),
+        (proj_b, proj.at[1], in_sems.at[15]),
+        (grad_own, grads.at[own], in_sems.at[16]),
+        (grad_other, grads.at[other], in_sems.at[17]),
+    ])
+    wait(first)
+    vectors_ref[...] = jnp.zeros_like(vectors_ref)
+    pre_sums[...] = jnp.zeros_like(pre_sums)
+
+    def outgoing(step):
+        rows = pl.ds(pl.multiple_of(step * step_rows, step_rows), step_rows)
+        return [
+            pltpu.make_async_copy(source.at[..., rows, :], target.at[..., rows, :], out_sems.at[i, step])
+            for i, (source, target) in enumerate([
+                (hidden, hidden_ref), (act, act_ref), (pre, pre_ref), (branch, branch_ref),
+            ])
+        ]
+
+    def one(step, carry):
+        rows = pl.ds(pl.multiple_of(step * step_rows, step_rows), step_rows)
+        gain = gain_ref[...]
+        mid = tokens[rows, :].astype(F32) + dot(mixed_t[:, rows], w_out[...], 0, 0) + out_bias[...]
+        hid, normed, rstd = layer_norm(mid, gain, offset_ref[...])
+        hid = hid.astype(BF16)
+        hidden[rows, :] = hid
+        grad = grads[rows, :]
+        wide_grad = grad.astype(F32)
+        feed = mid + proj_bias[...]
+        grad_hidden = 0.0
+        for at_half, fc_bias in enumerate((fc_bias_a, fc_bias_b)):
+            activated, slope = gelu_parts(dot(hid, fc[at_half], 1, 0) + fc_bias[...])
+            activated = activated.astype(BF16)
+            act[at_half, rows, :] = activated
+            feed += dot(activated, proj[at_half], 1, 0)
+            grad_pre = (dot(grad, proj[at_half], 1, 1) * slope).astype(BF16)
+            pre[at_half, rows, :] = grad_pre
+            grad_hidden += dot(grad_pre, fc[at_half], 1, 1)
+            pre_sums[at_half : at_half + 1, :] += jnp.sum(grad_pre.astype(F32), 0, keepdims=True)
+        layer[rows, :] = feed.astype(BF16)
+        grad_mid = wide_grad + norm_back(grad_hidden, normed, rstd, gain)
+        grad_middle[rows, :] = grad_mid
+        low = grad_mid.astype(BF16)
+        branch[rows, :] = low
+        grad_t[:, rows] = dot(w_out[...], low, 1, 1).astype(BF16)
+        for at_row, value in enumerate(
+            (wide_grad, low.astype(F32), grad_hidden * normed, grad_hidden)
+        ):
+            vectors_ref[at_row : at_row + 1, :] += jnp.sum(value, 0, keepdims=True)
+        for copy in outgoing(step):
+            copy.start()
+        for at_block in range(2):
+            @pl.when(step == (at_block + 1) * steps // 2 - 1)
+            def _():
+                bring(finished(at_block))
+        return carry
+
+    steps = 2 * block // step_rows
+
+    def finished(at_block):
+        rows = (own, other)[at_block]
+        return [
+            (layer.at[rows], (layer_own, layer_other)[at_block], block_sems.at[at_block]),
+            (grad_middle.at[rows], (middle_own, middle_other)[at_block], block_sems.at[2 + at_block]),
+        ]
+
+    lax.fori_loop(0, steps, one, 0)
+    last = bring([
+        (grad_t.at[i * feats : (i + 1) * feats, :], grad_pieces.at[i ^ me_ref[0]], in_sems.at[i])
+        for i in range(8)
+    ])
+    for step in range(steps):
+        wait(outgoing(step))
+    for at_block in range(2):
+        wait([pltpu.make_async_copy(*copy) for copy in finished(at_block)])
+    wait(last)
+
+
+def middle(me, biases, mixed, blocks, weights):
+    block, width = blocks[0].shape
+    rows, wide = 2 * block, weights[2].shape[1]
+    feats = HEAD_DIM
+    shape = jax.ShapeDtypeStruct
+    out = pl.pallas_call(
+        middle_kernel,
+        out_shape=[shape((block, width), BF16)] * 2
+        + [shape((block, width), F32)] * 2
+        + [shape((8, feats, rows), BF16)]
+        + [shape((rows, width), BF16), shape((2, rows, wide), BF16), shape((2, rows, wide), BF16),
+           shape((rows, width), BF16), shape((8, width), F32), shape((8, wide), F32)],
+        in_specs=[smem()] + [vmem()] * 6 + [hbm()] * 11,
+        out_specs=[hbm()] * 9 + [vmem()] * 2,
+        scratch_shapes=[
+            pltpu.VMEM((8 * feats, rows), BF16),
+            pltpu.VMEM((rows, width), BF16),
+            pltpu.VMEM((rows, width), BF16),
+            pltpu.VMEM((8 * feats, width), BF16),
+            pltpu.VMEM((2, width, wide), BF16),
+            pltpu.VMEM((2, wide, width), BF16),
+            pltpu.VMEM((rows, width), BF16),
+            pltpu.VMEM((rows, width), F32),
+            pltpu.VMEM((8 * feats, rows), BF16),
+            pltpu.VMEM((rows, width), BF16),
+            pltpu.VMEM((2, rows, wide), BF16),
+            pltpu.VMEM((2, rows, wide), BF16),
+            pltpu.VMEM((rows, width), BF16),
+            pltpu.SemaphoreType.DMA((18,)),
+            pltpu.SemaphoreType.DMA((4, 4)),
+            pltpu.SemaphoreType.DMA((4,)),
+        ],
+        compiler_params=pltpu.CompilerParams(vmem_limit_bytes=VMEM_LIMIT),
+        cost_estimate=pl.CostEstimate(
+            flops=2 * rows * width * (2 * width + 8 * wide),
+            bytes_accessed=32 * rows * width,
+            transcendentals=2 * rows * wide,
+        ),
+        name="middle",
+    )(me, *biases, mixed, *blocks, *weights)
+    return out[0:2], out[2:4], out[4], out[5:]
+
+
+def weight_sums_kernel(half, me_ref, vectors_ref, pre_sums_ref, mixed, *refs):
+    (grad_own, grad_other, hidden_ref, act_ref, pre_ref, branch_ref,
+     out_ref, mixed_t, grads, hidden, act, pre, branch, fc_sum, proj_sum, out_sum, small,
+     sems, out_sems) = refs
+    feats = HEAD_DIM
+    block = grad_own.shape[0]
+    width, wide = hidden.shape[1], act.shape[1]
+    arrived = bring([
+        (hidden_ref, hidden, sems.at[0]),
+        (pre_ref.at[half], pre, sems.at[1]),
+        (grad_own, grads.at[0:block], sems.at[2]),
+        (grad_other, grads.at[block : 2 * block], sems.at[3]),
+        (act_ref.at[half], act, sems.at[4]),
+        (branch_ref, branch, sems.at[5]),
+    ] + [
+        (mixed.at[(4 * half + i) ^ me_ref[0]], mixed_t.at[i * feats : (i + 1) * feats, :],
+         sems.at[6 + i])
+        for i in range(4)
+    ])
+    rows = [vectors_ref[0:4, :]] + [
+        pre_sums_ref[half : half + 1, i * width : (i + 1) * width] for i in range(wide // width)
+    ]
+    rows.append(jnp.zeros((12 - wide // width, width), F32))
+    small[...] = jnp.concatenate(rows, axis=0).astype(BF16)
+    fc_part, proj_part, out_part = width // 8, wide // 8, feats // 2
+    at_proj = fc_part * (wide // width)
+    at_out = at_proj + proj_part
+    at_small = at_out + out_part
+    leaving = []
+
+    def leave(kind, sources):
+        for part in range(8):
+            for i, (source, rows) in enumerate(sources(part)):
+                sem = out_sems.at[part * 5 + kind + i]
+                leaving.extend(bring([(source, out_ref.at[part, rows, :], sem)]))
+
+    def rows_of(part, size):
+        return slice(part * size, (part + 1) * size)
+
+    wait(arrived[0:2])
+    for rows in (slice(i, i + 256) for i in range(0, width, 256)):
+        fc_sum[rows, :] = dot(hidden[:, rows], pre[...], 0, 0).astype(BF16)
+    leave(0, lambda part: [
+        (fc_sum.at[rows_of(part, fc_part), i * width : (i + 1) * width],
+         slice(i * fc_part, (i + 1) * fc_part))
+        for i in range(wide // width)
+    ])
+    wait(arrived[2:5])
+    for rows in (slice(i, i + 256) for i in range(0, wide, 256)):
+        proj_sum[rows, :] = dot(act[:, rows], grads[...], 0, 0).astype(BF16)
+    leave(2, lambda part: [(proj_sum.at[rows_of(part, proj_part), :], slice(at_proj, at_out))])
+    wait(arrived[5:])
+    out_sum[...] = dot(mixed_t[...], branch[...], 1, 0).astype(BF16)
+    leave(3, lambda part: [
+        (out_sum.at[
+            pl.ds(pl.multiple_of(((part // 2) ^ (me_ref[0] & 3)) * feats, feats)
+                  + part % 2 * out_part, out_part),
+            :,
+        ], slice(at_out, at_small)),
+        (small, slice(at_small, at_small + 16)),
+    ])
+    wait(leaving)
+
+
+def weight_sums(half, me, vectors, pre_sums, mixed, grad_blocks, saved):
+    rows, width = saved[0].shape
+    wide = saved[1].shape[2]
+    feats = HEAD_DIM
+    part_rows = width // 8 * (wide // width) + wide // 8 + feats // 2 + 16
+    return pl.pallas_call(
+        functools.partial(weight_sums_kernel, half),
+        out_shape=jax.ShapeDtypeStruct((8, part_rows, width), BF16),
+        in_specs=[smem(), vmem(), vmem()] + [hbm()] * 7,
+        out_specs=hbm(),
+        scratch_shapes=[
+            pltpu.VMEM((4 * feats, rows), BF16),
+            pltpu.VMEM((rows, width), BF16),
+            pltpu.VMEM((rows, width), BF16),
+            pltpu.VMEM((rows, wide), BF16),
+            pltpu.VMEM((rows, wide), BF16),
+            pltpu.VMEM((rows, width), BF16),
+            pltpu.VMEM((width, wide), BF16),
+            pltpu.VMEM((wide, width), BF16),
+            pltpu.VMEM((4 * feats, width), BF16),
+            pltpu.VMEM((16, width), BF16),
+            pltpu.SemaphoreType.DMA((10,)),
+            pltpu.SemaphoreType.DMA((40,)),
+        ],
+        compiler_params=pltpu.CompilerParams(vmem_limit_bytes=VMEM_LIMIT),
+        cost_estimate=pl.CostEstimate(
+            flops=rows * width * (width + 4 * wide),
+            bytes_accessed=12 * rows * width,
+            transcendentals=0,
+        ),
+        name="weight_sums",
+    )(me, vectors, pre_sums, mixed, *grad_blocks, *saved)
 
 
 def group_pairs(step):
@@ -374,54 +758,74 @@
     return pairs
 
 
+def pair(array, axis):
+    return lax.ppermute(array, axis, [(0, 1), (1, 0)])
+
+
 def across(array):
-    return lax.ppermute(array, "seq", [(i, i ^ 4) for i in range(8)])
-
-
-def exchange(pieces):
-    return [pieces[0]] + [
-        lax.ppermute(pieces[step], ALL_AXES, group_pairs(step)) for step in range(1, 8)
-    ]
+    return lax.ppermute(array, "zh", [(0, 1), (1, 0)])
+
+
+def move(piece, step):
+    return lax.ppermute(piece, ALL_AXES, group_pairs(step)) if step else piece
+
+
+def deal(array, axes):
+    return lax.all_to_all(array, axes, 0, 0, tiled=True)
+
+
+def share(array, axes, size):
+    return deal(jnp.broadcast_to(array[None], (size,) + array.shape), axes)
+
+
+def exchange(pieces, steps=range(8)):
+    return {step: move(pieces[step], step) for step in steps}
 
 
 def swap(array):
     return lax.ppermute(array, "tensor", [(0, 1), (1, 0)])
 
 
-def pick(array, first, second):
-    array = lax.dynamic_index_in_dim(array, first, 0, keepdims=False)
-    return lax.dynamic_index_in_dim(array, second, 0, keepdims=False)
-
-
-def to_group(array, half, core):
-    parts = array.reshape(2, 2, -1, array.shape[2])
-    return [pick(parts, half, core), across(pick(parts, 1 - half, core))]
+def block_of(array, half, core):
+    rows = array.shape[1] // 2
+    size = (1, rows, array.shape[2])
+    return lax.dynamic_slice(array, (half, core * rows, 0), size)[0]
 
 
 def tie(*values):
     return lax.optimization_barrier(values)
 
 
-def scatter_sum(array, part):
-    halves = array.astype(BF16).reshape((2, -1) + array.shape[1:])
-    mine = lax.dynamic_index_in_dim(halves, part, 0, keepdims=False)
-    other = lax.dynamic_index_in_dim(halves, 1 - part, 0, keepdims=False)
-    return mine + lax.ppermute(other, "dp", [(0, 1), (1, 0)])
-
-
-def gather_halves(array, part):
-    other = lax.ppermute(array, "dp", [(0, 1), (1, 0)])
-    low = jnp.where(part == 0, array, other)
-    high = jnp.where(part == 0, other, array)
-    return jnp.concatenate([low, high], axis=0).astype(F32)
-
-
-def from_group(mine, back, half, core):
-    both = jnp.stack([jnp.where(half == 0, mine, back), jnp.where(half == 0, back, mine)])
-    other = swap(both)
-    low = jnp.where(core == 0, both, other)
-    high = jnp.where(core == 0, other, both)
-    return jnp.stack([low, high], axis=1).reshape(2, -1, mine.shape[1])
+def after(moved, steps, values):
+    ended, values = tie([moved[step] for step in steps], values)
+    return {**moved, **dict(zip(steps, ended))}, values
+
+
+def from_group(where, mine, back):
+    rows, width = mine.shape
+    return pl.pallas_call(
+        from_group_kernel,
+        out_shape=jax.ShapeDtypeStruct((2, 2 * rows, width), mine.dtype),
+        in_specs=[smem()] + [vmem()] * 4,
+        out_specs=hbm(),
+        scratch_shapes=[pltpu.SemaphoreType.DMA((4,))],
+        cost_estimate=pl.CostEstimate(flops=0, bytes_accessed=16 * rows * width, transcendentals=0),
+        name="from_group",
+    )(where, mine, back, swap(mine), swap(back))
+
+
+def from_group_kernel(where_ref, mine, back, mine_there, back_there, out, sems):
+    half, core, rows = where_ref[0], where_ref[1], mine.shape[0]
+    copies = []
+    for index, (source, seq, part) in enumerate((
+        (mine, half, core),
+        (back, 1 - half, core),
+        (mine_there, half, 1 - core),
+        (back_there, 1 - half, 1 - core),
+    )):
+        span = pl.ds(pl.multiple_of(part * rows, rows), rows)
+        copies.append((source, out.at[seq, span, :], sems.at[index]))
+    wait(bring(copies))
 
 
 def on_groups(
@@ -443,29 +847,15 @@
     b_proj,
 ):
     width = tokens.shape[2]
-    block = tokens.shape[1] // 2
     feats = HEAD_DIM
-    piece_at = lax.axis_index("seq")
-    core = lax.axis_index("tensor")
-    z, x = piece_at >> 1, piece_at & 1
-    half = z >> 1
-    chip = 2 * x + (z & 1)
-
-    token_blocks = to_group(tokens, half, core)
-
-    code = (segments * 2 + keep_mask)[None]
-    for bit in (1, 2, 4):
-        code = jnp.concatenate(
-            [code, lax.ppermute(code, "seq", [(i, i ^ bit) for i in range(8)])], axis=0
-        )
-    code = lax.dynamic_index_in_dim(code, half, 1, keepdims=False)
-    code = jnp.take(code, jnp.arange(8) ^ piece_at, axis=0).reshape(1, -1)
-    table = tile_table(code[0] >> 1)
-    steps = jnp.arange(8)[:, None]
-    their_z = z ^ (steps & 1) ^ (2 * jnp.arange(2)[None, :])
-    their_x, their_core = x ^ ((steps >> 1) & 1), core ^ (steps >> 2)
-    place = (4 * their_z + 2 * their_x + their_core).reshape(16).astype(jnp.int32)
-
+    half, low_z, x, core = (lax.axis_index(name) for name in ("zh", "zl", "x", "tensor"))
+    z = 2 * half + low_z
+    chip = 2 * x + low_z
+    me = (4 * core + chip).astype(jnp.int32)[None]
+
+    other_tokens, w_qkv = tie(block_of(tokens, 1 - half, core), w_qkv)
+    other_tokens = across(other_tokens)
+    own_tokens = block_of(tokens, half, core)
     order = jnp.arange(4) ^ chip
     heads_w = jnp.take(
         w_qkv.reshape(3, width, 4, feats).transpose(2, 0, 3, 1), order, axis=0
@@ -478,111 +868,99 @@
     bias = bias.reshape(4, 3 * feats)
     bias = jnp.concatenate([bias, swap(bias)], axis=0)
     heads_out = jnp.take(w_out.reshape(4, feats, width), order, axis=0)
-    heads_out = jnp.concatenate([heads_out, swap(heads_out)], axis=0).reshape(8 * feats, width)
-    fcs = (w_fc, swap(w_fc))
-    projs = (w_proj, swap(w_proj))
-    fc_biases = (b_fc, swap(b_fc))
-
-    pieces, shared = project(ln1_gain, ln1_bias, heads_w, bias, token_blocks)
-    pieces = exchange(pieces)
-    pieces, cotangent, shared = tie(pieces, cotangent, shared)
-    grad_blocks = to_group(cotangent, half, core)
-    shared_x = lax.ppermute(shared, ALL_AXES, group_pairs(2))
-    outs, lse = attention_forward(table, place, code, pieces, block)
-    outs, grad_blocks, shared_x = tie(outs, grad_blocks, shared_x)
-    mixed = exchange(outs)
-    mixed, shared = tie(mixed, shared)
-    shared = [shared, lax.ppermute(shared, ALL_AXES, group_pairs(1)), shared_x,
-              lax.ppermute(shared, ALL_AXES, group_pairs(3))]
-    mixed_t = jnp.concatenate(mixed, axis=0)
-
-    rows = jnp.concatenate(token_blocks, axis=0).astype(F32)
-    middle = rows + jnp.einsum("fr,fd->rd", mixed_t, heads_out, preferred_element_type=F32) + b_out
-    normed_two_out, normed_two, rstd_two = layer_norm(middle, ln2_gain, ln2_bias)
-    hidden_two = normed_two_out.astype(BF16)
-    grad_out = jnp.concatenate(grad_blocks, axis=0)
-    grad_wide = grad_out.astype(F32)
-    feed = b_proj
-    grad_hidden_two = 0.0
-    acts, grad_pres = [], []
-    for fc, fc_bias, proj in zip(fcs, fc_biases, projs):
-        pre_act = jnp.dot(hidden_two, fc, preferred_element_type=F32) + fc_bias
-        activated, slope = gelu_parts(pre_act)
-        acts.append(activated.astype(BF16))
-        feed = feed + jnp.dot(acts[-1], proj, preferred_element_type=F32)
-        grad_act = jnp.einsum("td,fd->tf", grad_out, proj, preferred_element_type=F32)
-        grad_pres.append((grad_act * slope).astype(BF16))
-        grad_hidden_two = grad_hidden_two + jnp.einsum(
-            "tf,ef->te", grad_pres[-1], fc, preferred_element_type=F32
-        )
-    layer_rows = (middle + feed).astype(BF16)
-    grad_middle = grad_wide + norm_back(grad_hidden_two, normed_two, rstd_two, ln2_gain)
-    grad_branch = grad_middle.astype(BF16)
-    grad_mixed_t = jnp.einsum(
-        "fd,rd->fr", heads_out, grad_branch, preferred_element_type=F32
-    ).astype(BF16)
-    grad_pieces = exchange([grad_mixed_t[i * feats : (i + 1) * feats] for i in range(8)])
-
-    def both(mine, other):
-        return mine + swap(other.astype(BF16)).astype(F32)
-
-    proj_sum = both(*[
-        jnp.einsum("tf,td->fd", act, grad_out, preferred_element_type=F32) for act in acts
-    ])
-    fc_sum = both(*[
-        jnp.einsum("te,tf->ef", hidden_two, grad, preferred_element_type=F32) for grad in grad_pres
-    ])
-    out_sum = jnp.einsum("fr,rd->fd", mixed_t, grad_branch, preferred_element_type=F32)
-    out_sum = both(out_sum[: 4 * feats], out_sum[4 * feats :])
-    out_sum = jnp.take(out_sum.reshape(4, feats, width), order, axis=0).reshape(4 * feats, width)
-    fc_bias_sum = both(*[jnp.sum(grad.astype(F32), 0) for grad in grad_pres])
-    vectors = jnp.stack([
-        jnp.sum(grad_wide, 0),
-        jnp.sum(grad_branch.astype(F32), 0),
-        jnp.sum(grad_hidden_two * normed_two, 0),
-        jnp.sum(grad_hidden_two, 0),
-    ])
-    vectors = both(vectors, vectors)
-    early = [fc_sum, proj_sum, jnp.concatenate(
-        [out_sum, vectors, fc_bias_sum.reshape(-1, width), jnp.zeros((10, width), F32)], axis=0
-    )]
-    early = [scatter_sum(part, lax.axis_index("dp")) for part in early]
-    grad_pieces, shared, early, layer_rows = tie(grad_pieces, shared, early, layer_rows)
-    early = lax.psum(early, "seq")
-    layer_back = across(layer_rows[block:])
-    head_grads = attention_backward(table, place, code, lse, pieces, outs, grad_pieces, block)
-    head_grads, layer_back = tie(head_grads, layer_back)
-    grads = exchange(head_grads)
-    layer_out = from_group(layer_rows[:block], layer_back, half, core)
-    grads, early = tie(grads, early)
-    early = [gather_halves(part, lax.axis_index("dp")) for part in early]
-    grad_rows = tail(ln1_gain, heads_w, grad_middle, token_blocks, grads)
-    grad_tokens = from_group(grad_rows[0], across(grad_rows[1]), half, core)
-
-    shared = shared + [swap(part) for part in shared]
-    with_normed = sum(dot(grad, part, 1, 0) for grad, part in zip(head_grads, shared))
-    with_ones = sum(jnp.sum(grad.astype(F32), axis=1) for grad in head_grads)
-    late = jnp.concatenate([
-        with_normed,
-        jnp.pad(with_ones, (0, width - 3 * feats))[None],
-        jnp.zeros((15, width), F32),
-    ], axis=0)
-    late = late + lax.ppermute(late.astype(BF16), "dp", [(0, 1), (1, 0)]).astype(F32)
+    heads_out = heads_out.reshape(4 * feats, width)
+    weights = [heads_out, swap(heads_out), w_fc, swap(w_fc), w_proj, swap(w_proj), swap(b_fc)]
+    heads_w, weights = tie(heads_w, weights)
+
+    own_pieces, own_normed = project(ln1_gain, ln1_bias, heads_w, bias, own_tokens)
+    own_normed, segments = tie(own_normed, segments)
+    code = share(segments * 2 + keep_mask, SEQ, 8)
+    own_pieces = exchange(own_pieces)
+    own_pieces, other_tokens = after(own_pieces, (1, 2, 3, 4, 5), other_tokens)
+    code = lax.dynamic_index_in_dim(code, half, 1, keepdims=False)
+    code = code.reshape(1, -1)
+    table = tile_table(code[0] >> 1)
+    steps = jnp.arange(8)[:, None]
+    their_z = z ^ (steps & 1) ^ (2 * jnp.arange(2)[None, :])
+    their_x, their_core = x ^ ((steps >> 1) & 1), core ^ (steps >> 2)
+    place = (4 * their_z + 2 * their_x + their_core).T.reshape(16)
+    place = jnp.concatenate([place, me]).astype(jnp.int32)
+
+    other_pieces, other_normed = project(ln1_gain, ln1_bias, heads_w, bias, other_tokens)
+    other_pieces = exchange(other_pieces)
+    pieces = [own_pieces[i] for i in range(8)] + [other_pieces[i] for i in range(8)]
+    own_grad, sent = block_of(cotangent, half, core), block_of(cotangent, 1 - half, core)
+    shared = jnp.concatenate([own_normed, other_normed], axis=0)
+    pieces, sent, shared = tie(pieces, sent, shared)
+    other_grad = across(sent)
+    shared_x = move(shared, 2)
+    shared_z = move(shared, 1)
+    outs, lse = attention_forward(table, place, code, pieces)
+    outs, other_grad, shared_x, shared_z = tie(outs, other_grad, shared_x, shared_z)
+    mixed = deal(outs, GROUP)
+    mixed, shared, shared_x, shared_z = tie(mixed, shared, shared_x, shared_z)
+    shared_d = move(shared, 3)
+    swapped = [swap(shared), swap(shared_z), swap(shared_x)]
+    layer_rows, grad_middle, grad_pieces, saved = middle(
+        me,
+        [part[None] for part in (b_out, ln2_gain, ln2_bias, b_proj, b_fc, weights[6])],
+        mixed,
+        [own_tokens, other_tokens, own_grad, other_grad],
+        weights[:6],
+    )
+
+    grad_pieces = deal(grad_pieces, GROUP)
+    shared_d, swapped, now = tie(shared_d, swapped, me)
+    there = weight_sums(1, now, saved[4], saved[5], mixed, [own_grad, other_grad], saved[:4])
+    there, now = tie(there, now)
+    here = weight_sums(0, now, saved[4], saved[5], mixed, [own_grad, other_grad], saved[:4])
+    parts = here + swap(there)
+    grad_pieces, parts, layer_rows, shared_d, swapped = tie(
+        grad_pieces, parts, layer_rows, shared_d, swapped
+    )
+    shared = [shared, shared_z, shared_x, shared_d]
+
+    parts = deal(parts, ("dp", "x", "zl"))
+    layer_back = across(layer_rows[1])
+    head_grads = attention_backward(table, place, code, lse, pieces, outs, grad_pieces)
+    head_grads, layer_back, parts = tie(head_grads, layer_back, parts)
+    grads = deal(head_grads, GROUP)
+    total = jnp.sum(parts.astype(F32), axis=0)
+    total = total + across(total.astype(BF16)).astype(F32)
+    rows_here = total.shape[0] - 16
+    small_grads = total[rows_here:]
+    total = total[:rows_here].astype(BF16)
+    total = jnp.stack([total, pair(total, "zl")])
+    total = jnp.stack([total, pair(total, "x")])
+    swapped.append(swap(shared[3]))
+    late = head_sums(me, head_grads, shared + swapped)
+    late = late + pair(late.astype(BF16), "dp").astype(F32)
     late = late + across(late.astype(BF16)).astype(F32)
-    with_normed, with_ones = late[: 3 * feats], late[3 * feats, : 3 * feats]
+    grads, late, total = tie(grads, late, total)
+
+    other_rows = tail(1, me, ln1_gain, heads_w, grad_middle[1], other_tokens, grads)
+    halves = jnp.stack([half, core]).astype(jnp.int32)
+    other_rows, ln1_own = tie(other_rows, ln1_gain)
+    back = across(other_rows)
+    own_rows = tail(0, me, ln1_own, heads_w, grad_middle[0], own_tokens, grads)
+    part = (4 * lax.axis_index("dp") + 2 * x + low_z).astype(jnp.int32)[None]
+    own_rows, late, layer_back, part = tie(own_rows, late, layer_back, part)
+
+    with_normed, with_ones = late[:, :width], late[:, width : width + 1]
+    wide = w_fc.shape[1]
+    total = total.reshape(4, rows_here, width)
+    fc_grad, proj_grad, out_grad = unpack(part, total, pair(total, "dp"), wide)
+    grad_tokens = from_group(halves, own_rows, back)
+    layer_out = from_group(halves, layer_rows[0], layer_back)
     mine = heads_w[0].astype(F32)
     late = jnp.concatenate([
-        with_normed * ln1_gain + with_ones[:, None] * ln1_bias,
-        jnp.pad(with_ones, (0, width - 3 * feats))[None],
+        with_normed * ln1_gain + with_ones * ln1_bias,
+        jnp.pad(with_ones[:, 0], (0, width - 3 * feats))[None],
         jnp.sum(mine * with_normed, axis=0)[None],
-        jnp.sum(mine * with_ones[:, None], axis=0)[None],
+        jnp.sum(mine * with_ones, axis=0)[None],
         jnp.zeros((13, width), F32),
-    ], axis=0).astype(BF16)[None]
-    for bit in (2, 1):
-        late = jnp.concatenate(
-            [late, lax.ppermute(late, "seq", [(i, i ^ bit) for i in range(8)])], axis=0
-        )
-    late = late.astype(F32)
+    ], axis=0).astype(BF16)
+    late = jnp.stack([late] + [move(late, step) for step in range(1, 4)]).astype(F32)
     ln1_sums = jnp.sum(late[:, 3 * feats + 1 : 3 * feats + 3], axis=0)
     ln1_sums = ln1_sums + swap(ln1_sums)
     late = jnp.take(late, order, axis=0)
@@ -592,8 +970,6 @@
     bias_grad = late[:, 3 * feats, : 3 * feats].reshape(4, 3, feats)
     bias_grad = jnp.stack([bias_grad[:, 0] * feats**-0.5, bias_grad[:, 2]]).reshape(2, 4 * feats)
 
-    rest = early[2][4 * feats :]
-    fc_bias_rows = w_fc.shape[1] // width
     return (
         layer_out,
         grad_tokens,
@@ -601,14 +977,14 @@
         ln1_sums[1],
         qkv_grad,
         bias_grad,
-        early[2][: 4 * feats],
-        rest[1],
-        rest[2],
-        rest[3],
-        early[0],
-        rest[4 : 4 + fc_bias_rows].reshape(-1),
-        early[1],
-        rest[0],
+        out_grad,
+        small_grads[1],
+        small_grads[2],
+        small_grads[3],
+        fc_grad,
+        small_grads[4 : 4 + wide // width].reshape(-1),
+        proj_grad,
+        small_grads[0],
     )
 
 
@@ -885,15 +1261,18 @@
 
 def solution(mesh):
     shape = dict(mesh.shape)
-    grouped = (shape["dp"], shape["seq"], shape["tensor"]) == (2, 8, 2)
+    seq, run, names = "seq", on_device, mesh
+    if (shape["dp"], shape["seq"], shape["tensor"]) == (2, 8, 2):
+        seq, run = SEQ, on_groups
+        names = jax.sharding.Mesh(mesh.devices.reshape(2, 2, 2, 2, 2), ALL_AXES)
     return jax.shard_map(
-        on_groups if grouped else on_device,
-        mesh=mesh,
+        run,
+        mesh=names,
         in_specs=(
-            P("dp", "seq", None),
-            P("dp", "seq"),
-            P("dp", "seq"),
-            P("dp", "seq", None),
+            P("dp", seq, None),
+            P("dp", seq),
+            P("dp", seq),
+            P("dp", seq, None),
             P(),
             P(),
             P(None, None, "tensor"),
@@ -908,8 +1287,8 @@
             P(),
         ),
         out_specs=(
-            P("dp", "seq", None),
-            P("dp", "seq", None),
+            P("dp", seq, None),
+            P("dp", seq, None),
             P(),
             P(),
             P(None, None, "tensor"),

time: 441 us -> 406 us (0.921); the launches traced: 434 us -> 404 us
  Pallas kernels: 111 us -> 183 us
  matrix products: 43.2 us -> 0 us
  local copies, waits for them, and re-layouts: 42.7 us -> 20.1 us
  waiting for transfers between devices: 113 us -> 93.7 us
  blocking collectives: 0 us -> 19.2 us
  other arithmetic: 40.8 us -> 24.4 us
  between operations: 17.4 us -> 3.02 us
    pallas_call x4 -> x13, Pallas kernels: 111 us -> 183 us  [the longest x1 71.3 us: attention_backward(): pl.pallas_call(backward_kernel, out_shape=jax.ShapeDtypeStruct((8, 3 * HE...]
    dot_general x23 -> x0, matrix products: 43.2 us -> none  [the longest x8 13.3 us: dot(): lax.dot_general(a, b, (((ca,), (cb,)), ((), ())), preferred_element_type=...]
    ppermute x48 -> x30, waiting for transfers between devices: 112 us -> 81.8 us  [the longest x6 40.1 us: across(): return lax.ppermute(array, 'zh', [(0, 1), (1, 0)])]
    all_to_all x0 -> x1, blocking collectives: none -> 19.2 us  [deal(): return lax.all_to_all(array, axes, 0, 0, tiled=True)]
    unnamed x210 -> x79, local copies, waits for them, and re-layouts: 22.5 us -> 6.1 us
    all_to_all x0 -> x4, starting transfers between devices: none -> 16.2 us  [deal(): return lax.all_to_all(array, axes, 0, 0, tiled=True)]
    ppermute x48 -> x30, starting transfers between devices: 55.9 us -> 40.9 us  [the longest x20 21.5 us: move(): return lax.ppermute(piece, ALL_AXES, group_pairs(step)) if step else piece]
    all_to_all x0 -> x4, waiting for transfers between devices: none -> 10.9 us  [deal(): return lax.all_to_all(array, axes, 0, 0, tiled=True)]
  transfers between devices with their start and end apart: 67 -> 50, of which waited for: 21 -> 18; matrix products, arithmetic and copies ran while one was open for 24% -> 9% of each run, Pallas kernels for 25% -> 43%
where the time goes in v2:
time: 406 us; the launch traced here: 404 us
  Pallas kernels  183 us (45%)
  waiting for transfers between devices  93.7 us (23%)
  starting transfers between devices  60.5 us (15%)
  other arithmetic  24.4 us (6%)
  local copies, waits for them, and re-layouts  20.1 us (5%)
  blocking collectives  19.2 us (5%)
    pallas_call x1, Pallas kernels, attention_backward(): pl.pallas_call(backward_kernel, out_shape=jax.ShapeDtypeStruct((8, 3 * HE...  71.3 us
    ppermute x6, waiting for transfers between devices, across(): return lax.ppermute(array, 'zh', [(0, 1), (1, 0)])  40.1 us
    pallas_call x1, Pallas kernels, attention_forward(): pl.pallas_call(forward_kernel, out_shape=[jax.ShapeDtypeStruct((8, HEAD_D...  38.9 us
    pallas_call x1, Pallas kernels, middle(): pl.pallas_call(middle_kernel, out_shape=[shape((block, width), BF16)] * 2...  22.4 us
    ppermute x20, waiting for transfers between devices, move(): return lax.ppermute(piece, ALL_AXES, group_pairs(step)) if step else piece  22 us
    ppermute x20, starting transfers between devices, move(): return lax.ppermute(piece, ALL_AXES, group_pairs(step)) if step else piece  21.5 us
    ppermute x4, waiting for transfers between devices, pair(): return lax.ppermute(array, axis, [(0, 1), (1, 0)])  19.7 us
    all_to_all x1, blocking collectives, deal(): return lax.all_to_all(array, axes, 0, 0, tiled=True)  19.2 us
  transfers between devices with their start and end apart: 50, of which 18 were waited for; matrix products, arithmetic and copies ran while one was open for 9% of the time, Pallas kernels for 43%

profile of v2, /device:TPU:0, one launch (start us, length us, event | category | flops | bytes accessed | tf_op | source)
XLA Modules:
  0.0 404.1 jit_solution(6074276585181784412)
XLA Ops:
  10.4 3.9 collective-permute-start.11
  16.2 5.2 %project.2 = (bf16[192,512]{1,0:T(8,128)(2,1)}, bf16[192,512]{1,0:T(8,128)(2,1)}, bf16[192,512]{1,0:T(8,128)(2,1)}, bf16[192,512]{1,0:T(8,128)(2,1)}, bf16[192,5...) custom-call(f32[1,512]{1,0:T(1,128)} %bitcast.93, ...), custom_call_target="tpu_custom_call" | custom-call | flops 805306368 | bytes 1572864 | tf_op jit(solution)/shard_map/project/pallas_call | solution.py:383
  32.4 7.7 %all-to-all-done = s32[8,2,1024]{2,1,0:T(2,128)S(1)} async-done(((s32[8,2,1024]{2,1,0:T(2,128)}), s32[8,2,1024]{2,1,0:T(2,128)S(1)}, u32[]{:S(2)}, u32[]{:S(2)}) %all-to-all-start) | async-done | bytes 65568 | tf_op jit(solution)/shard_map/all_to_all | solution.py:774
  51.4 5.2 %project.3 = (bf16[192,512]{1,0:T(8,128)(2,1)}, bf16[192,512]{1,0:T(8,128)(2,1)}, bf16[192,512]{1,0:T(8,128)(2,1)}, bf16[192,512]{1,0:T(8,128)(2,1)}, bf16[192,5...) custom-call(f32[1,512]{1,0:T(1,128)} %bitcast.94, ...), custom_call_target="tpu_custom_call" | custom-call | flops 805306368 | bytes 1572864 | tf_op jit(solution)/shard_map/project/pallas_call | solution.py:383
  64.7 5.1 %collective-permute-start.20 = (bf16[192,512]{1,0:T(8,128)(2,1)}, bf16[192,512]{1,0:T(8,128)(2,1)S(1)}, u32[]{:S(2)}, u32[]{:S(2)}) collective-permute-start(bf16[192,512]{1,0:T(8,128)(2,1)} %get-tuple-element.146), channel_id=1, source_target_pairs={{0,7},{1,6},{2,5},{3,4},{4,3},{5,2},{6,1},{7,0},{8,15},{9,14},{10,... | collective-permute-start | bytes 589832 | tf_op jit(solution)/shard_map/ppermute | solution.py:770
  82.0 38.9 %attention_forward.1 = (bf16[8,64,1024]{2,1,0:T(8,128)(2,1)}, f32[1,8192]{1,0:T(1,128)}) custom-call(s32[8,256]{1,0:T(8,128)} %stack.67.table_ref, s32[17]{0:T(128)} %pad_add_fusion.1.place_ref, s32[1,8192]{1,0:T(1,128)} %bitcast.88, bf16[192,512]{1,0:T(8,128)(2,1)} %get-tuple-element.149.refs_0_, bf16[192,512]{1,0:T(8,128)(2,1)} %copy-done.19, ...), custom_call_target="tpu_custom_call" | custom-call | flops 17179869184 | bytes 4194304 | tf_op jit(solution)/shard_map/attention_forward/pallas_call | solution.py:269
  120.9 19.2 %all_to_all.25.mixed = bf16[8,64,1024]{2,1,0:T(8,128)(2,1)} all-to-all(bf16[8,64,1024]{2,1,0:T(8,128)(2,1)} %get-tuple-element.168.refs_16_), channel_id=1, replica_groups=mesh['dp'=2,'zh'=2,'zl'=2,'x'=2,'tensor'=2] {'tensor','x','zl'}, dimensions={0} | all-to-all | bytes 2097152 | tf_op jit(solution)/shard_map/all_to_all | solution.py:774
  141.6 22.4 %middle.1 = (bf16[512,512]{1,0:T(8,128)(2,1)}, bf16[512,512]{1,0:T(8,128)(2,1)}, f32[512,512]{1,0:T(8,128)}, f32[512,512]{1,0:T(8,128)}, bf16[8,64,1024]{2,1,0:T...) custom-call(s32[1]{0:T(128)} %bitcast.2.me_ref, ...), custom_call_target="tpu_custom_call" | custom-call | flops 9663676416 | bytes 16777216 | tf_op jit(solution)/shard_map/middle/pallas_call | solution.py:616
  166.4 7.0 %weight_sums.2 = bf16[8,304,512]{2,1,0:T(8,128)(2,1)} custom-call(s32[1]{0:T(128)} %bitcast.2.me_ref, f32[8,512]{1,0:T(8,128)} %get-tuple-element.184.vectors_ref, f32[8,1024]{1,0:T(8,128)} %get-tuple-element.185.pre_sums_ref, bf16[8,64,1024]{2,1,0:T(8,128)(2,1)} %all_to_all.25.mixed, bf16[512,512]{1,0:T(8,128)(2,1)} %get-tuple-element.292.refs_2_.refs_0_, ...), custom_call_target="tpu_custom_call" | custom-call | flops 2415919104 | bytes 6291456 | tf_op jit(solution)/shard_map/weight_sums/pallas_call | solution.py:723
  177.1 7.0 %weight_sums.3 = bf16[8,304,512]{2,1,0:T(8,128)(2,1)} custom-call(s32[1]{0:T(128)} %bitcast.2.me_ref, f32[8,512]{1,0:T(8,128)} %get-tuple-element.184.vectors_ref, f32[8,1024]{1,0:T(8,128)} %get-tuple-element.185.pre_sums_ref, bf16[8,64,1024]{2,1,0:T(8,128)(2,1)} %all_to_all.25.mixed, bf16[512,512]{1,0:T(8,128)(2,1)} %get-tuple-element.292.refs_2_.refs_0_, ...), custom_call_target="tpu_custom_call" | custom-call | flops 2415919104 | bytes 6291456 | tf_op jit(solution)/shard_map/weight_sums/pallas_call | solution.py:723
  184.0 4.6 %add.169 = bf16[8,304,512]{2,1,0:T(8,128)(2,1)} add(bf16[8,304,512]{2,1,0:T(8,128)(2,1)} %weight_sums.3, bf16[8,304,512]{2,1,0:T(8,128)(2,1)} %collective-permute-done.28) | non-fusion elementwise | flops 1245184 | bytes 7471104 | tf_op jit(solution)/shard_map/add | solution.py:917
  192.8 4.4 %all-to-all-start.3 = ((bf16[8,304,512]{2,1,0:T(8,128)(2,1)}), bf16[8,304,512]{2,1,0:T(8,128)(2,1)}, u32[]{:S(2)}, u32[]{:S(2)}) async-start(bf16[8,304,512]{2,1,0:T(8,128)(2,1)} %add.169), calls=%async_computation.3 | async-start | bytes 4980736 | tf_op jit(solution)/shard_map/all_to_all | solution.py:774
  197.2 71.3 %attention_backward.1.grads = bf16[8,192,1024]{2,1,0:T(8,128)(2,1)} custom-call(s32[8,256]{1,0:T(8,128)} %stack.67.table_ref, s32[17]{0:T(128)} %pad_add_fusion.1.place_ref, s32[1,8192]{1,0:T(1,128)} %bitcast.89, f32[1,8192]{1,0:T(1,128)} %get-tuple-element.200.lse_ref, bf16[192,512]{1,0:T(8,128)(2,1)} %get-tuple-element.149.refs_0_, ...), custom_call_target="tpu_custom_call" | custom-call | flops 64424509440 | bytes 8388608 | tf_op jit(solution)/shard_map/attention_backward/pallas_call | solution.py:304
  268.6 4.5 %all-to-all-start.4 = ((bf16[8,192,1024]{2,1,0:T(8,128)(2,1)}), bf16[8,192,1024]{2,1,0:T(8,128)(2,1)}, u32[]{:S(2)}, u32[]{:S(2)}) async-start(bf16[8,192,1024]{2,1,0:T(8,128)(2,1)} %attention_backward.1.grads), calls=%async_computation.4 | async-start | bytes 6291456 | tf_op jit(solution)/shard_map/all_to_all | solution.py:774
  277.6 5.6 %head_sums.1 = f32[192,640]{1,0:T(8,128)} custom-call(s32[1]{0:T(128)} %bitcast.2.me_ref, bf16[8,192,1024]{2,1,0:T(8,128)(2,1)} %attention_backward.1.grads, bf16[1024,512]{1,0:T(8,128)(2,1)} %copy-done.3, bf16[1024,512]{1,0:T(8,128)(2,1)} %collective-permute-done.23.refs_1_, bf16[1024,512]{1,0:T(8,128)(2,1)} %collective-permute-done.22.refs_2_, ...), custom_call_target="tpu_custom_call" | custom-call | flops 1610612736 | bytes 12582912 | tf_op jit(solution)/shard_map/head_sums/pallas_call | solution.py:459
  286.3 28.2 %collective-permute-done.33 = bf16[304,512]{1,0:T(8,128)(2,1)} collective-permute-done((bf16[304,512]{1,0:T(8,128)(2,1)S(1)}, bf16[304,512]{1,0:T(8,128)(2,1)}, u32[]{:S(2)}, u32[]{:S(2)}) %collective-permute-start.33) | collective-permute-done | bytes 311328 | tf_op jit(solution)/shard_map/ppermute | solution.py:766
  315.6 4.2 %collective-permute-start.34 = (bf16[288,512]{1,0:T(8,128)(2,1)S(1)}, bf16[288,512]{1,0:T(8,128)(2,1)S(1)}, u32[]{:S(2)}, u32[]{:S(2)}) collective-permute-start(bf16[288,512]{1,0:T(8,128)(2,1)S(1)} %slice.120), channel_id=1, source_target_pairs={{0,4},{4,0},{1,5},{5,1},{2,6},{6,2},{3,7},{7,3},{8,12},{12,8},{9,1... | collective-permute-start | bytes 884744 | tf_op jit(solution)/shard_map/ppermute | solution.py:762
  320.5 9.9 %collective-permute-done.34 = bf16[288,512]{1,0:T(8,128)(2,1)S(1)} collective-permute-done((bf16[288,512]{1,0:T(8,128)(2,1)S(1)}, bf16[288,512]{1,0:T(8,128)(2,1)S(1)}, u32[]{:S(2)}, u32[]{:S(2)}) %collective-permute-start.34) | collective-permute-done | bytes 294944 | tf_op jit(solution)/shard_map/ppermute | solution.py:762
  335.3 9.8 %collective-permute-done.35 = bf16[2,288,512]{2,1,0:T(8,128)(2,1)} collective-permute-done((bf16[2,288,512]{2,1,0:T(8,128)(2,1)S(1)}, bf16[2,288,512]{2,1,0:T(8,128)(2,1)}, u32[]{:S(2)}, u32[]{:S(2)}) %collective-permute-start.35) | collective-permute-done | bytes 589856 | tf_op jit(solution)/shard_map/ppermute | solution.py:762
  347.3 5.4 %tail.2 = bf16[512,512]{1,0:T(8,128)(2,1)} custom-call(s32[1]{0:T(128)} %bitcast.2.me_ref, f32[1,512]{1,0:T(1,128)} %bitcast.95, bf16[1536,512]{1,0:T(8,128)(2,1)} %bitcast.75, f32[512,512]{1,0:T(8,128)} %get-tuple-element.199.middle_ref, bf16[512,512]{1,0:T(8,128)(2,1)} %copy-done.6, bf16[8,192,1024]{2,1,0:T(8,128)(2,1)} %all-to-all-done.4.grads), custom_call_target="tpu_custom_call" | custom-call | flops 805306368 | bytes 1572864 | tf_op jit(solution)/shard_map/tail/pallas_call | solution.py:415
  352.7 5.4 %tail.3.mine = bf16[512,512]{1,0:T(8,128)(2,1)} custom-call(s32[1]{0:T(128)} %bitcast.2.me_ref, f32[1,512]{1,0:T(1,128)} %bitcast.96, bf16[1536,512]{1,0:T(8,128)(2,1)} %bitcast.76, f32[512,512]{1,0:T(8,128)} %get-tuple-element.212.middle_ref, bf16[512,512]{1,0:T(8,128)(2,1)} %get-tuple-element.294.block.refs_0_, bf16[8,192,1024]{2,1,0:T(8,128)(2,1)} %all-to-all-done.4.grads), custom_call_target="tpu_custom_call" | custom-call | flops 805306368 | bytes 1572864 | tf_op jit(solution)/shard_map/tail/pallas_call | solution.py:415
  364.2 4.2 %collective-permute-done.43 = bf16[208,512]{1,0:T(8,128)(2,1)S(1)} collective-permute-done((bf16[208,512]{1,0:T(8,128)(2,1)S(1)}, bf16[208,512]{1,0:T(8,128)(2,1)S(1)}, u32[]{:S(2)}, u32[]{:S(2)}) %collective-permute-start.43) | collective-permute-done | bytes 213024 | tf_op jit(solution)/shard_map/ppermute | solution.py:770
  380.2 10.9 %collective-permute-done.38.back = bf16[512,512]{1,0:T(8,128)(2,1)} collective-permute-done((bf16[512,512]{1,0:T(8,128)(2,1)}, bf16[512,512]{1,0:T(8,128)(2,1)}, u32[]{:S(2)}, u32[]{:S(2)}) %collective-permute-start.38) | collective-permute-done | bytes 524320 | tf_op jit(solution)/shard_map/ppermute | solution.py:766
  399.9 4.0 unpack.1
  (258 shorter events, 107.4 us)
Async XLA Ops:
  10.4 32.9 %collective-permute-start.11 = (bf16[512,512]{1,0:T(8,128)(2,1)S(1)}, bf16[512,512]{1,0:T(8,128)(2,1)S(1)}, u32[]{:S(2)}, u32[]{:S(2)}) collective-permute-start(bf16[512,512]{1,0:T(8,128)(2,1)S(1)} %get-tuple-element.130), channel_id=1, source_target_pairs={{0,8},{8,0},{1,9},{9,1},{2,10},{10,2},{3,11},{11,3},{4,12},{12,4},... | collective-permute-start | bytes 1572872 | tf_op jit(solution)/shard_map/ppermute | solution.py:766
  22.1 17.9 %all-to-all-start = ((s32[8,2,1024]{2,1,0:T(2,128)}), s32[8,2,1024]{2,1,0:T(2,128)S(1)}, u32[]{:S(2)}, u32[]{:S(2)}) async-start(s32[8,2,1024]{2,1,0:T(2,128)} %broadcast_in_dim.177), calls=%async_computation | async-start | bytes 131072 | tf_op jit(solution)/shard_map/all_to_all | solution.py:774
  32.3 16.2 %collective-permute-start.8 = (bf16[192,512]{1,0:T(8,128)(2,1)S(1)}, bf16[192,512]{1,0:T(8,128)(2,1)}, u32[]{:S(2)}, u32[]{:S(2)}) collective-permute-start(bf16[192,512]{1,0:T(8,128)(2,1)S(1)} %copy-done.32), channel_id=1, source_target_pairs={{0,6},{1,7},{2,4},{3,5},{4,2},{5,3},{6,0},{7,1},{8,14},{9,15},{10,... | collective-permute-start | bytes 589832 | tf_op jit(solution)/shard_map/ppermute | solution.py:770
  32.4 16.1 %collective-permute-start.9 = (bf16[192,512]{1,0:T(8,128)(2,1)S(1)}, bf16[192,512]{1,0:T(8,128)(2,1)}, u32[]{:S(2)}, u32[]{:S(2)}) collective-permute-start(bf16[192,512]{1,0:T(8,128)(2,1)S(1)} %copy-done.31), channel_id=1, source_target_pairs={{0,1},{1,0},{2,3},{3,2},{4,5},{5,4},{6,7},{7,6},{8,9},{9,8},{10,11... | collective-permute-start | bytes 589832 | tf_op jit(solution)/shard_map/ppermute | solution.py:770
  44.1 16.8 %collective-permute-start.12 = (bf16[192,512]{1,0:T(8,128)(2,1)}, bf16[192,512]{1,0:T(8,128)(2,1)S(1)}, u32[]{:S(2)}, u32[]{:S(2)}) collective-permute-start(bf16[192,512]{1,0:T(8,128)(2,1)} %get-tuple-element.136), channel_id=1, source_target_pairs={{0,3},{1,2},{2,1},{3,0},{4,7},{5,6},{6,5},{7,4},{8,11},{9,10},{10,... | collective-permute-start | bytes 589832 | tf_op jit(solution)/shard_map/ppermute | solution.py:770
  45.3 15.6 %collective-permute-start.13 = (bf16[192,512]{1,0:T(8,128)(2,1)}, bf16[192,512]{1,0:T(8,128)(2,1)S(1)}, u32[]{:S(2)}, u32[]{:S(2)}) collective-permute-start(bf16[192,512]{1,0:T(8,128)(2,1)} %get-tuple-element.137), channel_id=1, source_target_pairs={{0,7},{1,6},{2,5},{3,4},{4,3},{5,2},{6,1},{7,0},{8,15},{9,14},{10,... | collective-permute-start | bytes 589832 | tf_op jit(solution)/shard_map/ppermute | solution.py:770
  77.0 43.9 %collective-permute-start.22 = (bf16[1024,512]{1,0:T(8,128)(2,1)S(1)}, bf16[1024,512]{1,0:T(8,128)(2,1)}, u32[]{:S(2)}, u32[]{:S(2)}) collective-permute-start(bf16[1024,512]{1,0:T(8,128)(2,1)S(1)} %pad_maximum_fusion.2.refs_0_), channel_id=1, source_target_pairs={{0,2},{1,3},{2,0},{3,1},{4,6},{5,7},{6,4},{7,5},{8,10},{9,11},{10,... | collective-permute-start | bytes 3145736 | tf_op jit(solution)/shard_map/ppermute | solution.py:770
  78.4 42.6 %collective-permute-start.23 = (bf16[1024,512]{1,0:T(8,128)(2,1)S(1)}, bf16[1024,512]{1,0:T(8,128)(2,1)}, u32[]{:S(2)}, u32[]{:S(2)}) collective-permute-start(bf16[1024,512]{1,0:T(8,128)(2,1)S(1)} %pad_maximum_fusion.2.refs_0_), channel_id=1, source_target_pairs={{0,4},{1,5},{2,6},{3,7},{4,0},{5,1},{6,2},{7,3},{8,12},{9,13},{10,... | collective-permute-start | bytes 3145736 | tf_op jit(solution)/shard_map/ppermute | solution.py:770
  79.3 41.6 %collective-permute-start.21 = (bf16[512,512]{1,0:T(8,128)(2,1)}, bf16[512,512]{1,0:T(8,128)(2,1)}, u32[]{:S(2)}, u32[]{:S(2)}) collective-permute-start(bf16[512,512]{1,0:T(8,128)(2,1)} %get-tuple-element.166), channel_id=1, source_target_pairs={{0,8},{8,0},{1,9},{9,1},{2,10},{10,2},{3,11},{11,3},{4,12},{12,4},... | collective-permute-start | bytes 1572872 | tf_op jit(solution)/shard_map/ppermute | solution.py:766
  140.2 26.2 %collective-permute-start.24 = (bf16[1024,512]{1,0:T(8,128)(2,1)S(1)}, bf16[1024,512]{1,0:T(8,128)(2,1)}, u32[]{:S(2)}, u32[]{:S(2)}) collective-permute-start(bf16[1024,512]{1,0:T(8,128)(2,1)S(1)} %pad_maximum_fusion.2.refs_0_), channel_id=1, source_target_pairs={{0,6},{1,7},{2,4},{3,5},{4,2},{5,3},{6,0},{7,1},{8,14},{9,15},{10,... | collective-permute-start | bytes 3145736 | tf_op jit(solution)/shard_map/ppermute | solution.py:770
  141.1 25.3 %collective-permute-start.25 = (bf16[1024,512]{1,0:T(8,128)(2,1)S(1)}, bf16[1024,512]{1,0:T(8,128)(2,1)}, u32[]{:S(2)}, u32[]{:S(2)}) collective-permute-start(bf16[1024,512]{1,0:T(8,128)(2,1)S(1)} %pad_maximum_fusion.2.refs_0_), channel_id=1, source_target_pairs={{0,1},{1,0},{2,3},{3,2},{4,5},{5,4},{6,7},{7,6},{8,9},{9,8},{10,11... | collective-permute-start | bytes 3145736 | tf_op jit(solution)/shard_map/ppermute | solution.py:786
  141.1 25.3 %collective-permute-start.26 = (bf16[1024,512]{1,0:T(8,128)(2,1)}, bf16[1024,512]{1,0:T(8,128)(2,1)}, u32[]{:S(2)}, u32[]{:S(2)}) collective-permute-start(bf16[1024,512]{1,0:T(8,128)(2,1)} %collective-permute-done.23.refs_1_), channel_id=1, source_target_pairs={{0,1},{1,0},{2,3},{3,2},{4,5},{5,4},{6,7},{7,6},{8,9},{9,8},{10,11... | collective-permute-start | bytes 3145736 | tf_op jit(solution)/shard_map/ppermute | solution.py:786
  141.6 24.8 %collective-permute-start.27 = (bf16[1024,512]{1,0:T(8,128)(2,1)}, bf16[1024,512]{1,0:T(8,128)(2,1)}, u32[]{:S(2)}, u32[]{:S(2)}) collective-permute-start(bf16[1024,512]{1,0:T(8,128)(2,1)} %collective-permute-done.22.refs_2_), channel_id=1, source_target_pairs={{0,1},{1,0},{2,3},{3,2},{4,5},{5,4},{6,7},{7,6},{8,9},{9,8},{10,11... | collective-permute-start | bytes 3145736 | tf_op jit(solution)/shard_map/ppermute | solution.py:786
  173.5 18.4 %all-to-all-start.2 = ((bf16[8,64,1024]{2,1,0:T(8,128)(2,1)}), bf16[8,64,1024]{2,1,0:T(8,128)(2,1)S(1)}, u32[]{:S(2)}, u32[]{:S(2)}) async-start(bf16[8,64,1024]{2,1,0:T(8,128)(2,1)} %get-tuple-element.179), calls=%async_computation.2 | async-start | bytes 2097152 | tf_op jit(solution)/shard_map/all_to_all | solution.py:774
  191.9 76.7 %collective-permute-start.29 = (bf16[512,512]{1,0:T(8,128)(2,1)}, bf16[512,512]{1,0:T(8,128)(2,1)}, u32[]{:S(2)}, u32[]{:S(2)}) collective-permute-start(bf16[512,512]{1,0:T(8,128)(2,1)} %get-tuple-element.202), channel_id=1, source_target_pairs={{0,8},{8,0},{1,9},{9,1},{2,10},{10,2},{3,11},{11,3},{4,12},{12,4},... | collective-permute-start | bytes 1572872 | tf_op jit(solution)/shard_map/ppermute | solution.py:766
  192.8 75.7 %all-to-all-start.3 = ((bf16[8,304,512]{2,1,0:T(8,128)(2,1)}), bf16[8,304,512]{2,1,0:T(8,128)(2,1)}, u32[]{:S(2)}, u32[]{:S(2)}) async-start(bf16[8,304,512]{2,1,0:T(8,128)(2,1)} %add.169), calls=%async_computation.3 | async-start | bytes 4980736 | tf_op jit(solution)/shard_map/all_to_all | solution.py:774
  268.6 78.7 %all-to-all-start.4 = ((bf16[8,192,1024]{2,1,0:T(8,128)(2,1)}), bf16[8,192,1024]{2,1,0:T(8,128)(2,1)}, u32[]{:S(2)}, u32[]{:S(2)}) async-start(bf16[8,192,1024]{2,1,0:T(8,128)(2,1)} %attention_backward.1.grads), calls=%async_computation.4 | async-start | bytes 6291456 | tf_op jit(solution)/shard_map/all_to_all | solution.py:774
  275.6 38.9 %collective-permute-start.33 = (bf16[304,512]{1,0:T(8,128)(2,1)S(1)}, bf16[304,512]{1,0:T(8,128)(2,1)}, u32[]{:S(2)}, u32[]{:S(2)}) collective-permute-start(bf16[304,512]{1,0:T(8,128)(2,1)S(1)} %convert_element_type.76), channel_id=1, source_target_pairs={{0,8},{8,0},{1,9},{9,1},{2,10},{10,2},{3,11},{11,3},{4,12},{12,4},... | collective-permute-start | bytes 933896 | tf_op jit(solution)/shard_map/ppermute | solution.py:766
  284.3 35.4 %collective-permute-start.31 = (bf16[192,640]{1,0:T(8,128)(2,1)S(1)}, bf16[192,640]{1,0:T(8,128)(2,1)S(1)}, u32[]{:S(2)}, u32[]{:S(2)}) collective-permute-start(bf16[192,640]{1,0:T(8,128)(2,1)S(1)} %convert_element_type.71), channel_id=1, source_target_pairs={{0,16},{16,0},{1,17},{17,1},{2,18},{18,2},{3,19},{19,3},{4,20},{20... | collective-permute-start | bytes 737288 | tf_op jit(solution)/shard_map/ppermute | solution.py:762
  332.6 59.9 %collective-permute-start.36 = (bf16[512,512]{1,0:T(8,128)(2,1)}, bf16[512,512]{1,0:T(8,128)(2,1)}, u32[]{:S(2)}, u32[]{:S(2)}) collective-permute-start(bf16[512,512]{1,0:T(8,128)(2,1)} %get-tuple-element.198.mine), channel_id=1, source_target_pairs={{0,1},{1,0},{2,3},{3,2},{4,5},{5,4},{6,7},{7,6},{8,9},{9,8},{10,11... | collective-permute-start | bytes 1572872 | tf_op jit(solution)/shard_map/ppermute | solution.py:786
  363.9 28.7 %collective-permute-start.37 = (bf16[512,512]{1,0:T(8,128)(2,1)}, bf16[512,512]{1,0:T(8,128)(2,1)}, u32[]{:S(2)}, u32[]{:S(2)}) collective-permute-start(bf16[512,512]{1,0:T(8,128)(2,1)} %collective-permute-done.29.back), channel_id=1, source_target_pairs={{0,1},{1,0},{2,3},{3,2},{4,5},{5,4},{6,7},{7,6},{8,9},{9,8},{10,11... | collective-permute-start | bytes 1572872 | tf_op jit(solution)/shard_map/ppermute | solution.py:786
  368.4 22.6 %collective-permute-start.38 = (bf16[512,512]{1,0:T(8,128)(2,1)}, bf16[512,512]{1,0:T(8,128)(2,1)}, u32[]{:S(2)}, u32[]{:S(2)}) collective-permute-start(bf16[512,512]{1,0:T(8,128)(2,1)} %tail.2), channel_id=1, source_target_pairs={{0,8},{8,0},{1,9},{9,1},{2,10},{10,2},{3,11},{11,3},{4,12},{12,4},... | collective-permute-start | bytes 1572872 | tf_op jit(solution)/shard_map/ppermute | solution.py:766
  369.8 30.1 %collective-permute-start.45 = (bf16[4,288,512]{2,1,0:T(8,128)(2,1)}, bf16[4,288,512]{2,1,0:T(8,128)(2,1)}, u32[]{:S(2)}, u32[]{:S(2)}) collective-permute-start(bf16[4,288,512]{2,1,0:T(8,128)(2,1)} %bitcast.46.near), channel_id=1, source_target_pairs={{0,16},{16,0},{1,17},{17,1},{2,18},{18,2},{3,19},{19,3},{4,20},{20... | collective-permute-start | bytes 3538952 | tf_op jit(solution)/shard_map/ppermute | solution.py:762
  379.6 15.8 %collective-permute-start.39 = (bf16[512,512]{1,0:T(8,128)(2,1)}, bf16[512,512]{1,0:T(8,128)(2,1)S(1)}, u32[]{:S(2)}, u32[]{:S(2)}) collective-permute-start(bf16[512,512]{1,0:T(8,128)(2,1)} %tail.3.mine), channel_id=1, source_target_pairs={{0,1},{1,0},{2,3},{3,2},{4,5},{5,4},{6,7},{7,6},{8,9},{9,8},{10,11... | collective-permute-start | bytes 1572872 | tf_op jit(solution)/shard_map/ppermute | solution.py:786
  (64 other events, 604.3 us)

commit v3 on v2

--- a/solution.py
+++ b/solution.py
@@ -474,12 +474,8 @@
     )(me, grads, *normed)
 
 
-def unpack_kernel(part_ref, near, far, fc_ref, proj_ref, out_ref, stage, sems):
-    wait(bring([
-        (source.at[step % 4], stage.at[step ^ part_ref[0]], sems.at[step])
-        for step, source in enumerate([near] * 4 + [far] * 4)
-    ]))
-    width = near.shape[2]
+def unpack_kernel(stage, fc_ref, proj_ref, out_ref):
+    width = stage.shape[2]
     fc_rows, proj_rows, out_rows = fc_ref.shape[0] // 8, proj_ref.shape[0] // 8, out_ref.shape[0] // 8
     for part in range(8):
         start = 0
@@ -493,20 +489,19 @@
             start += rows
 
 
-def unpack(part, near, far, wide):
-    rows, width = near.shape[1:]
+def unpack(parts, wide):
+    rows, width = parts.shape[1:]
     feats = rows - width // 8 * (wide // width) - wide // 8
     shape = jax.ShapeDtypeStruct
     return pl.pallas_call(
         unpack_kernel,
         out_shape=[shape((width, wide), F32), shape((wide, width), F32), shape((8 * feats, width), F32)],
-        in_specs=[smem()] + [hbm()] * 2,
+        in_specs=[vmem()],
         out_specs=[vmem()] * 3,
-        scratch_shapes=[pltpu.VMEM((8, rows, width), BF16), pltpu.SemaphoreType.DMA((8,))],
         compiler_params=pltpu.CompilerParams(vmem_limit_bytes=VMEM_LIMIT),
         cost_estimate=pl.CostEstimate(flops=0, bytes_accessed=48 * rows * width, transcendentals=0),
         name="unpack",
-    )(part, near, far)
+    )(parts)
 
 
 def middle_kernel(
@@ -801,7 +796,7 @@
     return {**moved, **dict(zip(steps, ended))}, values
 
 
-def from_group(where, mine, back):
+def from_group(where, mine, mine_there, back, rank=0):
     rows, width = mine.shape
     return pl.pallas_call(
         from_group_kernel,
@@ -809,9 +804,11 @@
         in_specs=[smem()] + [vmem()] * 4,
         out_specs=hbm(),
         scratch_shapes=[pltpu.SemaphoreType.DMA((4,))],
-        cost_estimate=pl.CostEstimate(flops=0, bytes_accessed=16 * rows * width, transcendentals=0),
+        cost_estimate=pl.CostEstimate(
+            flops=rank * 10**10, bytes_accessed=16 * rows * width, transcendentals=0
+        ),
         name="from_group",
-    )(where, mine, back, swap(mine), swap(back))
+    )(where, mine, back, mine_there, swap(back))
 
 
 def from_group_kernel(where_ref, mine, back, mine_there, back_there, out, sems):
@@ -876,7 +873,7 @@
     own_normed, segments = tie(own_normed, segments)
     code = share(segments * 2 + keep_mask, SEQ, 8)
     own_pieces = exchange(own_pieces)
-    own_pieces, other_tokens = after(own_pieces, (1, 2, 3, 4, 5), other_tokens)
+    own_pieces, other_tokens = after(own_pieces, (2, 4), other_tokens)
     code = lax.dynamic_index_in_dim(code, half, 1, keepdims=False)
     code = code.reshape(1, -1)
     table = tile_table(code[0] >> 1)
@@ -911,12 +908,14 @@
 
     grad_pieces = deal(grad_pieces, GROUP)
     shared_d, swapped, now = tie(shared_d, swapped, me)
+    swapped.append(swap(shared_d))
     there = weight_sums(1, now, saved[4], saved[5], mixed, [own_grad, other_grad], saved[:4])
     there, now = tie(there, now)
     here = weight_sums(0, now, saved[4], saved[5], mixed, [own_grad, other_grad], saved[:4])
     parts = here + swap(there)
-    grad_pieces, parts, layer_rows, shared_d, swapped = tie(
-        grad_pieces, parts, layer_rows, shared_d, swapped
+    layer_there = swap(layer_rows[0])
+    grad_pieces, parts, layer_rows, layer_there, shared_d, swapped = tie(
+        grad_pieces, parts, layer_rows, layer_there, shared_d, swapped
     )
     shared = [shared, shared_z, shared_x, shared_d]
 
@@ -930,28 +929,10 @@
     rows_here = total.shape[0] - 16
     small_grads = total[rows_here:]
     total = total[:rows_here].astype(BF16)
-    total = jnp.stack([total, pair(total, "zl")])
-    total = jnp.stack([total, pair(total, "x")])
-    swapped.append(swap(shared[3]))
     late = head_sums(me, head_grads, shared + swapped)
     late = late + pair(late.astype(BF16), "dp").astype(F32)
     late = late + across(late.astype(BF16)).astype(F32)
-    grads, late, total = tie(grads, late, total)
-
-    other_rows = tail(1, me, ln1_gain, heads_w, grad_middle[1], other_tokens, grads)
-    halves = jnp.stack([half, core]).astype(jnp.int32)
-    other_rows, ln1_own = tie(other_rows, ln1_gain)
-    back = across(other_rows)
-    own_rows = tail(0, me, ln1_own, heads_w, grad_middle[0], own_tokens, grads)
-    part = (4 * lax.axis_index("dp") + 2 * x + low_z).astype(jnp.int32)[None]
-    own_rows, late, layer_back, part = tie(own_rows, late, layer_back, part)
-
     with_normed, with_ones = late[:, :width], late[:, width : width + 1]
-    wide = w_fc.shape[1]
-    total = total.reshape(4, rows_here, width)
-    fc_grad, proj_grad, out_grad = unpack(part, total, pair(total, "dp"), wide)
-    grad_tokens = from_group(halves, own_rows, back)
-    layer_out = from_group(halves, layer_rows[0], layer_back)
     mine = heads_w[0].astype(F32)
     late = jnp.concatenate([
         with_normed * ln1_gain + with_ones * ln1_bias,
@@ -960,7 +941,23 @@
         jnp.sum(mine * with_ones, axis=0)[None],
         jnp.zeros((13, width), F32),
     ], axis=0).astype(BF16)
-    late = jnp.stack([late] + [move(late, step) for step in range(1, 4)]).astype(F32)
+    total = jnp.broadcast_to(total[None], (8,) + total.shape)
+    grads, late, total = tie(grads, late, total)
+    other_rows = tail(1, me, ln1_gain, heads_w, grad_middle[1], other_tokens, grads)
+    halves = jnp.stack([half, core]).astype(jnp.int32)
+    other_rows, ln1_own, total = tie(other_rows, ln1_gain, total)
+    back = across(other_rows)
+    own_rows = tail(0, me, ln1_own, heads_w, grad_middle[0], own_tokens, grads)
+    own_there = swap(own_rows)
+    total = deal(total, ("dp", "x", "zl"))
+    own_there, layer_back, late = tie(own_there, layer_back, late)
+    late = [late] + [move(late, step) for step in range(1, 4)]
+
+    wide = w_fc.shape[1]
+    fc_grad, proj_grad, out_grad = unpack(total, wide)
+    grad_tokens = from_group(halves, own_rows, own_there, back, 6)
+    layer_out = from_group(halves, layer_rows[0], layer_there, layer_back)
+    late = jnp.stack(late).astype(F32)
     ln1_sums = jnp.sum(late[:, 3 * feats + 1 : 3 * feats + 3], axis=0)
     ln1_sums = ln1_sums + swap(ln1_sums)
     late = jnp.take(late, order, axis=0)

time: 406 us -> 392 us (0.966)
  waiting for transfers between devices: 93.7 us -> 85.3 us
    ppermute x4 -> x1, waiting for transfers between devices: 19.7 us -> 4 us  [pair(): return lax.ppermute(array, axis, [(0, 1), (1, 0)])]
    all_to_all x4 -> x5, waiting for transfers between devices: 10.9 us -> 23.5 us  [deal(): return lax.all_to_all(array, axes, 0, 0, tiled=True)]
    ppermute x4 -> x1, starting transfers between devices: 9.49 us -> 0.07 us  [pair(): return lax.ppermute(array, axis, [(0, 1), (1, 0)])]
    ppermute x20, waiting for transfers between devices: 22 us -> 13.2 us  [move(): return lax.ppermute(piece, ALL_AXES, group_pairs(step)) if step else piece]
    all_to_all x4 -> x5, starting transfers between devices: 16.2 us -> 21.2 us  [deal(): return lax.all_to_all(array, axes, 0, 0, tiled=True)]
  transfers between devices with their start and end apart: 50 -> 48, of which waited for: 18 -> 15; matrix products, arithmetic and copies ran while one was open for 9% -> 8% of each run, Pallas kernels for 43% -> 42%
where the time goes in v3:
time: 392 us
  Pallas kernels  185 us (47%)
  waiting for transfers between devices  85.3 us (22%)
  starting transfers between devices  59.4 us (15%)
  other arithmetic  20.4 us (5%)
  local copies, waits for them, and re-layouts  19.4 us (5%)
  blocking collectives  19.2 us (5%)
    pallas_call x1, Pallas kernels, attention_backward(): pl.pallas_call(backward_kernel, out_shape=jax.ShapeDtypeStruct((8, 3 * HE...  72.8 us
    ppermute x6, waiting for transfers between devices, across(): return lax.ppermute(array, 'zh', [(0, 1), (1, 0)])  43.6 us
    pallas_call x1, Pallas kernels, attention_forward(): pl.pallas_call(forward_kernel, out_shape=[jax.ShapeDtypeStruct((8, HEAD_D...  39.7 us
    all_to_all x5, waiting for transfers between devices, deal(): return lax.all_to_all(array, axes, 0, 0, tiled=True)  23.5 us
    pallas_call x1, Pallas kernels, middle(): pl.pallas_call(middle_kernel, out_shape=[shape((block, width), BF16)] * 2...  22.4 us
    all_to_all x5, starting transfers between devices, deal(): return lax.all_to_all(array, axes, 0, 0, tiled=True)  21.2 us
    ppermute x20, starting transfers between devices, move(): return lax.ppermute(piece, ALL_AXES, group_pairs(step)) if step else piece  20.5 us
    all_to_all x1, blocking collectives, deal(): return lax.all_to_all(array, axes, 0, 0, tiled=True)  19.2 us
  transfers between devices with their start and end apart: 48, of which 15 were waited for; matrix products, arithmetic and copies ran while one was open for 8% of the time, Pallas kernels for 42%

profile of v3, /device:TPU:0, one launch (start us, length us, event | category | flops | bytes accessed | tf_op | source)
XLA Modules:
  0.0 391.9 jit_solution(5150166548829876166)
XLA Ops:
  15.6 5.2 %project.2 = (bf16[192,512]{1,0:T(8,128)(2,1)}, bf16[192,512]{1,0:T(8,128)(2,1)}, bf16[192,512]{1,0:T(8,128)(2,1)}, bf16[192,512]{1,0:T(8,128)(2,1)}, bf16[192,5...) custom-call(f32[1,512]{1,0:T(1,128)} %bitcast.84, ...), custom_call_target="tpu_custom_call" | custom-call | flops 805306368 | bytes 1572864 | tf_op jit(solution)/shard_map/project/pallas_call | solution.py:383
  31.8 8.2 %all-to-all-done = s32[8,2,1024]{2,1,0:T(2,128)S(1)} async-done(((s32[8,2,1024]{2,1,0:T(2,128)}), s32[8,2,1024]{2,1,0:T(2,128)S(1)}, u32[]{:S(2)}, u32[]{:S(2)}) %all-to-all-start) | async-done | bytes 65568 | tf_op jit(solution)/shard_map/all_to_all | solution.py:769
  46.2 5.1 %project.3 = (bf16[192,512]{1,0:T(8,128)(2,1)}, bf16[192,512]{1,0:T(8,128)(2,1)}, bf16[192,512]{1,0:T(8,128)(2,1)}, bf16[192,512]{1,0:T(8,128)(2,1)}, bf16[192,5...) custom-call(f32[1,512]{1,0:T(1,128)} %bitcast.85, ...), custom_call_target="tpu_custom_call" | custom-call | flops 805306368 | bytes 1572864 | tf_op jit(solution)/shard_map/project/pallas_call | solution.py:383
  69.3 4.1 %collective-permute-done.20.refs_15_ = bf16[192,512]{1,0:T(8,128)(2,1)S(1)} collective-permute-done((bf16[192,512]{1,0:T(8,128)(2,1)}, bf16[192,512]{1,0:T(8,128)(2,1)S(1)}, u32[]{:S(2)}, u32[]{:S(2)}) %collective-permute-start.20) | collective-permute-done | bytes 196640 | tf_op jit(solution)/shard_map/ppermute | solution.py:765
  78.2 39.7 %attention_forward.1 = (bf16[8,64,1024]{2,1,0:T(8,128)(2,1)}, f32[1,8192]{1,0:T(1,128)}) custom-call(s32[8,256]{1,0:T(8,128)} %stack.51.table_ref, s32[17]{0:T(128)} %pad_add_fusion.1.place_ref, s32[1,8192]{1,0:T(1,128)} %bitcast.79, bf16[192,512]{1,0:T(8,128)(2,1)} %get-tuple-element.145.refs_0_, bf16[192,512]{1,0:T(8,128)(2,1)} %collective-permute-done.6.refs_1_, ...), custom_call_target="tpu_custom_call" | custom-call | flops 17179869184 | bytes 4194304 | tf_op jit(solution)/shard_map/attention_forward/pallas_call | solution.py:269
  118.0 19.2 %all_to_all.30.mixed = bf16[8,64,1024]{2,1,0:T(8,128)(2,1)} all-to-all(bf16[8,64,1024]{2,1,0:T(8,128)(2,1)} %get-tuple-element.164.refs_16_), channel_id=1, replica_groups=mesh['dp'=2,'zh'=2,'zl'=2,'x'=2,'tensor'=2] {'tensor','x','zl'}, dimensions={0} | all-to-all | bytes 2097152 | tf_op jit(solution)/shard_map/all_to_all | solution.py:769
  138.6 22.4 %middle.1 = (bf16[512,512]{1,0:T(8,128)(2,1)}, bf16[512,512]{1,0:T(8,128)(2,1)}, f32[512,512]{1,0:T(8,128)}, f32[512,512]{1,0:T(8,128)}, bf16[8,64,1024]{2,1,0:T...) custom-call(s32[1]{0:T(128)} %bitcast.2.me_ref, ...), custom_call_target="tpu_custom_call" | custom-call | flops 9663676416 | bytes 16777216 | tf_op jit(solution)/shard_map/middle/pallas_call | solution.py:611
  163.5 6.9 %weight_sums.2 = bf16[8,304,512]{2,1,0:T(8,128)(2,1)} custom-call(s32[1]{0:T(128)} %bitcast.2.me_ref, f32[8,512]{1,0:T(8,128)} %get-tuple-element.180.vectors_ref, f32[8,1024]{1,0:T(8,128)} %get-tuple-element.181.pre_sums_ref, bf16[8,64,1024]{2,1,0:T(8,128)(2,1)} %all_to_all.30.mixed, bf16[512,512]{1,0:T(8,128)(2,1)} %get-tuple-element.290.refs_2_.refs_0_, ...), custom_call_target="tpu_custom_call" | custom-call | flops 2415919104 | bytes 6291456 | tf_op jit(solution)/shard_map/weight_sums/pallas_call | solution.py:718
  170.5 4.2 %all-to-all-start.2 = ((bf16[8,64,1024]{2,1,0:T(8,128)(2,1)}), bf16[8,64,1024]{2,1,0:T(8,128)(2,1)}, u32[]{:S(2)}, u32[]{:S(2)}) async-start(bf16[8,64,1024]{2,1,0:T(8,128)(2,1)} %get-tuple-element.175), calls=%async_computation.2 | async-start | bytes 2097152 | tf_op jit(solution)/shard_map/all_to_all | solution.py:769
  175.3 6.9 %weight_sums.3 = bf16[8,304,512]{2,1,0:T(8,128)(2,1)} custom-call(s32[1]{0:T(128)} %bitcast.2.me_ref, f32[8,512]{1,0:T(8,128)} %get-tuple-element.180.vectors_ref, f32[8,1024]{1,0:T(8,128)} %get-tuple-element.181.pre_sums_ref, bf16[8,64,1024]{2,1,0:T(8,128)(2,1)} %all_to_all.30.mixed, bf16[512,512]{1,0:T(8,128)(2,1)} %get-tuple-element.290.refs_2_.refs_0_, ...), custom_call_target="tpu_custom_call" | custom-call | flops 2415919104 | bytes 6291456 | tf_op jit(solution)/shard_map/weight_sums/pallas_call | solution.py:718
  182.3 4.6 %add.163 = bf16[8,304,512]{2,1,0:T(8,128)(2,1)} add(bf16[8,304,512]{2,1,0:T(8,128)(2,1)} %weight_sums.3, bf16[8,304,512]{2,1,0:T(8,128)(2,1)} %collective-permute-done.28) | non-fusion elementwise | flops 1245184 | bytes 7471104 | tf_op jit(solution)/shard_map/add | solution.py:915
  190.6 4.4 %all-to-all-start.3 = ((bf16[8,304,512]{2,1,0:T(8,128)(2,1)}), bf16[8,304,512]{2,1,0:T(8,128)(2,1)}, u32[]{:S(2)}, u32[]{:S(2)}) async-start(bf16[8,304,512]{2,1,0:T(8,128)(2,1)} %add.163), calls=%async_computation.3 | async-start | bytes 4980736 | tf_op jit(solution)/shard_map/all_to_all | solution.py:769
  195.0 72.8 %attention_backward.1.grads = bf16[8,192,1024]{2,1,0:T(8,128)(2,1)} custom-call(s32[8,256]{1,0:T(8,128)} %stack.51.table_ref, s32[17]{0:T(128)} %pad_add_fusion.1.place_ref, s32[1,8192]{1,0:T(1,128)} %bitcast.80, f32[1,8192]{1,0:T(1,128)} %get-tuple-element.196.lse_ref, bf16[192,512]{1,0:T(8,128)(2,1)} %get-tuple-element.145.refs_0_, ...), custom_call_target="tpu_custom_call" | custom-call | flops 64424509440 | bytes 8388608 | tf_op jit(solution)/shard_map/attention_backward/pallas_call | solution.py:304
  267.9 4.5 %all-to-all-start.4 = ((bf16[8,192,1024]{2,1,0:T(8,128)(2,1)}), bf16[8,192,1024]{2,1,0:T(8,128)(2,1)}, u32[]{:S(2)}, u32[]{:S(2)}) async-start(bf16[8,192,1024]{2,1,0:T(8,128)(2,1)} %attention_backward.1.grads), calls=%async_computation.4 | async-start | bytes 6291456 | tf_op jit(solution)/shard_map/all_to_all | solution.py:769
  272.3 5.6 %head_sums.1 = f32[192,640]{1,0:T(8,128)} custom-call(s32[1]{0:T(128)} %bitcast.2.me_ref, bf16[8,192,1024]{2,1,0:T(8,128)(2,1)} %attention_backward.1.grads, bf16[1024,512]{1,0:T(8,128)(2,1)} %copy-done.3, bf16[1024,512]{1,0:T(8,128)(2,1)} %collective-permute-done.23.refs_1_, bf16[1024,512]{1,0:T(8,128)(2,1)} %collective-permute-done.22.refs_2_, ...), custom_call_target="tpu_custom_call" | custom-call | flops 1610612736 | bytes 12582912 | tf_op jit(solution)/shard_map/head_sums/pallas_call | solution.py:459
  283.3 4.0 %collective-permute-done.32 = bf16[192,640]{1,0:T(8,128)(2,1)S(1)} collective-permute-done((bf16[192,640]{1,0:T(8,128)(2,1)S(1)}, bf16[192,640]{1,0:T(8,128)(2,1)S(1)}, u32[]{:S(2)}, u32[]{:S(2)}) %collective-permute-start.32) | collective-permute-done | bytes 245792 | tf_op jit(solution)/shard_map/ppermute | solution.py:757
  289.5 24.5 %collective-permute-done.34 = bf16[304,512]{1,0:T(8,128)(2,1)S(1)} collective-permute-done((bf16[304,512]{1,0:T(8,128)(2,1)S(1)}, bf16[304,512]{1,0:T(8,128)(2,1)S(1)}, u32[]{:S(2)}, u32[]{:S(2)}) %collective-permute-start.34) | collective-permute-done | bytes 311328 | tf_op jit(solution)/shard_map/ppermute | solution.py:761
  314.1 4.9 %collective-permute-done.33 = bf16[192,640]{1,0:T(8,128)(2,1)S(1)} collective-permute-done((bf16[192,640]{1,0:T(8,128)(2,1)S(1)}, bf16[192,640]{1,0:T(8,128)(2,1)S(1)}, u32[]{:S(2)}, u32[]{:S(2)}) %collective-permute-start.33) | collective-permute-done | bytes 245792 | tf_op jit(solution)/shard_map/ppermute | solution.py:761
  323.2 5.4 %tail.2 = bf16[512,512]{1,0:T(8,128)(2,1)} custom-call(s32[1]{0:T(128)} %bitcast.2.me_ref, f32[1,512]{1,0:T(1,128)} %bitcast.86, bf16[1536,512]{1,0:T(8,128)(2,1)} %bitcast.67, f32[512,512]{1,0:T(8,128)} %get-tuple-element.195.middle_ref, bf16[512,512]{1,0:T(8,128)(2,1)} %copy-done.6, bf16[8,192,1024]{2,1,0:T(8,128)(2,1)} %all-to-all-done.4.grads), custom_call_target="tpu_custom_call" | custom-call | flops 805306368 | bytes 1572864 | tf_op jit(solution)/shard_map/tail/pallas_call | solution.py:415
  328.6 5.4 %tail.3.mine = bf16[512,512]{1,0:T(8,128)(2,1)} custom-call(s32[1]{0:T(128)} %bitcast.2.me_ref, f32[1,512]{1,0:T(1,128)} %bitcast.87, bf16[1536,512]{1,0:T(8,128)(2,1)} %bitcast.68, f32[512,512]{1,0:T(8,128)} %get-tuple-element.210.middle_ref, bf16[512,512]{1,0:T(8,128)(2,1)} %get-tuple-element.292.block.refs_0_, bf16[8,192,1024]{2,1,0:T(8,128)(2,1)} %all-to-all-done.4.grads), custom_call_target="tpu_custom_call" | custom-call | flops 805306368 | bytes 1572864 | tf_op jit(solution)/shard_map/tail/pallas_call | solution.py:415
  342.2 4.4 %all-to-all-start.5 = ((bf16[8,288,512]{2,1,0:T(8,128)(2,1)}), bf16[8,288,512]{2,1,0:T(8,128)(2,1)}, u32[]{:S(2)}, u32[]{:S(2)}) async-start(bf16[8,288,512]{2,1,0:T(8,128)(2,1)} %broadcast_in_dim.189), calls=%async_computation.5 | async-start | bytes 4718592 | tf_op jit(solution)/shard_map/all_to_all | solution.py:769
  346.7 14.2 %collective-permute-done.37.back = bf16[512,512]{1,0:T(8,128)(2,1)} collective-permute-done((bf16[512,512]{1,0:T(8,128)(2,1)S(1)}, bf16[512,512]{1,0:T(8,128)(2,1)}, u32[]{:S(2)}, u32[]{:S(2)}) %collective-permute-start.37) | collective-permute-done | bytes 524320 | tf_op jit(solution)/shard_map/ppermute | solution.py:761
  376.3 11.6 %all-to-all-done.5.stage = bf16[8,288,512]{2,1,0:T(8,128)(2,1)} async-done(((bf16[8,288,512]{2,1,0:T(8,128)(2,1)}), bf16[8,288,512]{2,1,0:T(8,128)(2,1)}, u32[]{:S(2)}, u32[]{:S(2)}) %all-to-all-start.5) | async-done | bytes 2359328 | tf_op jit(solution)/shard_map/all_to_all | solution.py:769
  387.9 4.0 %unpack.1 = (f32[512,1024]{1,0:T(8,128)}, f32[1024,512]{1,0:T(8,128)}, f32[256,512]{1,0:T(8,128)}) custom-call(bf16[8,288,512]{2,1,0:T(8,128)(2,1)} %all-to-all-done.5.stage), custom_call_target="tpu_custom_call" | custom-call | bytes 7077888 | tf_op jit(solution)/shard_map/unpack/pallas_call | solution.py:496
  (238 shorter events, 96.9 us)
Async XLA Ops:
  10.4 33.6 %collective-permute-start.9 = (bf16[512,512]{1,0:T(8,128)(2,1)S(1)}, bf16[512,512]{1,0:T(8,128)(2,1)S(1)}, u32[]{:S(2)}, u32[]{:S(2)}) collective-permute-start(bf16[512,512]{1,0:T(8,128)(2,1)S(1)} %get-tuple-element.127), channel_id=1, source_target_pairs={{0,8},{8,0},{1,9},{9,1},{2,10},{10,2},{3,11},{11,3},{4,12},{12,4},... | collective-permute-start | bytes 1572872 | tf_op jit(solution)/shard_map/ppermute | solution.py:761
  21.5 18.5 %all-to-all-start = ((s32[8,2,1024]{2,1,0:T(2,128)}), s32[8,2,1024]{2,1,0:T(2,128)S(1)}, u32[]{:S(2)}, u32[]{:S(2)}) async-start(s32[8,2,1024]{2,1,0:T(2,128)} %broadcast_in_dim.178), calls=%async_computation | async-start | bytes 131072 | tf_op jit(solution)/shard_map/all_to_all | solution.py:769
  28.2 23.1 %collective-permute-start.6 = (bf16[192,512]{1,0:T(8,128)(2,1)}, bf16[192,512]{1,0:T(8,128)(2,1)}, u32[]{:S(2)}, u32[]{:S(2)}) collective-permute-start(bf16[192,512]{1,0:T(8,128)(2,1)} %get-tuple-element.124), channel_id=1, source_target_pairs={{0,4},{1,5},{2,6},{3,7},{4,0},{5,1},{6,2},{7,3},{8,12},{9,13},{10,... | collective-permute-start | bytes 589832 | tf_op jit(solution)/shard_map/ppermute | solution.py:765
  31.7 20.9 %collective-permute-start.10 = (bf16[192,512]{1,0:T(8,128)(2,1)}, bf16[192,512]{1,0:T(8,128)(2,1)}, u32[]{:S(2)}, u32[]{:S(2)}) collective-permute-start(bf16[192,512]{1,0:T(8,128)(2,1)} %get-tuple-element.129), channel_id=1, source_target_pairs={{0,6},{1,7},{2,4},{3,5},{4,2},{5,3},{6,0},{7,1},{8,14},{9,15},{10,... | collective-permute-start | bytes 589832 | tf_op jit(solution)/shard_map/ppermute | solution.py:765
  73.4 44.6 %collective-permute-start.22 = (bf16[1024,512]{1,0:T(8,128)(2,1)S(1)}, bf16[1024,512]{1,0:T(8,128)(2,1)}, u32[]{:S(2)}, u32[]{:S(2)}) collective-permute-start(bf16[1024,512]{1,0:T(8,128)(2,1)S(1)} %pad_maximum_fusion.1.refs_0_), channel_id=1, source_target_pairs={{0,2},{1,3},{2,0},{3,1},{4,6},{5,7},{6,4},{7,5},{8,10},{9,11},{10,... | collective-permute-start | bytes 3145736 | tf_op jit(solution)/shard_map/ppermute | solution.py:765
  74.0 44.0 %collective-permute-start.23 = (bf16[1024,512]{1,0:T(8,128)(2,1)S(1)}, bf16[1024,512]{1,0:T(8,128)(2,1)}, u32[]{:S(2)}, u32[]{:S(2)}) collective-permute-start(bf16[1024,512]{1,0:T(8,128)(2,1)S(1)} %pad_maximum_fusion.1.refs_0_), channel_id=1, source_target_pairs={{0,4},{1,5},{2,6},{3,7},{4,0},{5,1},{6,2},{7,3},{8,12},{9,13},{10,... | collective-permute-start | bytes 3145736 | tf_op jit(solution)/shard_map/ppermute | solution.py:765
  74.8 43.1 %collective-permute-start.21 = (bf16[512,512]{1,0:T(8,128)(2,1)}, bf16[512,512]{1,0:T(8,128)(2,1)}, u32[]{:S(2)}, u32[]{:S(2)}) collective-permute-start(bf16[512,512]{1,0:T(8,128)(2,1)} %get-tuple-element.162), channel_id=1, source_target_pairs={{0,8},{8,0},{1,9},{9,1},{2,10},{10,2},{3,11},{11,3},{4,12},{12,4},... | collective-permute-start | bytes 1572872 | tf_op jit(solution)/shard_map/ppermute | solution.py:761
  137.2 26.2 %collective-permute-start.24 = (bf16[1024,512]{1,0:T(8,128)(2,1)S(1)}, bf16[1024,512]{1,0:T(8,128)(2,1)}, u32[]{:S(2)}, u32[]{:S(2)}) collective-permute-start(bf16[1024,512]{1,0:T(8,128)(2,1)S(1)} %pad_maximum_fusion.1.refs_0_), channel_id=1, source_target_pairs={{0,6},{1,7},{2,4},{3,5},{4,2},{5,3},{6,0},{7,1},{8,14},{9,15},{10,... | collective-permute-start | bytes 3145736 | tf_op jit(solution)/shard_map/ppermute | solution.py:765
  138.1 25.3 %collective-permute-start.25 = (bf16[1024,512]{1,0:T(8,128)(2,1)S(1)}, bf16[1024,512]{1,0:T(8,128)(2,1)}, u32[]{:S(2)}, u32[]{:S(2)}) collective-permute-start(bf16[1024,512]{1,0:T(8,128)(2,1)S(1)} %pad_maximum_fusion.1.refs_0_), channel_id=1, source_target_pairs={{0,1},{1,0},{2,3},{3,2},{4,5},{5,4},{6,7},{7,6},{8,9},{9,8},{10,11... | collective-permute-start | bytes 3145736 | tf_op jit(solution)/shard_map/ppermute | solution.py:781
  138.1 25.3 %collective-permute-start.26 = (bf16[1024,512]{1,0:T(8,128)(2,1)}, bf16[1024,512]{1,0:T(8,128)(2,1)}, u32[]{:S(2)}, u32[]{:S(2)}) collective-permute-start(bf16[1024,512]{1,0:T(8,128)(2,1)} %collective-permute-done.23.refs_1_), channel_id=1, source_target_pairs={{0,1},{1,0},{2,3},{3,2},{4,5},{5,4},{6,7},{7,6},{8,9},{9,8},{10,11... | collective-permute-start | bytes 3145736 | tf_op jit(solution)/shard_map/ppermute | solution.py:781
  138.6 24.8 %collective-permute-start.27 = (bf16[1024,512]{1,0:T(8,128)(2,1)}, bf16[1024,512]{1,0:T(8,128)(2,1)}, u32[]{:S(2)}, u32[]{:S(2)}) collective-permute-start(bf16[1024,512]{1,0:T(8,128)(2,1)} %collective-permute-done.22.refs_2_), channel_id=1, source_target_pairs={{0,1},{1,0},{2,3},{3,2},{4,5},{5,4},{6,7},{7,6},{8,9},{9,8},{10,11... | collective-permute-start | bytes 3145736 | tf_op jit(solution)/shard_map/ppermute | solution.py:781
  170.5 19.1 %all-to-all-start.2 = ((bf16[8,64,1024]{2,1,0:T(8,128)(2,1)}), bf16[8,64,1024]{2,1,0:T(8,128)(2,1)}, u32[]{:S(2)}, u32[]{:S(2)}) async-start(bf16[8,64,1024]{2,1,0:T(8,128)(2,1)} %get-tuple-element.175), calls=%async_computation.2 | async-start | bytes 2097152 | tf_op jit(solution)/shard_map/all_to_all | solution.py:769
  174.8 14.9 %collective-permute-start.30 = (bf16[1024,512]{1,0:T(8,128)(2,1)}, bf16[1024,512]{1,0:T(8,128)(2,1)S(1)}, u32[]{:S(2)}, u32[]{:S(2)}) collective-permute-start(bf16[1024,512]{1,0:T(8,128)(2,1)} %collective-permute-done.24.refs_3_), channel_id=1, source_target_pairs={{0,1},{1,0},{2,3},{3,2},{4,5},{5,4},{6,7},{7,6},{8,9},{9,8},{10,11... | collective-permute-start | bytes 3145736 | tf_op jit(solution)/shard_map/ppermute | solution.py:781
  189.6 78.2 %collective-permute-start.31 = (bf16[512,512]{1,0:T(8,128)(2,1)}, bf16[512,512]{1,0:T(8,128)(2,1)}, u32[]{:S(2)}, u32[]{:S(2)}) collective-permute-start(bf16[512,512]{1,0:T(8,128)(2,1)} %get-tuple-element.198), channel_id=1, source_target_pairs={{0,8},{8,0},{1,9},{9,1},{2,10},{10,2},{3,11},{11,3},{4,12},{12,4},... | collective-permute-start | bytes 1572872 | tf_op jit(solution)/shard_map/ppermute | solution.py:761
  190.6 77.2 %all-to-all-start.3 = ((bf16[8,304,512]{2,1,0:T(8,128)(2,1)}), bf16[8,304,512]{2,1,0:T(8,128)(2,1)}, u32[]{:S(2)}, u32[]{:S(2)}) async-start(bf16[8,304,512]{2,1,0:T(8,128)(2,1)} %add.163), calls=%async_computation.3 | async-start | bytes 4980736 | tf_op jit(solution)/shard_map/all_to_all | solution.py:769
  267.9 53.8 %all-to-all-start.4 = ((bf16[8,192,1024]{2,1,0:T(8,128)(2,1)}), bf16[8,192,1024]{2,1,0:T(8,128)(2,1)}, u32[]{:S(2)}, u32[]{:S(2)}) async-start(bf16[8,192,1024]{2,1,0:T(8,128)(2,1)} %attention_backward.1.grads), calls=%async_computation.4 | async-start | bytes 6291456 | tf_op jit(solution)/shard_map/all_to_all | solution.py:769
  281.3 32.7 %collective-permute-start.34 = (bf16[304,512]{1,0:T(8,128)(2,1)S(1)}, bf16[304,512]{1,0:T(8,128)(2,1)S(1)}, u32[]{:S(2)}, u32[]{:S(2)}) collective-permute-start(bf16[304,512]{1,0:T(8,128)(2,1)S(1)} %convert_element_type.71), channel_id=1, source_target_pairs={{0,8},{8,0},{1,9},{9,1},{2,10},{10,2},{3,11},{11,3},{4,12},{12,4},... | collective-permute-start | bytes 933896 | tf_op jit(solution)/shard_map/ppermute | solution.py:761
  287.4 31.6 %collective-permute-start.33 = (bf16[192,640]{1,0:T(8,128)(2,1)S(1)}, bf16[192,640]{1,0:T(8,128)(2,1)S(1)}, u32[]{:S(2)}, u32[]{:S(2)}) collective-permute-start(bf16[192,640]{1,0:T(8,128)(2,1)S(1)} %fusion.3), channel_id=1, source_target_pairs={{0,8},{8,0},{1,9},{9,1},{2,10},{10,2},{3,11},{11,3},{4,12},{12,4},... | collective-permute-start | bytes 737288 | tf_op jit(solution)/shard_map/ppermute | solution.py:761
  334.4 26.4 %collective-permute-start.37 = (bf16[512,512]{1,0:T(8,128)(2,1)S(1)}, bf16[512,512]{1,0:T(8,128)(2,1)}, u32[]{:S(2)}, u32[]{:S(2)}) collective-permute-start(bf16[512,512]{1,0:T(8,128)(2,1)S(1)} %copy-done.7), channel_id=1, source_target_pairs={{0,8},{8,0},{1,9},{9,1},{2,10},{10,2},{3,11},{11,3},{4,12},{12,4},... | collective-permute-start | bytes 1572872 | tf_op jit(solution)/shard_map/ppermute | solution.py:761
  337.8 23.0 %collective-permute-start.41 = (bf16[208,512]{1,0:T(8,128)(2,1)S(1)}, bf16[208,512]{1,0:T(8,128)(2,1)S(1)}, u32[]{:S(2)}, u32[]{:S(2)}) collective-permute-start(bf16[208,512]{1,0:T(8,128)(2,1)S(1)} %concatenate.21), channel_id=1, source_target_pairs={{0,6},{1,7},{2,4},{3,5},{4,2},{5,3},{6,0},{7,1},{8,14},{9,15},{10,... | collective-permute-start | bytes 638984 | tf_op jit(solution)/shard_map/ppermute | solution.py:765
  340.3 20.6 %collective-permute-start.40 = (bf16[208,512]{1,0:T(8,128)(2,1)S(1)}, bf16[208,512]{1,0:T(8,128)(2,1)S(1)}, u32[]{:S(2)}, u32[]{:S(2)}) collective-permute-start(bf16[208,512]{1,0:T(8,128)(2,1)S(1)} %concatenate.21), channel_id=1, source_target_pairs={{0,2},{1,3},{2,0},{3,1},{4,6},{5,7},{6,4},{7,5},{8,10},{9,11},{10,... | collective-permute-start | bytes 638984 | tf_op jit(solution)/shard_map/ppermute | solution.py:765
  340.8 20.0 %collective-permute-start.39 = (bf16[208,512]{1,0:T(8,128)(2,1)S(1)}, bf16[208,512]{1,0:T(8,128)(2,1)S(1)}, u32[]{:S(2)}, u32[]{:S(2)}) collective-permute-start(bf16[208,512]{1,0:T(8,128)(2,1)S(1)} %concatenate.21), channel_id=1, source_target_pairs={{0,4},{1,5},{2,6},{3,7},{4,0},{5,1},{6,2},{7,3},{8,12},{9,13},{10,... | collective-permute-start | bytes 638984 | tf_op jit(solution)/shard_map/ppermute | solution.py:765
  342.2 45.7 %all-to-all-start.5 = ((bf16[8,288,512]{2,1,0:T(8,128)(2,1)}), bf16[8,288,512]{2,1,0:T(8,128)(2,1)}, u32[]{:S(2)}, u32[]{:S(2)}) async-start(bf16[8,288,512]{2,1,0:T(8,128)(2,1)} %broadcast_in_dim.189), calls=%async_computation.5 | async-start | bytes 4718592 | tf_op jit(solution)/shard_map/all_to_all | solution.py:769
  346.6 23.9 %collective-permute-start.36 = (bf16[512,512]{1,0:T(8,128)(2,1)}, bf16[512,512]{1,0:T(8,128)(2,1)}, u32[]{:S(2)}, u32[]{:S(2)}) collective-permute-start(bf16[512,512]{1,0:T(8,128)(2,1)} %collective-permute-done.31.back), channel_id=1, source_target_pairs={{0,1},{1,0},{2,3},{3,2},{4,5},{5,4},{6,7},{7,6},{8,9},{9,8},{10,11... | collective-permute-start | bytes 1572872 | tf_op jit(solution)/shard_map/ppermute | solution.py:781
  (57 other events, 554.6 us)

commit v4 on v3

--- a/solution.py
+++ b/solution.py
@@ -50,10 +50,12 @@
     for index in range(16):
         span = at(place_ref[index])
         for part_at, (array, rows, piece_rows) in enumerate(whole):
+            first = (index // 8) * TILE
             if len(pieces) == 16:
                 piece = pieces[index].at[piece_rows, :]
+            elif len(pieces) == 8:
+                piece = pieces[index % 8].at[piece_rows, first : first + TILE]
             else:
-                first = (index // 8) * TILE
                 device = (index % 8) ^ place_ref[16]
                 piece = pieces[0].at[device, piece_rows, first : first + TILE]
             copies.append((piece, array.at[rows, span], sems.at[parts + part_at, index]))
@@ -105,8 +107,8 @@
 
 
 def forward_kernel(table_ref, place_ref, code_ref, *refs):
-    pieces, outs, lse_ref = refs[:16], refs[16:17], refs[17]
-    query_t, key_t, value_t, key_row, out_t, score_a, score_b, accum, peak, sems = refs[18:]
+    pieces, outs, lse_ref = refs[:16], refs[16:24], refs[24]
+    query_t, key_t, value_t, key_row, out_t, score_a, score_b, accum, peak, sems = refs[25:]
     feats = HEAD_DIM
     head = slice(0, feats)
     arrived = bring(moves(place_ref, sems, [
@@ -170,9 +172,9 @@
 
 
 def backward_kernel(table_ref, place_ref, code_ref, lse_ref, *refs):
-    pieces, mixed, grads, outs = refs[:16], refs[16:17], refs[17:18], refs[18:19]
+    pieces, mixed, grads, outs = refs[:16], refs[16:24], refs[24:25], refs[25:26]
     (query_t, key_t, value_t, grad_t, mixed_t, key_row, value_row, query_row, grad_row, delta,
-     sum_q, sum_k, sum_v, score_a, score_b, dp_a, dp_b, sems) = refs[19:]
+     sum_q, sum_k, sum_v, score_a, score_b, dp_a, dp_b, sems) = refs[26:]
     feats = HEAD_DIM
     head = slice(0, feats)
     of_key, of_value = slice(feats, 2 * feats), slice(2 * feats, 3 * feats)
@@ -269,11 +271,10 @@
     out = pl.pallas_call(
         forward_kernel,
         out_shape=[
-            jax.ShapeDtypeStruct((8, HEAD_DIM, 2 * TILE), BF16),
-            jax.ShapeDtypeStruct((1, length), F32),
-        ],
+            jax.ShapeDtypeStruct((HEAD_DIM, 2 * TILE), BF16)
+        ] * 8 + [jax.ShapeDtypeStruct((1, length), F32)],
         in_specs=[smem(), smem(), vmem()] + [hbm()] * 16,
-        out_specs=[hbm(), vmem()],
+        out_specs=[hbm()] * 8 + [vmem()],
         scratch_shapes=[
             pltpu.VMEM((wide, length), BF16),
             pltpu.VMEM((HEAD_DIM, length), BF16),
@@ -294,7 +295,7 @@
         ),
         name="attention_forward",
     )(table, place, code, *pieces)
-    return out
+    return out[:8], out[8]
 
 
 def attention_backward(table, place, code, lse, pieces, mixed, grads):
@@ -304,7 +305,7 @@
     return pl.pallas_call(
         backward_kernel,
         out_shape=jax.ShapeDtypeStruct((8, 3 * HEAD_DIM, 2 * TILE), BF16),
-        in_specs=[smem(), smem(), vmem(), vmem()] + [hbm()] * 18,
+        in_specs=[smem(), smem(), vmem(), vmem()] + [hbm()] * 25,
         out_specs=hbm(),
         scratch_shapes=[
             pltpu.VMEM((wide, length), BF16),
@@ -333,7 +334,7 @@
             transcendentals=pairs * TILE * TILE,
         ),
         name="attention_backward",
-    )(table, place, code, lse, *pieces, mixed, grads)
+    )(table, place, code, lse, *pieces, *mixed, grads)
 
 
 def tile_table(segment_row):
@@ -505,8 +506,9 @@
 
 
 def middle_kernel(
-    me_ref, out_bias, gain_ref, offset_ref, proj_bias, fc_bias_a, fc_bias_b, mixed, *refs
+    me_ref, out_bias, gain_ref, offset_ref, proj_bias, fc_bias_a, fc_bias_b, *refs
 ):
+    mixed, refs = refs[:8], refs[8:]
     (tokens_own, tokens_other, grad_own, grad_other, out_a, out_b, fc_a, fc_b, proj_a, proj_b,
      layer_own, layer_other, middle_own, middle_other, grad_pieces, *refs) = refs
     (hidden_ref, act_ref, pre_ref, branch_ref, vectors_ref, pre_sums,
@@ -516,7 +518,7 @@
     block = tokens_own.shape[0]
     wide = fc_a.shape[1]
     step_rows = 256
-    first = bring([(mixed.at[i ^ me_ref[0]], mixed_t.at[i * feats : (i + 1) * feats, :], in_sems.at[i])
+    first = bring([(mixed[i], mixed_t.at[i * feats : (i + 1) * feats, :], in_sems.at[i])
                    for i in range(8)])
     own, other = slice(0, block), slice(block, 2 * block)
     first += bring([
@@ -615,7 +617,7 @@
         + [shape((8, feats, rows), BF16)]
         + [shape((rows, width), BF16), shape((2, rows, wide), BF16), shape((2, rows, wide), BF16),
            shape((rows, width), BF16), shape((8, width), F32), shape((8, wide), F32)],
-        in_specs=[smem()] + [vmem()] * 6 + [hbm()] * 11,
+        in_specs=[smem()] + [vmem()] * 6 + [hbm()] * 18,
         out_specs=[hbm()] * 9 + [vmem()] * 2,
         scratch_shapes=[
             pltpu.VMEM((8 * feats, rows), BF16),
@@ -637,16 +639,17 @@
         ],
         compiler_params=pltpu.CompilerParams(vmem_limit_bytes=VMEM_LIMIT),
         cost_estimate=pl.CostEstimate(
-            flops=2 * rows * width * (2 * width + 8 * wide),
+            flops=3 * rows * width * (2 * width + 8 * wide),
             bytes_accessed=32 * rows * width,
             transcendentals=2 * rows * wide,
         ),
         name="middle",
-    )(me, *biases, mixed, *blocks, *weights)
+    )(me, *biases, *mixed, *blocks, *weights)
     return out[0:2], out[2:4], out[4], out[5:]
 
 
-def weight_sums_kernel(half, me_ref, vectors_ref, pre_sums_ref, mixed, *refs):
+def weight_sums_kernel(half, me_ref, vectors_ref, pre_sums_ref, *refs):
+    mixed, refs = refs[:4], refs[4:]
     (grad_own, grad_other, hidden_ref, act_ref, pre_ref, branch_ref,
      out_ref, mixed_t, grads, hidden, act, pre, branch, fc_sum, proj_sum, out_sum, small,
      sems, out_sems) = refs
@@ -661,9 +664,8 @@
         (act_ref.at[half], act, sems.at[4]),
         (branch_ref, branch, sems.at[5]),
     ] + [
-        (mixed.at[(4 * half + i) ^ me_ref[0]], mixed_t.at[i * feats : (i + 1) * feats, :],
-         sems.at[6 + i])
-        for i in range(4)
+        (piece, mixed_t.at[i * feats : (i + 1) * feats, :], sems.at[6 + i])
+        for i, piece in enumerate(mixed)
     ])
     rows = [vectors_ref[0:4, :]] + [
         pre_sums_ref[half : half + 1, i * width : (i + 1) * width] for i in range(wide // width)
@@ -718,7 +720,7 @@
     return pl.pallas_call(
         functools.partial(weight_sums_kernel, half),
         out_shape=jax.ShapeDtypeStruct((8, part_rows, width), BF16),
-        in_specs=[smem(), vmem(), vmem()] + [hbm()] * 7,
+        in_specs=[smem(), vmem(), vmem()] + [hbm()] * 10,
         out_specs=hbm(),
         scratch_shapes=[
             pltpu.VMEM((4 * feats, rows), BF16),
@@ -736,12 +738,12 @@
         ],
         compiler_params=pltpu.CompilerParams(vmem_limit_bytes=VMEM_LIMIT),
         cost_estimate=pl.CostEstimate(
-            flops=rows * width * (width + 4 * wide),
+            flops=3 * rows * width * (width + 4 * wide),
             bytes_accessed=12 * rows * width,
             transcendentals=0,
         ),
         name="weight_sums",
-    )(me, vectors, pre_sums, mixed, *grad_blocks, *saved)
+    )(me, vectors, pre_sums, *mixed[4 * half : 4 * half + 4], *grad_blocks, *saved)
 
 
 def group_pairs(step):
@@ -874,6 +876,8 @@
     code = share(segments * 2 + keep_mask, SEQ, 8)
     own_pieces = exchange(own_pieces)
     own_pieces, other_tokens = after(own_pieces, (2, 4), other_tokens)
+    other_pieces, other_normed = project(ln1_gain, ln1_bias, heads_w, bias, other_tokens)
+    code, other_normed = tie(code, other_normed)
     code = lax.dynamic_index_in_dim(code, half, 1, keepdims=False)
     code = code.reshape(1, -1)
     table = tile_table(code[0] >> 1)
@@ -883,7 +887,6 @@
     place = (4 * their_z + 2 * their_x + their_core).T.reshape(16)
     place = jnp.concatenate([place, me]).astype(jnp.int32)
 
-    other_pieces, other_normed = project(ln1_gain, ln1_bias, heads_w, bias, other_tokens)
     other_pieces = exchange(other_pieces)
     pieces = [own_pieces[i] for i in range(8)] + [other_pieces[i] for i in range(8)]
     own_grad, sent = block_of(cotangent, half, core), block_of(cotangent, 1 - half, core)
@@ -894,7 +897,8 @@
     shared_z = move(shared, 1)
     outs, lse = attention_forward(table, place, code, pieces)
     outs, other_grad, shared_x, shared_z = tie(outs, other_grad, shared_x, shared_z)
-    mixed = deal(outs, GROUP)
+    mixed = exchange(outs)
+    mixed = [mixed[i] for i in range(8)]
     mixed, shared, shared_x, shared_z = tie(mixed, shared, shared_x, shared_z)
     shared_d = move(shared, 3)
     swapped = [swap(shared), swap(shared_z), swap(shared_x)]

time: 392 us -> 390 us (level)
  blocking collectives: 19.2 us -> 0 us
  waiting for transfers between devices: 85.3 us -> 95.7 us
  starting transfers between devices: 59.4 us -> 69.4 us
    all_to_all x1 -> x0, blocking collectives: 19.2 us -> none  [deal(): return lax.all_to_all(array, axes, 0, 0, tiled=True)]
    ppermute x20 -> x27, waiting for transfers between devices: 13.2 us -> 24.3 us  [move(): return lax.ppermute(piece, ALL_AXES, group_pairs(step)) if step else piece]
    ppermute x20 -> x27, starting transfers between devices: 20.5 us -> 27.8 us  [move(): return lax.ppermute(piece, ALL_AXES, group_pairs(step)) if step else piece]
    all_to_all x5, waiting for transfers between devices: 23.5 us -> 17.8 us  [deal(): return lax.all_to_all(array, axes, 0, 0, tiled=True)]
    ppermute x6, waiting for transfers between devices: 43.6 us -> 49.3 us  [across(): return lax.ppermute(array, 'zh', [(0, 1), (1, 0)])]
  transfers between devices with their start and end apart: 48 -> 55, of which waited for: 15 -> 17; matrix products, arithmetic and copies ran while one was open for 8% -> 8% of each run, Pallas kernels for 42% -> 41%
where the time goes in v4:
time: 390 us
  Pallas kernels  183 us (47%)
  waiting for transfers between devices  95.7 us (25%)
  starting transfers between devices  69.4 us (18%)
  other arithmetic  20.5 us (5%)
  local copies, waits for them, and re-layouts  18.5 us (5%)
    pallas_call x1, Pallas kernels, attention_backward(): pl.pallas_call(backward_kernel, out_shape=jax.ShapeDtypeStruct((8, 3 * HE...  71.1 us
    ppermute x6, waiting for transfers between devices, across(): return lax.ppermute(array, 'zh', [(0, 1), (1, 0)])  49.3 us
    pallas_call x1, Pallas kernels, attention_forward(): pl.pallas_call(forward_kernel, out_shape=[jax.ShapeDtypeStruct((HEAD_DIM,...  39.1 us
    ppermute x27, starting transfers between devices, move(): return lax.ppermute(piece, ALL_AXES, group_pairs(step)) if step else piece  27.8 us
    ppermute x27, waiting for transfers between devices, move(): return lax.ppermute(piece, ALL_AXES, group_pairs(step)) if step else piece  24.3 us
    pallas_call x1, Pallas kernels, middle(): pl.pallas_call(middle_kernel, out_shape=[shape((block, width), BF16)] * 2...  22.1 us
    all_to_all x5, starting transfers between devices, deal(): return lax.all_to_all(array, axes, 0, 0, tiled=True)  21.2 us
    all_to_all x5, waiting for transfers between devices, deal(): return lax.all_to_all(array, axes, 0, 0, tiled=True)  17.8 us
  transfers between devices with their start and end apart: 55, of which 17 were waited for; matrix products, arithmetic and copies ran while one was open for 8% of the time, Pallas kernels for 41%

profile of v4, /device:TPU:0, one launch (start us, length us, event | category | flops | bytes accessed | tf_op | source)
XLA Modules:
  0.0 389.6 jit_solution(4573861475528739435)
XLA Ops:
  11.6 4.0 %collective-permute-start.8 = (bf16[512,512]{1,0:T(8,128)(2,1)S(1)}, bf16[512,512]{1,0:T(8,128)(2,1)S(1)}, u32[]{:S(2)}, u32[]{:S(2)}) collective-permute-start(bf16[512,512]{1,0:T(8,128)(2,1)S(1)} %get-tuple-element.148), channel_id=1, source_target_pairs={{0,8},{8,0},{1,9},{9,1},{2,10},{10,2},{3,11},{11,3},{4,12},{12,4},... | collective-permute-start | bytes 1572872 | tf_op jit(solution)/shard_map/ppermute | solution.py:763
  17.0 5.2 %project.2 = (bf16[192,512]{1,0:T(8,128)(2,1)}, bf16[192,512]{1,0:T(8,128)(2,1)}, bf16[192,512]{1,0:T(8,128)(2,1)}, bf16[192,512]{1,0:T(8,128)(2,1)}, bf16[192,5...) custom-call(f32[1,512]{1,0:T(1,128)} %bitcast.84, ...), custom_call_target="tpu_custom_call" | custom-call | flops 805306368 | bytes 1572864 | tf_op jit(solution)/shard_map/project/pallas_call | solution.py:384
  31.7 8.5 %collective-permute-done.8.block.refs_9_ = bf16[512,512]{1,0:T(8,128)(2,1)S(1)} collective-permute-done((bf16[512,512]{1,0:T(8,128)(2,1)S(1)}, bf16[512,512]{1,0:T(8,128)(2,1)S(1)}, u32[]{:S(2)}, u32[]{:S(2)}) %collective-permute-start.8) | collective-permute-done | bytes 524320 | tf_op jit(solution)/shard_map/ppermute | solution.py:763
  43.0 5.1 %project.3 = (bf16[192,512]{1,0:T(8,128)(2,1)}, bf16[192,512]{1,0:T(8,128)(2,1)}, bf16[192,512]{1,0:T(8,128)(2,1)}, bf16[192,512]{1,0:T(8,128)(2,1)}, bf16[192,5...) custom-call(f32[1,512]{1,0:T(1,128)} %bitcast.85, ...), custom_call_target="tpu_custom_call" | custom-call | flops 805306368 | bytes 1572864 | tf_op jit(solution)/shard_map/project/pallas_call | solution.py:384
  70.7 4.2 %collective-permute-done.20.refs_15_ = bf16[192,512]{1,0:T(8,128)(2,1)S(1)} collective-permute-done((bf16[192,512]{1,0:T(8,128)(2,1)}, bf16[192,512]{1,0:T(8,128)(2,1)S(1)}, u32[]{:S(2)}, u32[]{:S(2)}) %collective-permute-start.20) | collective-permute-done | bytes 196640 | tf_op jit(solution)/shard_map/ppermute | solution.py:767
  79.4 39.1 %attention_forward.1 = (bf16[64,1024]{1,0:T(8,128)(2,1)}, bf16[64,1024]{1,0:T(8,128)(2,1)}, bf16[64,1024]{1,0:T(8,128)(2,1)}, bf16[64,1024]{1,0:T(8,128)(2,1)}, ...) custom-call(s32[8,256]{1,0:T(8,128)} %stack.51.table_ref, ...), custom_call_target="tpu_custom_call" | custom-call | flops 17179869184 | bytes 4194304 | tf_op jit(solution)/shard_map/attention_forward/pallas_call | solution.py:271
  128.4 5.4 %collective-permute-done.29.refs_6_.refs_2_ = bf16[64,1024]{1,0:T(8,128)(2,1)S(1)} collective-permute-done((bf16[64,1024]{1,0:T(8,128)(2,1)}, bf16[64,1024]{1,0:T(8,128)(2,1)S(1)}, u32[]{:S(2)}, u32[]{:S(2)}) %collective-permute-start.29) | collective-permute-done | bytes 131104 | tf_op jit(solution)/shard_map/ppermute | solution.py:767
  135.5 22.1 %middle.1 = (bf16[512,512]{1,0:T(8,128)(2,1)}, bf16[512,512]{1,0:T(8,128)(2,1)}, f32[512,512]{1,0:T(8,128)}, f32[512,512]{1,0:T(8,128)}, bf16[8,64,1024]{2,1,0:T...) custom-call(s32[1]{0:T(128)} %bitcast.2.me_ref, ...), custom_call_target="tpu_custom_call" | custom-call | flops 14495514624 | bytes 16777216 | tf_op jit(solution)/shard_map/middle/pallas_call | solution.py:613
  160.0 6.9 %weight_sums.2 = bf16[8,304,512]{2,1,0:T(8,128)(2,1)} custom-call(s32[1]{0:T(128)} %bitcast.2.me_ref, f32[8,512]{1,0:T(8,128)} %get-tuple-element.226.vectors_ref, f32[8,1024]{1,0:T(8,128)} %get-tuple-element.227.pre_sums_ref, bf16[64,1024]{1,0:T(8,128)(2,1)} %copy-done.32, bf16[64,1024]{1,0:T(8,128)(2,1)} %copy-done.33, bf16[64,1024]{1,0:T(8,128)(2,1)} %copy-done.34, ...), custom_call_target="tpu_custom_call" | custom-call | flops 7247757312 | bytes 6291456 | tf_op jit(solution)/shard_map/weight_sums/pallas_call | solution.py:720
  167.1 4.2 %all-to-all-start.1 = ((bf16[8,64,1024]{2,1,0:T(8,128)(2,1)}), bf16[8,64,1024]{2,1,0:T(8,128)(2,1)}, u32[]{:S(2)}, u32[]{:S(2)}) async-start(bf16[8,64,1024]{2,1,0:T(8,128)(2,1)} %get-tuple-element.221), calls=%async_computation.1 | async-start | bytes 2097152 | tf_op jit(solution)/shard_map/all_to_all | solution.py:771
  171.9 6.9 %weight_sums.3 = bf16[8,304,512]{2,1,0:T(8,128)(2,1)} custom-call(s32[1]{0:T(128)} %bitcast.2.me_ref, f32[8,512]{1,0:T(8,128)} %get-tuple-element.226.vectors_ref, f32[8,1024]{1,0:T(8,128)} %get-tuple-element.227.pre_sums_ref, bf16[64,1024]{1,0:T(8,128)(2,1)} %get-tuple-element.206.refs_0_.refs_16_, bf16[64,1024]{1,0:T(8,128)(2,1)} %copy-done.29, ...), custom_call_target="tpu_custom_call" | custom-call | flops 7247757312 | bytes 6291456 | tf_op jit(solution)/shard_map/weight_sums/pallas_call | solution.py:720
  178.9 4.6 %add.163 = bf16[8,304,512]{2,1,0:T(8,128)(2,1)} add(bf16[8,304,512]{2,1,0:T(8,128)(2,1)} %weight_sums.3, bf16[8,304,512]{2,1,0:T(8,128)(2,1)} %collective-permute-done.35) | non-fusion elementwise | flops 1245184 | bytes 7471104 | tf_op jit(solution)/shard_map/add | solution.py:919
  187.2 4.6 %all-to-all-start.2 = ((bf16[8,304,512]{2,1,0:T(8,128)(2,1)}), bf16[8,304,512]{2,1,0:T(8,128)(2,1)}, u32[]{:S(2)}, u32[]{:S(2)}) async-start(bf16[8,304,512]{2,1,0:T(8,128)(2,1)} %add.163), calls=%async_computation.2 | async-start | bytes 4980736 | tf_op jit(solution)/shard_map/all_to_all | solution.py:771
  191.9 71.1 %attention_backward.1.grads = bf16[8,192,1024]{2,1,0:T(8,128)(2,1)} custom-call(s32[8,256]{1,0:T(8,128)} %stack.51.table_ref, s32[17]{0:T(128)} %pad_add_fusion.1.place_ref, s32[1,8192]{1,0:T(1,128)} %bitcast.80, f32[1,8192]{1,0:T(1,128)} %get-tuple-element.242.lse_ref, bf16[192,512]{1,0:T(8,128)(2,1)} %get-tuple-element.170.refs_0_, ...), custom_call_target="tpu_custom_call" | custom-call | flops 64424509440 | bytes 8388608 | tf_op jit(solution)/shard_map/attention_backward/pallas_call | solution.py:305
  263.0 4.5 %all-to-all-start.3 = ((bf16[8,192,1024]{2,1,0:T(8,128)(2,1)}), bf16[8,192,1024]{2,1,0:T(8,128)(2,1)}, u32[]{:S(2)}, u32[]{:S(2)}) async-start(bf16[8,192,1024]{2,1,0:T(8,128)(2,1)} %attention_backward.1.grads), calls=%async_computation.3 | async-start | bytes 6291456 | tf_op jit(solution)/shard_map/all_to_all | solution.py:771
  267.5 5.6 %head_sums.1 = f32[192,640]{1,0:T(8,128)} custom-call(s32[1]{0:T(128)} %bitcast.2.me_ref, bf16[8,192,1024]{2,1,0:T(8,128)(2,1)} %attention_backward.1.grads, bf16[1024,512]{1,0:T(8,128)(2,1)} %copy-done.3, bf16[1024,512]{1,0:T(8,128)(2,1)} %collective-permute-done.23.refs_1_, bf16[1024,512]{1,0:T(8,128)(2,1)} %collective-permute-done.22.refs_2_, ...), custom_call_target="tpu_custom_call" | custom-call | flops 1610612736 | bytes 12582912 | tf_op jit(solution)/shard_map/head_sums/pallas_call | solution.py:460
  280.2 4.2 %collective-permute-done.39 = bf16[192,640]{1,0:T(8,128)(2,1)S(1)} collective-permute-done((bf16[192,640]{1,0:T(8,128)(2,1)S(1)}, bf16[192,640]{1,0:T(8,128)(2,1)S(1)}, u32[]{:S(2)}, u32[]{:S(2)}) %collective-permute-start.39) | collective-permute-done | bytes 245792 | tf_op jit(solution)/shard_map/ppermute | solution.py:759
  286.0 23.2 %collective-permute-done.41 = bf16[304,512]{1,0:T(8,128)(2,1)S(1)} collective-permute-done((bf16[304,512]{1,0:T(8,128)(2,1)S(1)}, bf16[304,512]{1,0:T(8,128)(2,1)S(1)}, u32[]{:S(2)}, u32[]{:S(2)}) %collective-permute-start.41) | collective-permute-done | bytes 311328 | tf_op jit(solution)/shard_map/ppermute | solution.py:763
  309.3 4.9 %collective-permute-done.40 = bf16[192,640]{1,0:T(8,128)(2,1)S(1)} collective-permute-done((bf16[192,640]{1,0:T(8,128)(2,1)S(1)}, bf16[192,640]{1,0:T(8,128)(2,1)S(1)}, u32[]{:S(2)}, u32[]{:S(2)}) %collective-permute-start.40) | collective-permute-done | bytes 245792 | tf_op jit(solution)/shard_map/ppermute | solution.py:763
  318.4 5.4 %tail.2 = bf16[512,512]{1,0:T(8,128)(2,1)} custom-call(s32[1]{0:T(128)} %bitcast.2.me_ref, f32[1,512]{1,0:T(1,128)} %bitcast.86, bf16[1536,512]{1,0:T(8,128)(2,1)} %bitcast.67, f32[512,512]{1,0:T(8,128)} %get-tuple-element.241.middle_ref, bf16[512,512]{1,0:T(8,128)(2,1)} %copy-done.6, bf16[8,192,1024]{2,1,0:T(8,128)(2,1)} %all-to-all-done.3.grads), custom_call_target="tpu_custom_call" | custom-call | flops 805306368 | bytes 1572864 | tf_op jit(solution)/shard_map/tail/pallas_call | solution.py:416
  323.8 5.5 %tail.3.mine = bf16[512,512]{1,0:T(8,128)(2,1)} custom-call(s32[1]{0:T(128)} %bitcast.2.me_ref, f32[1,512]{1,0:T(1,128)} %bitcast.87, bf16[1536,512]{1,0:T(8,128)(2,1)} %bitcast.68, f32[512,512]{1,0:T(8,128)} %get-tuple-element.256.middle_ref, bf16[512,512]{1,0:T(8,128)(2,1)} %get-tuple-element.338.block.refs_8_, bf16[8,192,1024]{2,1,0:T(8,128)(2,1)} %all-to-all-done.3.grads), custom_call_target="tpu_custom_call" | custom-call | flops 805306368 | bytes 1572864 | tf_op jit(solution)/shard_map/tail/pallas_call | solution.py:416
  338.8 4.5 %all-to-all-start.4 = ((bf16[8,288,512]{2,1,0:T(8,128)(2,1)}), bf16[8,288,512]{2,1,0:T(8,128)(2,1)}, u32[]{:S(2)}, u32[]{:S(2)}) async-start(bf16[8,288,512]{2,1,0:T(8,128)(2,1)} %broadcast_in_dim.189), calls=%async_computation.4 | async-start | bytes 4718592 | tf_op jit(solution)/shard_map/all_to_all | solution.py:771
  343.3 12.7 %collective-permute-done.44.back = bf16[512,512]{1,0:T(8,128)(2,1)} collective-permute-done((bf16[512,512]{1,0:T(8,128)(2,1)S(1)}, bf16[512,512]{1,0:T(8,128)(2,1)}, u32[]{:S(2)}, u32[]{:S(2)}) %collective-permute-start.44) | collective-permute-done | bytes 524320 | tf_op jit(solution)/shard_map/ppermute | solution.py:763
  371.5 14.1 %all-to-all-done.4.stage = bf16[8,288,512]{2,1,0:T(8,128)(2,1)} async-done(((bf16[8,288,512]{2,1,0:T(8,128)(2,1)}), bf16[8,288,512]{2,1,0:T(8,128)(2,1)}, u32[]{:S(2)}, u32[]{:S(2)}) %all-to-all-start.4) | async-done | bytes 2359328 | tf_op jit(solution)/shard_map/all_to_all | solution.py:771
  (263 shorter events, 110.1 us)
Async XLA Ops:
  11.6 28.6 %collective-permute-start.8 = (bf16[512,512]{1,0:T(8,128)(2,1)S(1)}, bf16[512,512]{1,0:T(8,128)(2,1)S(1)}, u32[]{:S(2)}, u32[]{:S(2)}) collective-permute-start(bf16[512,512]{1,0:T(8,128)(2,1)S(1)} %get-tuple-element.148), channel_id=1, source_target_pairs={{0,8},{8,0},{1,9},{9,1},{2,10},{10,2},{3,11},{11,3},{4,12},{12,4},... | collective-permute-start | bytes 1572872 | tf_op jit(solution)/shard_map/ppermute | solution.py:763
  23.7 18.0 %collective-permute-start.7 = (bf16[192,512]{1,0:T(8,128)(2,1)}, bf16[192,512]{1,0:T(8,128)(2,1)}, u32[]{:S(2)}, u32[]{:S(2)}) collective-permute-start(bf16[192,512]{1,0:T(8,128)(2,1)} %get-tuple-element.147), channel_id=1, source_target_pairs={{0,1},{1,0},{2,3},{3,2},{4,5},{5,4},{6,7},{7,6},{8,9},{9,8},{10,11... | collective-permute-start | bytes 589832 | tf_op jit(solution)/shard_map/ppermute | solution.py:767
  24.4 23.7 %all-to-all-start = ((s32[8,2,1024]{2,1,0:T(2,128)}), s32[8,2,1024]{2,1,0:T(2,128)S(1)}, u32[]{:S(2)}, u32[]{:S(2)}) async-start(s32[8,2,1024]{2,1,0:T(2,128)} %broadcast_in_dim.178), calls=%async_computation | async-start | bytes 131072 | tf_op jit(solution)/shard_map/all_to_all | solution.py:771
  28.4 23.8 %collective-permute-start.9 = (bf16[192,512]{1,0:T(8,128)(2,1)}, bf16[192,512]{1,0:T(8,128)(2,1)}, u32[]{:S(2)}, u32[]{:S(2)}) collective-permute-start(bf16[192,512]{1,0:T(8,128)(2,1)} %get-tuple-element.153), channel_id=1, source_target_pairs={{0,4},{1,5},{2,6},{3,7},{4,0},{5,1},{6,2},{7,3},{8,12},{9,13},{10,... | collective-permute-start | bytes 589832 | tf_op jit(solution)/shard_map/ppermute | solution.py:767
  30.3 22.5 %collective-permute-start.10 = (bf16[192,512]{1,0:T(8,128)(2,1)}, bf16[192,512]{1,0:T(8,128)(2,1)}, u32[]{:S(2)}, u32[]{:S(2)}) collective-permute-start(bf16[192,512]{1,0:T(8,128)(2,1)} %get-tuple-element.155), channel_id=1, source_target_pairs={{0,6},{1,7},{2,4},{3,5},{4,2},{5,3},{6,0},{7,1},{8,14},{9,15},{10,... | collective-permute-start | bytes 589832 | tf_op jit(solution)/shard_map/ppermute | solution.py:767
  74.9 43.7 %collective-permute-start.22 = (bf16[1024,512]{1,0:T(8,128)(2,1)S(1)}, bf16[1024,512]{1,0:T(8,128)(2,1)}, u32[]{:S(2)}, u32[]{:S(2)}) collective-permute-start(bf16[1024,512]{1,0:T(8,128)(2,1)S(1)} %pad_maximum_fusion.1.refs_0_), channel_id=1, source_target_pairs={{0,2},{1,3},{2,0},{3,1},{4,6},{5,7},{6,4},{7,5},{8,10},{9,11},{10,... | collective-permute-start | bytes 3145736 | tf_op jit(solution)/shard_map/ppermute | solution.py:767
  75.3 43.3 %collective-permute-start.23 = (bf16[1024,512]{1,0:T(8,128)(2,1)S(1)}, bf16[1024,512]{1,0:T(8,128)(2,1)}, u32[]{:S(2)}, u32[]{:S(2)}) collective-permute-start(bf16[1024,512]{1,0:T(8,128)(2,1)S(1)} %pad_maximum_fusion.1.refs_0_), channel_id=1, source_target_pairs={{0,4},{1,5},{2,6},{3,7},{4,0},{5,1},{6,2},{7,3},{8,12},{9,13},{10,... | collective-permute-start | bytes 3145736 | tf_op jit(solution)/shard_map/ppermute | solution.py:767
  75.4 43.1 %collective-permute-start.21 = (bf16[512,512]{1,0:T(8,128)(2,1)}, bf16[512,512]{1,0:T(8,128)(2,1)}, u32[]{:S(2)}, u32[]{:S(2)}) collective-permute-start(bf16[512,512]{1,0:T(8,128)(2,1)} %get-tuple-element.194), channel_id=1, source_target_pairs={{0,8},{8,0},{1,9},{9,1},{2,10},{10,2},{3,11},{11,3},{4,12},{12,4},... | collective-permute-start | bytes 1572872 | tf_op jit(solution)/shard_map/ppermute | solution.py:763
  133.8 26.2 %collective-permute-start.31 = (bf16[1024,512]{1,0:T(8,128)(2,1)S(1)}, bf16[1024,512]{1,0:T(8,128)(2,1)}, u32[]{:S(2)}, u32[]{:S(2)}) collective-permute-start(bf16[1024,512]{1,0:T(8,128)(2,1)S(1)} %pad_maximum_fusion.1.refs_0_), channel_id=1, source_target_pairs={{0,6},{1,7},{2,4},{3,5},{4,2},{5,3},{6,0},{7,1},{8,14},{9,15},{10,... | collective-permute-start | bytes 3145736 | tf_op jit(solution)/shard_map/ppermute | solution.py:767
  134.8 25.2 %collective-permute-start.32 = (bf16[1024,512]{1,0:T(8,128)(2,1)S(1)}, bf16[1024,512]{1,0:T(8,128)(2,1)}, u32[]{:S(2)}, u32[]{:S(2)}) collective-permute-start(bf16[1024,512]{1,0:T(8,128)(2,1)S(1)} %pad_maximum_fusion.1.refs_0_), channel_id=1, source_target_pairs={{0,1},{1,0},{2,3},{3,2},{4,5},{5,4},{6,7},{7,6},{8,9},{9,8},{10,11... | collective-permute-start | bytes 3145736 | tf_op jit(solution)/shard_map/ppermute | solution.py:783
  134.9 25.2 %collective-permute-start.33 = (bf16[1024,512]{1,0:T(8,128)(2,1)}, bf16[1024,512]{1,0:T(8,128)(2,1)}, u32[]{:S(2)}, u32[]{:S(2)}) collective-permute-start(bf16[1024,512]{1,0:T(8,128)(2,1)} %collective-permute-done.23.refs_1_), channel_id=1, source_target_pairs={{0,1},{1,0},{2,3},{3,2},{4,5},{5,4},{6,7},{7,6},{8,9},{9,8},{10,11... | collective-permute-start | bytes 3145736 | tf_op jit(solution)/shard_map/ppermute | solution.py:783
  135.4 24.7 %collective-permute-start.34 = (bf16[1024,512]{1,0:T(8,128)(2,1)}, bf16[1024,512]{1,0:T(8,128)(2,1)}, u32[]{:S(2)}, u32[]{:S(2)}) collective-permute-start(bf16[1024,512]{1,0:T(8,128)(2,1)} %collective-permute-done.22.refs_2_), channel_id=1, source_target_pairs={{0,1},{1,0},{2,3},{3,2},{4,5},{5,4},{6,7},{7,6},{8,9},{9,8},{10,11... | collective-permute-start | bytes 3145736 | tf_op jit(solution)/shard_map/ppermute | solution.py:783
  167.1 19.1 %all-to-all-start.1 = ((bf16[8,64,1024]{2,1,0:T(8,128)(2,1)}), bf16[8,64,1024]{2,1,0:T(8,128)(2,1)}, u32[]{:S(2)}, u32[]{:S(2)}) async-start(bf16[8,64,1024]{2,1,0:T(8,128)(2,1)} %get-tuple-element.221), calls=%async_computation.1 | async-start | bytes 2097152 | tf_op jit(solution)/shard_map/all_to_all | solution.py:771
  186.2 76.8 %collective-permute-start.38 = (bf16[512,512]{1,0:T(8,128)(2,1)}, bf16[512,512]{1,0:T(8,128)(2,1)}, u32[]{:S(2)}, u32[]{:S(2)}) collective-permute-start(bf16[512,512]{1,0:T(8,128)(2,1)} %get-tuple-element.244), channel_id=1, source_target_pairs={{0,8},{8,0},{1,9},{9,1},{2,10},{10,2},{3,11},{11,3},{4,12},{12,4},... | collective-permute-start | bytes 1572872 | tf_op jit(solution)/shard_map/ppermute | solution.py:763
  187.2 75.8 %all-to-all-start.2 = ((bf16[8,304,512]{2,1,0:T(8,128)(2,1)}), bf16[8,304,512]{2,1,0:T(8,128)(2,1)}, u32[]{:S(2)}, u32[]{:S(2)}) async-start(bf16[8,304,512]{2,1,0:T(8,128)(2,1)} %add.163), calls=%async_computation.2 | async-start | bytes 4980736 | tf_op jit(solution)/shard_map/all_to_all | solution.py:771
  263.0 53.8 %all-to-all-start.3 = ((bf16[8,192,1024]{2,1,0:T(8,128)(2,1)}), bf16[8,192,1024]{2,1,0:T(8,128)(2,1)}, u32[]{:S(2)}, u32[]{:S(2)}) async-start(bf16[8,192,1024]{2,1,0:T(8,128)(2,1)} %attention_backward.1.grads), calls=%async_computation.3 | async-start | bytes 6291456 | tf_op jit(solution)/shard_map/all_to_all | solution.py:771
  280.2 29.0 %collective-permute-start.41 = (bf16[304,512]{1,0:T(8,128)(2,1)S(1)}, bf16[304,512]{1,0:T(8,128)(2,1)S(1)}, u32[]{:S(2)}, u32[]{:S(2)}) collective-permute-start(bf16[304,512]{1,0:T(8,128)(2,1)S(1)} %convert_element_type.71), channel_id=1, source_target_pairs={{0,8},{8,0},{1,9},{9,1},{2,10},{10,2},{3,11},{11,3},{4,12},{12,4},... | collective-permute-start | bytes 933896 | tf_op jit(solution)/shard_map/ppermute | solution.py:763
  284.5 29.7 %collective-permute-start.40 = (bf16[192,640]{1,0:T(8,128)(2,1)S(1)}, bf16[192,640]{1,0:T(8,128)(2,1)S(1)}, u32[]{:S(2)}, u32[]{:S(2)}) collective-permute-start(bf16[192,640]{1,0:T(8,128)(2,1)S(1)} %fusion.3), channel_id=1, source_target_pairs={{0,8},{8,0},{1,9},{9,1},{2,10},{10,2},{3,11},{11,3},{4,12},{12,4},... | collective-permute-start | bytes 737288 | tf_op jit(solution)/shard_map/ppermute | solution.py:763
  329.6 26.4 %collective-permute-start.44 = (bf16[512,512]{1,0:T(8,128)(2,1)S(1)}, bf16[512,512]{1,0:T(8,128)(2,1)}, u32[]{:S(2)}, u32[]{:S(2)}) collective-permute-start(bf16[512,512]{1,0:T(8,128)(2,1)S(1)} %copy-done.7), channel_id=1, source_target_pairs={{0,8},{8,0},{1,9},{9,1},{2,10},{10,2},{3,11},{11,3},{4,12},{12,4},... | collective-permute-start | bytes 1572872 | tf_op jit(solution)/shard_map/ppermute | solution.py:763
  333.1 22.9 %collective-permute-start.48 = (bf16[208,512]{1,0:T(8,128)(2,1)S(1)}, bf16[208,512]{1,0:T(8,128)(2,1)S(1)}, u32[]{:S(2)}, u32[]{:S(2)}) collective-permute-start(bf16[208,512]{1,0:T(8,128)(2,1)S(1)} %concatenate.21), channel_id=1, source_target_pairs={{0,6},{1,7},{2,4},{3,5},{4,2},{5,3},{6,0},{7,1},{8,14},{9,15},{10,... | collective-permute-start | bytes 638984 | tf_op jit(solution)/shard_map/ppermute | solution.py:767
  336.8 19.2 %collective-permute-start.47 = (bf16[208,512]{1,0:T(8,128)(2,1)S(1)}, bf16[208,512]{1,0:T(8,128)(2,1)S(1)}, u32[]{:S(2)}, u32[]{:S(2)}) collective-permute-start(bf16[208,512]{1,0:T(8,128)(2,1)S(1)} %concatenate.21), channel_id=1, source_target_pairs={{0,2},{1,3},{2,0},{3,1},{4,6},{5,7},{6,4},{7,5},{8,10},{9,11},{10,... | collective-permute-start | bytes 638984 | tf_op jit(solution)/shard_map/ppermute | solution.py:767
  337.4 18.7 %collective-permute-start.46 = (bf16[208,512]{1,0:T(8,128)(2,1)S(1)}, bf16[208,512]{1,0:T(8,128)(2,1)S(1)}, u32[]{:S(2)}, u32[]{:S(2)}) collective-permute-start(bf16[208,512]{1,0:T(8,128)(2,1)S(1)} %concatenate.21), channel_id=1, source_target_pairs={{0,4},{1,5},{2,6},{3,7},{4,0},{5,1},{6,2},{7,3},{8,12},{9,13},{10,... | collective-permute-start | bytes 638984 | tf_op jit(solution)/shard_map/ppermute | solution.py:767
  338.8 46.8 %all-to-all-start.4 = ((bf16[8,288,512]{2,1,0:T(8,128)(2,1)}), bf16[8,288,512]{2,1,0:T(8,128)(2,1)}, u32[]{:S(2)}, u32[]{:S(2)}) async-start(bf16[8,288,512]{2,1,0:T(8,128)(2,1)} %broadcast_in_dim.189), calls=%async_computation.4 | async-start | bytes 4718592 | tf_op jit(solution)/shard_map/all_to_all | solution.py:771
  343.3 22.4 %collective-permute-start.43 = (bf16[512,512]{1,0:T(8,128)(2,1)}, bf16[512,512]{1,0:T(8,128)(2,1)}, u32[]{:S(2)}, u32[]{:S(2)}) collective-permute-start(bf16[512,512]{1,0:T(8,128)(2,1)} %collective-permute-done.38.back), channel_id=1, source_target_pairs={{0,1},{1,0},{2,3},{3,2},{4,5},{5,4},{6,7},{7,6},{8,9},{9,8},{10,11... | collective-permute-start | bytes 1572872 | tf_op jit(solution)/shard_map/ppermute | solution.py:783
  (70 other events, 693.2 us)

commit v5 on v4

--- a/solution.py
+++ b/solution.py
@@ -949,13 +949,13 @@
     grads, late, total = tie(grads, late, total)
     other_rows = tail(1, me, ln1_gain, heads_w, grad_middle[1], other_tokens, grads)
     halves = jnp.stack([half, core]).astype(jnp.int32)
-    other_rows, ln1_own, total = tie(other_rows, ln1_gain, total)
+    other_rows, ln1_own, total, late = tie(other_rows, ln1_gain, total, late)
     back = across(other_rows)
     own_rows = tail(0, me, ln1_own, heads_w, grad_middle[0], own_tokens, grads)
     own_there = swap(own_rows)
     total = deal(total, ("dp", "x", "zl"))
-    own_there, layer_back, late = tie(own_there, layer_back, late)
     late = [late] + [move(late, step) for step in range(1, 4)]
+    own_there, layer_back = tie(own_there, layer_back)
 
     wide = w_fc.shape[1]
     fc_grad, proj_grad, out_grad = unpack(total, wide)

time: 390 us -> 388 us (level)
    all_to_all x5, waiting for transfers between devices: 17.8 us -> 13.3 us  [deal(): return lax.all_to_all(array, axes, 0, 0, tiled=True)]
  transfers between devices with their start and end apart: 55 -> 55, of which waited for: 17 -> 17; matrix products, arithmetic and copies ran while one was open for 8% -> 8% of each run, Pallas kernels for 41% -> 44%
where the time goes in v5:
time: 388 us; the launch traced here: 386 us
  Pallas kernels  185 us (48%)
  waiting for transfers between devices  93.5 us (24%)
  starting transfers between devices  65.7 us (17%)
  other arithmetic  20.4 us (5%)
  local copies, waits for them, and re-layouts  18.5 us (5%)
    pallas_call x1, Pallas kernels, attention_backward(): pl.pallas_call(backward_kernel, out_shape=jax.ShapeDtypeStruct((8, 3 * HE...  72.7 us
    ppermute x6, waiting for transfers between devices, across(): return lax.ppermute(array, 'zh', [(0, 1), (1, 0)])  52.6 us
    pallas_call x1, Pallas kernels, attention_forward(): pl.pallas_call(forward_kernel, out_shape=[jax.ShapeDtypeStruct((HEAD_DIM,...  39.9 us
    ppermute x27, starting transfers between devices, move(): return lax.ppermute(piece, ALL_AXES, group_pairs(step)) if step else piece  27.4 us
    ppermute x27, waiting for transfers between devices, move(): return lax.ppermute(piece, ALL_AXES, group_pairs(step)) if step else piece  24.3 us
    pallas_call x1, Pallas kernels, middle(): pl.pallas_call(middle_kernel, out_shape=[shape((block, width), BF16)] * 2...  22.1 us
    all_to_all x5, starting transfers between devices, deal(): return lax.all_to_all(array, axes, 0, 0, tiled=True)  21 us
    pallas_call x2, Pallas kernels, weight_sums(): pl.pallas_call(functools.partial(weight_sums_kernel, half), out_shape=jax...  13.9 us
  transfers between devices with their start and end apart: 55, of which 17 were waited for; matrix products, arithmetic and copies ran while one was open for 8% of the time, Pallas kernels for 44%

profile of v5, /device:TPU:0, one launch (start us, length us, event | category | flops | bytes accessed | tf_op | source)
XLA Modules:
  0.0 386.0 jit_solution(16765691040509519775)
XLA Ops:
  11.6 4.0 %collective-permute-start.8 = (bf16[512,512]{1,0:T(8,128)(2,1)S(1)}, bf16[512,512]{1,0:T(8,128)(2,1)S(1)}, u32[]{:S(2)}, u32[]{:S(2)}) collective-permute-start(bf16[512,512]{1,0:T(8,128)(2,1)S(1)} %get-tuple-element.148), channel_id=1, source_target_pairs={{0,8},{8,0},{1,9},{9,1},{2,10},{10,2},{3,11},{11,3},{4,12},{12,4},... | collective-permute-start | bytes 1572872 | tf_op jit(solution)/shard_map/ppermute | solution.py:763
  17.0 5.2 %project.2 = (bf16[192,512]{1,0:T(8,128)(2,1)}, bf16[192,512]{1,0:T(8,128)(2,1)}, bf16[192,512]{1,0:T(8,128)(2,1)}, bf16[192,512]{1,0:T(8,128)(2,1)}, bf16[192,5...) custom-call(f32[1,512]{1,0:T(1,128)} %bitcast.83, ...), custom_call_target="tpu_custom_call" | custom-call | flops 805306368 | bytes 1572864 | tf_op jit(solution)/shard_map/project/pallas_call | solution.py:384
  31.7 8.5 %collective-permute-done.8.block.refs_9_ = bf16[512,512]{1,0:T(8,128)(2,1)S(1)} collective-permute-done((bf16[512,512]{1,0:T(8,128)(2,1)S(1)}, bf16[512,512]{1,0:T(8,128)(2,1)S(1)}, u32[]{:S(2)}, u32[]{:S(2)}) %collective-permute-start.8) | collective-permute-done | bytes 524320 | tf_op jit(solution)/shard_map/ppermute | solution.py:763
  43.0 5.1 %project.3 = (bf16[192,512]{1,0:T(8,128)(2,1)}, bf16[192,512]{1,0:T(8,128)(2,1)}, bf16[192,512]{1,0:T(8,128)(2,1)}, bf16[192,512]{1,0:T(8,128)(2,1)}, bf16[192,5...) custom-call(f32[1,512]{1,0:T(1,128)} %bitcast.84, ...), custom_call_target="tpu_custom_call" | custom-call | flops 805306368 | bytes 1572864 | tf_op jit(solution)/shard_map/project/pallas_call | solution.py:384
  70.7 4.2 %collective-permute-done.20.refs_15_ = bf16[192,512]{1,0:T(8,128)(2,1)S(1)} collective-permute-done((bf16[192,512]{1,0:T(8,128)(2,1)}, bf16[192,512]{1,0:T(8,128)(2,1)S(1)}, u32[]{:S(2)}, u32[]{:S(2)}) %collective-permute-start.20) | collective-permute-done | bytes 196640 | tf_op jit(solution)/shard_map/ppermute | solution.py:767
  79.4 39.9 %attention_forward.1 = (bf16[64,1024]{1,0:T(8,128)(2,1)}, bf16[64,1024]{1,0:T(8,128)(2,1)}, bf16[64,1024]{1,0:T(8,128)(2,1)}, bf16[64,1024]{1,0:T(8,128)(2,1)}, ...) custom-call(s32[8,256]{1,0:T(8,128)} %stack.51.table_ref, ...), custom_call_target="tpu_custom_call" | custom-call | flops 17179869184 | bytes 4194304 | tf_op jit(solution)/shard_map/attention_forward/pallas_call | solution.py:271
  129.2 5.4 %collective-permute-done.29.refs_6_.refs_2_ = bf16[64,1024]{1,0:T(8,128)(2,1)S(1)} collective-permute-done((bf16[64,1024]{1,0:T(8,128)(2,1)}, bf16[64,1024]{1,0:T(8,128)(2,1)S(1)}, u32[]{:S(2)}, u32[]{:S(2)}) %collective-permute-start.29) | collective-permute-done | bytes 131104 | tf_op jit(solution)/shard_map/ppermute | solution.py:767
  136.3 22.1 %middle.1 = (bf16[512,512]{1,0:T(8,128)(2,1)}, bf16[512,512]{1,0:T(8,128)(2,1)}, f32[512,512]{1,0:T(8,128)}, f32[512,512]{1,0:T(8,128)}, bf16[8,64,1024]{2,1,0:T...) custom-call(s32[1]{0:T(128)} %bitcast.2.me_ref, ...), custom_call_target="tpu_custom_call" | custom-call | flops 14495514624 | bytes 16777216 | tf_op jit(solution)/shard_map/middle/pallas_call | solution.py:613
  160.9 7.0 %weight_sums.2 = bf16[8,304,512]{2,1,0:T(8,128)(2,1)} custom-call(s32[1]{0:T(128)} %bitcast.2.me_ref, f32[8,512]{1,0:T(8,128)} %get-tuple-element.226.vectors_ref, f32[8,1024]{1,0:T(8,128)} %get-tuple-element.227.pre_sums_ref, bf16[64,1024]{1,0:T(8,128)(2,1)} %copy-done.28, bf16[64,1024]{1,0:T(8,128)(2,1)} %copy-done.29, bf16[64,1024]{1,0:T(8,128)(2,1)} %copy-done.30, ...), custom_call_target="tpu_custom_call" | custom-call | flops 7247757312 | bytes 6291456 | tf_op jit(solution)/shard_map/weight_sums/pallas_call | solution.py:720
  167.9 4.3 %all-to-all-start.1 = ((bf16[8,64,1024]{2,1,0:T(8,128)(2,1)}), bf16[8,64,1024]{2,1,0:T(8,128)(2,1)}, u32[]{:S(2)}, u32[]{:S(2)}) async-start(bf16[8,64,1024]{2,1,0:T(8,128)(2,1)} %get-tuple-element.221), calls=%async_computation.1 | async-start | bytes 2097152 | tf_op jit(solution)/shard_map/all_to_all | solution.py:771
  172.8 6.9 %weight_sums.3 = bf16[8,304,512]{2,1,0:T(8,128)(2,1)} custom-call(s32[1]{0:T(128)} %bitcast.2.me_ref, f32[8,512]{1,0:T(8,128)} %get-tuple-element.226.vectors_ref, f32[8,1024]{1,0:T(8,128)} %get-tuple-element.227.pre_sums_ref, bf16[64,1024]{1,0:T(8,128)(2,1)} %get-tuple-element.206.refs_0_.refs_16_, bf16[64,1024]{1,0:T(8,128)(2,1)} %copy-done.25, ...), custom_call_target="tpu_custom_call" | custom-call | flops 7247757312 | bytes 6291456 | tf_op jit(solution)/shard_map/weight_sums/pallas_call | solution.py:720
  179.7 4.6 %add.163 = bf16[8,304,512]{2,1,0:T(8,128)(2,1)} add(bf16[8,304,512]{2,1,0:T(8,128)(2,1)} %weight_sums.3, bf16[8,304,512]{2,1,0:T(8,128)(2,1)} %collective-permute-done.35) | non-fusion elementwise | flops 1245184 | bytes 7471104 | tf_op jit(solution)/shard_map/add | solution.py:919
  188.0 4.6 %all-to-all-start.2 = ((bf16[8,304,512]{2,1,0:T(8,128)(2,1)}), bf16[8,304,512]{2,1,0:T(8,128)(2,1)}, u32[]{:S(2)}, u32[]{:S(2)}) async-start(bf16[8,304,512]{2,1,0:T(8,128)(2,1)} %add.163), calls=%async_computation.2 | async-start | bytes 4980736 | tf_op jit(solution)/shard_map/all_to_all | solution.py:771
  192.6 72.7 %attention_backward.1.grads = bf16[8,192,1024]{2,1,0:T(8,128)(2,1)} custom-call(s32[8,256]{1,0:T(8,128)} %stack.51.table_ref, s32[17]{0:T(128)} %pad_add_fusion.1.place_ref, s32[1,8192]{1,0:T(1,128)} %bitcast.79, f32[1,8192]{1,0:T(1,128)} %get-tuple-element.242.lse_ref, bf16[192,512]{1,0:T(8,128)(2,1)} %get-tuple-element.170.refs_0_, ...), custom_call_target="tpu_custom_call" | custom-call | flops 64424509440 | bytes 8388608 | tf_op jit(solution)/shard_map/attention_backward/pallas_call | solution.py:305
  265.3 4.5 %all-to-all-start.3 = ((bf16[8,192,1024]{2,1,0:T(8,128)(2,1)}), bf16[8,192,1024]{2,1,0:T(8,128)(2,1)}, u32[]{:S(2)}, u32[]{:S(2)}) async-start(bf16[8,192,1024]{2,1,0:T(8,128)(2,1)} %attention_backward.1.grads), calls=%async_computation.3 | async-start | bytes 6291456 | tf_op jit(solution)/shard_map/all_to_all | solution.py:771
  269.8 5.6 %head_sums.1 = f32[192,640]{1,0:T(8,128)} custom-call(s32[1]{0:T(128)} %bitcast.2.me_ref, bf16[8,192,1024]{2,1,0:T(8,128)(2,1)} %attention_backward.1.grads, bf16[1024,512]{1,0:T(8,128)(2,1)} %copy-done.3, bf16[1024,512]{1,0:T(8,128)(2,1)} %collective-permute-done.23.refs_1_, bf16[1024,512]{1,0:T(8,128)(2,1)} %collective-permute-done.22.refs_2_, ...), custom_call_target="tpu_custom_call" | custom-call | flops 1610612736 | bytes 12582912 | tf_op jit(solution)/shard_map/head_sums/pallas_call | solution.py:460
  286.9 24.6 %collective-permute-done.41 = bf16[304,512]{1,0:T(8,128)(2,1)S(1)} collective-permute-done((bf16[304,512]{1,0:T(8,128)(2,1)S(1)}, bf16[304,512]{1,0:T(8,128)(2,1)S(1)}, u32[]{:S(2)}, u32[]{:S(2)}) %collective-permute-start.41) | collective-permute-done | bytes 311328 | tf_op jit(solution)/shard_map/ppermute | solution.py:763
  312.2 4.3 %collective-permute-done.40 = bf16[192,640]{1,0:T(8,128)(2,1)S(1)} collective-permute-done((bf16[192,640]{1,0:T(8,128)(2,1)S(1)}, bf16[192,640]{1,0:T(8,128)(2,1)S(1)}, u32[]{:S(2)}, u32[]{:S(2)}) %collective-permute-start.40) | collective-permute-done | bytes 245792 | tf_op jit(solution)/shard_map/ppermute | solution.py:763
  320.7 5.4 %tail.2 = bf16[512,512]{1,0:T(8,128)(2,1)} custom-call(s32[1]{0:T(128)} %bitcast.2.me_ref, f32[1,512]{1,0:T(1,128)} %bitcast.85, bf16[1536,512]{1,0:T(8,128)(2,1)} %bitcast.67, f32[512,512]{1,0:T(8,128)} %get-tuple-element.241.middle_ref, bf16[512,512]{1,0:T(8,128)(2,1)} %copy-done.6, bf16[8,192,1024]{2,1,0:T(8,128)(2,1)} %all-to-all-done.3.grads), custom_call_target="tpu_custom_call" | custom-call | flops 805306368 | bytes 1572864 | tf_op jit(solution)/shard_map/tail/pallas_call | solution.py:416
  326.1 4.0 %collective-permute-start.48 = (bf16[208,512]{1,0:T(8,128)(2,1)S(1)}, bf16[208,512]{1,0:T(8,128)(2,1)S(1)}, u32[]{:S(2)}, u32[]{:S(2)}) collective-permute-start(bf16[208,512]{1,0:T(8,128)(2,1)S(1)} %concatenate.21), channel_id=1, source_target_pairs={{0,6},{1,7},{2,4},{3,5},{4,2},{5,3},{6,0},{7,1},{8,14},{9,15},{10,... | collective-permute-start | bytes 638984 | tf_op jit(solution)/shard_map/ppermute | solution.py:767
  331.4 5.5 %tail.3.mine = bf16[512,512]{1,0:T(8,128)(2,1)} custom-call(s32[1]{0:T(128)} %bitcast.2.me_ref, f32[1,512]{1,0:T(1,128)} %bitcast.86, bf16[1536,512]{1,0:T(8,128)(2,1)} %bitcast.68, f32[512,512]{1,0:T(8,128)} %get-tuple-element.257.middle_ref, bf16[512,512]{1,0:T(8,128)(2,1)} %get-tuple-element.338.block.refs_8_, bf16[8,192,1024]{2,1,0:T(8,128)(2,1)} %all-to-all-done.3.grads), custom_call_target="tpu_custom_call" | custom-call | flops 805306368 | bytes 1572864 | tf_op jit(solution)/shard_map/tail/pallas_call | solution.py:416
  338.3 4.4 %all-to-all-start.4 = ((bf16[8,288,512]{2,1,0:T(8,128)(2,1)}), bf16[8,288,512]{2,1,0:T(8,128)(2,1)}, u32[]{:S(2)}, u32[]{:S(2)}) async-start(bf16[8,288,512]{2,1,0:T(8,128)(2,1)} %broadcast_in_dim.189), calls=%async_computation.4 | async-start | bytes 4718592 | tf_op jit(solution)/shard_map/all_to_all | solution.py:771
  348.3 15.3 %collective-permute-done.44.back = bf16[512,512]{1,0:T(8,128)(2,1)} collective-permute-done((bf16[512,512]{1,0:T(8,128)(2,1)S(1)}, bf16[512,512]{1,0:T(8,128)(2,1)}, u32[]{:S(2)}, u32[]{:S(2)}) %collective-permute-start.44) | collective-permute-done | bytes 524320 | tf_op jit(solution)/shard_map/ppermute | solution.py:763
  372.5 9.6 %all-to-all-done.4.stage = bf16[8,288,512]{2,1,0:T(8,128)(2,1)} async-done(((bf16[8,288,512]{2,1,0:T(8,128)(2,1)}), bf16[8,288,512]{2,1,0:T(8,128)(2,1)}, u32[]{:S(2)}, u32[]{:S(2)}) %all-to-all-start.4) | async-done | bytes 2359328 | tf_op jit(solution)/shard_map/all_to_all | solution.py:771
  (255 shorter events, 105.8 us)
Async XLA Ops:
  11.6 28.6 %collective-permute-start.8 = (bf16[512,512]{1,0:T(8,128)(2,1)S(1)}, bf16[512,512]{1,0:T(8,128)(2,1)S(1)}, u32[]{:S(2)}, u32[]{:S(2)}) collective-permute-start(bf16[512,512]{1,0:T(8,128)(2,1)S(1)} %get-tuple-element.148), channel_id=1, source_target_pairs={{0,8},{8,0},{1,9},{9,1},{2,10},{10,2},{3,11},{11,3},{4,12},{12,4},... | collective-permute-start | bytes 1572872 | tf_op jit(solution)/shard_map/ppermute | solution.py:763
  22.2 18.0 %collective-permute-start.6 = (bf16[192,512]{1,0:T(8,128)(2,1)}, bf16[192,512]{1,0:T(8,128)(2,1)S(1)}, u32[]{:S(2)}, u32[]{:S(2)}) collective-permute-start(bf16[192,512]{1,0:T(8,128)(2,1)} %get-tuple-element.146), channel_id=1, source_target_pairs={{0,2},{1,3},{2,0},{3,1},{4,6},{5,7},{6,4},{7,5},{8,10},{9,11},{10,... | collective-permute-start | bytes 589832 | tf_op jit(solution)/shard_map/ppermute | solution.py:767
  23.8 18.0 %collective-permute-start.7 = (bf16[192,512]{1,0:T(8,128)(2,1)}, bf16[192,512]{1,0:T(8,128)(2,1)}, u32[]{:S(2)}, u32[]{:S(2)}) collective-permute-start(bf16[192,512]{1,0:T(8,128)(2,1)} %get-tuple-element.147), channel_id=1, source_target_pairs={{0,1},{1,0},{2,3},{3,2},{4,5},{5,4},{6,7},{7,6},{8,9},{9,8},{10,11... | collective-permute-start | bytes 589832 | tf_op jit(solution)/shard_map/ppermute | solution.py:767
  24.4 23.7 %all-to-all-start = ((s32[8,2,1024]{2,1,0:T(2,128)}), s32[8,2,1024]{2,1,0:T(2,128)S(1)}, u32[]{:S(2)}, u32[]{:S(2)}) async-start(s32[8,2,1024]{2,1,0:T(2,128)} %broadcast_in_dim.178), calls=%async_computation | async-start | bytes 131072 | tf_op jit(solution)/shard_map/all_to_all | solution.py:771
  28.4 23.8 %collective-permute-start.9 = (bf16[192,512]{1,0:T(8,128)(2,1)}, bf16[192,512]{1,0:T(8,128)(2,1)}, u32[]{:S(2)}, u32[]{:S(2)}) collective-permute-start(bf16[192,512]{1,0:T(8,128)(2,1)} %get-tuple-element.153), channel_id=1, source_target_pairs={{0,4},{1,5},{2,6},{3,7},{4,0},{5,1},{6,2},{7,3},{8,12},{9,13},{10,... | collective-permute-start | bytes 589832 | tf_op jit(solution)/shard_map/ppermute | solution.py:767
  30.3 22.5 %collective-permute-start.10 = (bf16[192,512]{1,0:T(8,128)(2,1)}, bf16[192,512]{1,0:T(8,128)(2,1)}, u32[]{:S(2)}, u32[]{:S(2)}) collective-permute-start(bf16[192,512]{1,0:T(8,128)(2,1)} %get-tuple-element.155), channel_id=1, source_target_pairs={{0,6},{1,7},{2,4},{3,5},{4,2},{5,3},{6,0},{7,1},{8,14},{9,15},{10,... | collective-permute-start | bytes 589832 | tf_op jit(solution)/shard_map/ppermute | solution.py:767
  74.9 44.5 %collective-permute-start.22 = (bf16[1024,512]{1,0:T(8,128)(2,1)S(1)}, bf16[1024,512]{1,0:T(8,128)(2,1)}, u32[]{:S(2)}, u32[]{:S(2)}) collective-permute-start(bf16[1024,512]{1,0:T(8,128)(2,1)S(1)} %pad_maximum_fusion.1.refs_0_), channel_id=1, source_target_pairs={{0,2},{1,3},{2,0},{3,1},{4,6},{5,7},{6,4},{7,5},{8,10},{9,11},{10,... | collective-permute-start | bytes 3145736 | tf_op jit(solution)/shard_map/ppermute | solution.py:767
  75.3 44.1 %collective-permute-start.23 = (bf16[1024,512]{1,0:T(8,128)(2,1)S(1)}, bf16[1024,512]{1,0:T(8,128)(2,1)}, u32[]{:S(2)}, u32[]{:S(2)}) collective-permute-start(bf16[1024,512]{1,0:T(8,128)(2,1)S(1)} %pad_maximum_fusion.1.refs_0_), channel_id=1, source_target_pairs={{0,4},{1,5},{2,6},{3,7},{4,0},{5,1},{6,2},{7,3},{8,12},{9,13},{10,... | collective-permute-start | bytes 3145736 | tf_op jit(solution)/shard_map/ppermute | solution.py:767
  75.4 43.9 %collective-permute-start.21 = (bf16[512,512]{1,0:T(8,128)(2,1)}, bf16[512,512]{1,0:T(8,128)(2,1)}, u32[]{:S(2)}, u32[]{:S(2)}) collective-permute-start(bf16[512,512]{1,0:T(8,128)(2,1)} %get-tuple-element.194), channel_id=1, source_target_pairs={{0,8},{8,0},{1,9},{9,1},{2,10},{10,2},{3,11},{11,3},{4,12},{12,4},... | collective-permute-start | bytes 1572872 | tf_op jit(solution)/shard_map/ppermute | solution.py:763
  134.6 26.2 %collective-permute-start.31 = (bf16[1024,512]{1,0:T(8,128)(2,1)S(1)}, bf16[1024,512]{1,0:T(8,128)(2,1)}, u32[]{:S(2)}, u32[]{:S(2)}) collective-permute-start(bf16[1024,512]{1,0:T(8,128)(2,1)S(1)} %pad_maximum_fusion.1.refs_0_), channel_id=1, source_target_pairs={{0,6},{1,7},{2,4},{3,5},{4,2},{5,3},{6,0},{7,1},{8,14},{9,15},{10,... | collective-permute-start | bytes 3145736 | tf_op jit(solution)/shard_map/ppermute | solution.py:767
  135.7 25.2 %collective-permute-start.32 = (bf16[1024,512]{1,0:T(8,128)(2,1)S(1)}, bf16[1024,512]{1,0:T(8,128)(2,1)}, u32[]{:S(2)}, u32[]{:S(2)}) collective-permute-start(bf16[1024,512]{1,0:T(8,128)(2,1)S(1)} %pad_maximum_fusion.1.refs_0_), channel_id=1, source_target_pairs={{0,1},{1,0},{2,3},{3,2},{4,5},{5,4},{6,7},{7,6},{8,9},{9,8},{10,11... | collective-permute-start | bytes 3145736 | tf_op jit(solution)/shard_map/ppermute | solution.py:783
  135.7 25.2 %collective-permute-start.33 = (bf16[1024,512]{1,0:T(8,128)(2,1)}, bf16[1024,512]{1,0:T(8,128)(2,1)}, u32[]{:S(2)}, u32[]{:S(2)}) collective-permute-start(bf16[1024,512]{1,0:T(8,128)(2,1)} %collective-permute-done.23.refs_1_), channel_id=1, source_target_pairs={{0,1},{1,0},{2,3},{3,2},{4,5},{5,4},{6,7},{7,6},{8,9},{9,8},{10,11... | collective-permute-start | bytes 3145736 | tf_op jit(solution)/shard_map/ppermute | solution.py:783
  136.2 24.7 %collective-permute-start.34 = (bf16[1024,512]{1,0:T(8,128)(2,1)}, bf16[1024,512]{1,0:T(8,128)(2,1)}, u32[]{:S(2)}, u32[]{:S(2)}) collective-permute-start(bf16[1024,512]{1,0:T(8,128)(2,1)} %collective-permute-done.22.refs_2_), channel_id=1, source_target_pairs={{0,1},{1,0},{2,3},{3,2},{4,5},{5,4},{6,7},{7,6},{8,9},{9,8},{10,11... | collective-permute-start | bytes 3145736 | tf_op jit(solution)/shard_map/ppermute | solution.py:783
  167.9 19.2 %all-to-all-start.1 = ((bf16[8,64,1024]{2,1,0:T(8,128)(2,1)}), bf16[8,64,1024]{2,1,0:T(8,128)(2,1)}, u32[]{:S(2)}, u32[]{:S(2)}) async-start(bf16[8,64,1024]{2,1,0:T(8,128)(2,1)} %get-tuple-element.221), calls=%async_computation.1 | async-start | bytes 2097152 | tf_op jit(solution)/shard_map/all_to_all | solution.py:771
  187.1 78.2 %collective-permute-start.38 = (bf16[512,512]{1,0:T(8,128)(2,1)}, bf16[512,512]{1,0:T(8,128)(2,1)}, u32[]{:S(2)}, u32[]{:S(2)}) collective-permute-start(bf16[512,512]{1,0:T(8,128)(2,1)} %get-tuple-element.244), channel_id=1, source_target_pairs={{0,8},{8,0},{1,9},{9,1},{2,10},{10,2},{3,11},{11,3},{4,12},{12,4},... | collective-permute-start | bytes 1572872 | tf_op jit(solution)/shard_map/ppermute | solution.py:763
  188.0 77.3 %all-to-all-start.2 = ((bf16[8,304,512]{2,1,0:T(8,128)(2,1)}), bf16[8,304,512]{2,1,0:T(8,128)(2,1)}, u32[]{:S(2)}, u32[]{:S(2)}) async-start(bf16[8,304,512]{2,1,0:T(8,128)(2,1)} %add.163), calls=%async_computation.2 | async-start | bytes 4980736 | tf_op jit(solution)/shard_map/all_to_all | solution.py:771
  265.3 53.8 %all-to-all-start.3 = ((bf16[8,192,1024]{2,1,0:T(8,128)(2,1)}), bf16[8,192,1024]{2,1,0:T(8,128)(2,1)}, u32[]{:S(2)}, u32[]{:S(2)}) async-start(bf16[8,192,1024]{2,1,0:T(8,128)(2,1)} %attention_backward.1.grads), calls=%async_computation.3 | async-start | bytes 6291456 | tf_op jit(solution)/shard_map/all_to_all | solution.py:771
  278.7 32.7 %collective-permute-start.41 = (bf16[304,512]{1,0:T(8,128)(2,1)S(1)}, bf16[304,512]{1,0:T(8,128)(2,1)S(1)}, u32[]{:S(2)}, u32[]{:S(2)}) collective-permute-start(bf16[304,512]{1,0:T(8,128)(2,1)S(1)} %convert_element_type.71), channel_id=1, source_target_pairs={{0,8},{8,0},{1,9},{9,1},{2,10},{10,2},{3,11},{11,3},{4,12},{12,4},... | collective-permute-start | bytes 933896 | tf_op jit(solution)/shard_map/ppermute | solution.py:763
  284.8 31.6 %collective-permute-start.40 = (bf16[192,640]{1,0:T(8,128)(2,1)S(1)}, bf16[192,640]{1,0:T(8,128)(2,1)S(1)}, u32[]{:S(2)}, u32[]{:S(2)}) collective-permute-start(bf16[192,640]{1,0:T(8,128)(2,1)S(1)} %fusion.3), channel_id=1, source_target_pairs={{0,8},{8,0},{1,9},{9,1},{2,10},{10,2},{3,11},{11,3},{4,12},{12,4},... | collective-permute-start | bytes 737288 | tf_op jit(solution)/shard_map/ppermute | solution.py:763
  326.1 16.6 %collective-permute-start.48 = (bf16[208,512]{1,0:T(8,128)(2,1)S(1)}, bf16[208,512]{1,0:T(8,128)(2,1)S(1)}, u32[]{:S(2)}, u32[]{:S(2)}) collective-permute-start(bf16[208,512]{1,0:T(8,128)(2,1)S(1)} %concatenate.21), channel_id=1, source_target_pairs={{0,6},{1,7},{2,4},{3,5},{4,2},{5,3},{6,0},{7,1},{8,14},{9,15},{10,... | collective-permute-start | bytes 638984 | tf_op jit(solution)/shard_map/ppermute | solution.py:767
  336.9 26.7 %collective-permute-start.44 = (bf16[512,512]{1,0:T(8,128)(2,1)S(1)}, bf16[512,512]{1,0:T(8,128)(2,1)}, u32[]{:S(2)}, u32[]{:S(2)}) collective-permute-start(bf16[512,512]{1,0:T(8,128)(2,1)S(1)} %copy-done.7), channel_id=1, source_target_pairs={{0,8},{8,0},{1,9},{9,1},{2,10},{10,2},{3,11},{11,3},{4,12},{12,4},... | collective-permute-start | bytes 1572872 | tf_op jit(solution)/shard_map/ppermute | solution.py:763
  338.3 43.8 %all-to-all-start.4 = ((bf16[8,288,512]{2,1,0:T(8,128)(2,1)}), bf16[8,288,512]{2,1,0:T(8,128)(2,1)}, u32[]{:S(2)}, u32[]{:S(2)}) async-start(bf16[8,288,512]{2,1,0:T(8,128)(2,1)} %broadcast_in_dim.189), calls=%async_computation.4 | async-start | bytes 4718592 | tf_op jit(solution)/shard_map/all_to_all | solution.py:771
  345.6 20.4 %collective-permute-start.49 = (f32[2,512]{1,0:T(2,128)S(1)}, f32[2,512]{1,0:T(2,128)S(1)}, u32[]{:S(2)}, u32[]{:S(2)}) collective-permute-start(f32[2,512]{1,0:T(2,128)S(1)} %slice_reduce_fusion.1), channel_id=1, source_target_pairs={{0,1},{1,0},{2,3},{3,2},{4,5},{5,4},{6,7},{7,6},{8,9},{9,8},{10,11... | collective-permute-start | bytes 12296 | tf_op jit(solution)/shard_map/ppermute | solution.py:783
  348.0 18.7 %collective-permute-start.43 = (bf16[512,512]{1,0:T(8,128)(2,1)}, bf16[512,512]{1,0:T(8,128)(2,1)}, u32[]{:S(2)}, u32[]{:S(2)}) collective-permute-start(bf16[512,512]{1,0:T(8,128)(2,1)} %collective-permute-done.38.back), channel_id=1, source_target_pairs={{0,1},{1,0},{2,3},{3,2},{4,5},{5,4},{6,7},{7,6},{8,9},{9,8},{10,11... | collective-permute-start | bytes 1572872 | tf_op jit(solution)/shard_map/ppermute | solution.py:783
  (66 other events, 694.5 us)
